TPU v7x, 32 devices: a whole 2x2x4 slice. The times are simulated.
32 devices in a mesh: dp: 8 (over y, x, core), layer: 4 (over z).
Axes of the slice: x: 2, y: 2, z: 4, core: 2. Of those that a mesh axis runs over, the one named last changes fastest.
Arguments:
- output_gradient: bfloat16 [2, 4, 128, 8, 8192], P(None, 'layer', 'dp'), may hold values from -20 to 20, as said below
- adapter_activation: bfloat16 [2, 4, 128, 8, 128], P(None, 'layer', 'dp'), may hold values from -6 to 6
- adaptive_variance: bfloat16 [2, 4, 8192, 128], P(None, 'layer'), may hold values from 0.0099487305 to 1
- holdout_feature: bfloat16 [2, 4, 64, 5120], P(None, 'layer', 'dp'), may hold values from -6 to 6
- lengths: int32 [128], P('dp'), may hold values from 1 to 8
- token_loss_mask: int32 [128, 8], P('dp'), may hold values 0 or 1
- sketch_seed: int32 [1], replicated, may hold values from 0 to 1048575
- step_size_weight: float32 [2], replicated, may hold values from 0.5 to 2
Outputs:
- scores: float32 [128, 64], P(('dp', 'layer'))
Inputs may be any that keep to these rules, and one draw needn't show every extreme that they name: Entries of output_gradient and adapter_activation at token slots where valid is 0 may hold any finite values within the stated range.
All inputs are finite; a program needn't handle non-finite values. No bound on the sum of `token_loss_mask` on one device may be relied on, other than what follows from the above.
Results may differ from a plain program's by a relative error of at most 0.004.
Values may be sent and summed in bfloat16 or wider, within the bound.
No kernel may reach another device: no remote copies, remote signals or barrier semaphores. Data moves between devices by JAX's collectives and lax.ppermute only.
A program may use at most 64 MiB of HBM per device.

v0:
```python
import math

import jax
import jax.numpy as jnp
from jax import lax
from jax.sharding import PartitionSpec as P


def projection(seed_value, layer_id, width, columns):
    row_ids = jnp.arange(width, dtype=jnp.int32)[:, None]
    col_ids = jnp.arange(columns, dtype=jnp.int32)[None, :]
    hashed = row_ids * 1103515245 + col_ids * 12345 + layer_id * 668265263 + seed_value * 374761393
    hashed = hashed ^ hashed >> 15
    hashed = hashed * 747796405
    hashed = hashed ^ hashed >> 13
    bit_value = hashed >> 7 & 1
    return (2 * bit_value - 1).astype(jnp.bfloat16)


def local(
    output_gradient,
    adapter_activation,
    adaptive_variance,
    holdout_feature,
    lengths,
    token_loss_mask,
    sketch_seed,
    step_size_weight,
):
    ckpt_count, layer_local, example_local, sequence_length, width = output_gradient.shape
    rank_column_count = adapter_activation.shape[-1]
    proj_cols = holdout_feature.shape[-1] // rank_column_count
    members_per_group = 4
    count_of_groups = example_local // members_per_group
    positions = jnp.arange(sequence_length, dtype=jnp.int32)[None, :]
    valid_marks = ((token_loss_mask == 1) & (positions < lengths[:, None])).astype(jnp.bfloat16)
    seed_value = sketch_seed[0]
    inv_root = 1.0 / math.sqrt(width)
    layer_base = lax.axis_index("layer") * layer_local
    per_ckpt = []
    for snapshot_index in range(ckpt_count):
        signs_table = projection(seed_value, layer_base + 0, width, proj_cols)
        scaling = jnp.sqrt(adaptive_variance[snapshot_index, 0].astype(jnp.float32)) + 1e-08

        def one_group(group_items):
            grad_rows, act_rows, mark_rows = group_items
            masked = act_rows * mark_rows[:, :, None]
            outer_sum = jnp.einsum(
                "etd,etr->edr", grad_rows, masked, preferred_element_type=jnp.float32
            )
            scaled = (outer_sum / scaling).astype(jnp.bfloat16)
            projected = (
                jnp.einsum("dk,edr->ekr", signs_table, scaled, preferred_element_type=jnp.float32)
                * inv_root
            )
            return projected.astype(jnp.bfloat16).reshape(
                members_per_group, proj_cols * rank_column_count
            )

        grouped = (
            output_gradient[snapshot_index, 0].reshape(
                count_of_groups, members_per_group, sequence_length, width
            ),
            adapter_activation[snapshot_index, 0].reshape(
                count_of_groups, members_per_group, sequence_length, rank_column_count
            ),
            valid_marks.reshape(count_of_groups, members_per_group, sequence_length),
        )
        layerwise_result = [
            lax.map(one_group, grouped).reshape(example_local, proj_cols * rank_column_count)
        ]
        per_ckpt.append(jnp.stack(layerwise_result))
    features = jnp.stack(per_ckpt)
    wide_features = features.astype(jnp.float32)
    squared_norm = jnp.sum(wide_features * wide_features, axis=(1, 3))
    block_scores = jnp.einsum(
        "clek,clvk->cev",
        features,
        lax.all_gather(holdout_feature, "dp", axis=2, tiled=True),
        preferred_element_type=jnp.float32,
    )
    common_part, norm_total = (
        lax.psum_scatter(block_scores, "layer", scatter_dimension=1, tiled=True),
        lax.psum_scatter(squared_norm, "layer", scatter_dimension=1, tiled=True),
    )
    result = jnp.zeros(common_part.shape[1:], jnp.float32)
    for snapshot_index in range(ckpt_count):
        result = (
            result
            + step_size_weight[snapshot_index]
            * common_part[snapshot_index]
            * lax.rsqrt(norm_total[snapshot_index] + 1e-06)[:, None]
        )
    return result


def solution(mesh):
    placed = (
        P(None, "layer", "dp", None, None),
        P(None, "layer", "dp", None, None),
        P(None, "layer", None, None),
        P(None, "layer", "dp", None),
        P("dp"),
        P("dp", None),
        P(),
        P(),
    )
    return jax.shard_map(
        local, mesh=mesh, in_specs=placed, out_specs=P(("dp", "layer"), None), check_vma=False
    )
```

profile of v0, /device:TPU:0, one launch (start us, length us, event | category | flops | bytes accessed | tf_op | source)
XLA Modules:
  0.0 103.2 jit_solution(1732131129999054017)
XLA Ops:
  6.5 0.7 all-gather.2.cloned.1.call-update
  7.3 8.0 %add_bitcast_fusion = (f32[8192,128]{1,0:T(8,128)}, f32[8192,128]{1,0:T(8,128)}) fusion(bf16[2,1,8192,128]{3,2,1,0:T(8,128)(2,1)} %param.14), kind=kLoop, calls=%fused_computation.84 | loop fusion | flops 4194304 | bytes 12582912 | tf_op jit(solution)/shard_map/add | solution.py:43
  15.3 1.6 %fusion.96 = (bf16[1,1,16,8,8192]{4,3,2,1,0:T(8,128)(2,1)S(1)}, bf16[1,1,16,8,8192]{4,3,2,1,0:T(8,128)(2,1)}) fusion(bf16[2,1,16,8,8192]{4,3,2,1,0:T(8,128)(2,1)S(1)} %copy-done), kind=kLoop, calls=%fused_computation.107 | loop fusion | bytes 8388608 | tf_op jit(solution)/shard_map/slice | solution.py:61
  17.0 0.1 copy.11
  17.7 0.1 fusion.90
  17.9 26.3 %while.22 = (s32[]{:T(128)}, bf16[4,4,5120]{2,1,0:T(4,128)(2,1)S(1)}, bf16[4,4,8,8192]{3,2,1,0:T(8,128)(2,1)}, bf16[4,4,8,128]{3,2,1,0:T(8,128)(2,1)S(1)}, bf16[...) while((s32[]{:T(128)}, ...), condition=%wide.region_1.2_spmd.clone, body=%wide.region_0.1_spmd.clone.sunk | while | flops 415346688 | bytes 4968181 | solution.py:70
  17.9 6.6 %fusion.110 = bf16[4,40,128]{2,1,0:T(8,128)(2,1)S(1)} fusion(f32[8192,128]{1,0:T(8,128)} %get-tuple-element.334, s32[]{:T(128)} %get-tuple-element.338, s32[]{:T(128)} %get-tuple-element.337, s32[40]{0:T(128)S(1)} %get-tuple-element.335, s32[8192]{0:T(1024)S(1)} %get-tuple-element.336, bf16[4,4,8,8192]{3,2,1,0:T(8,128)(2,1)} %get-tuple-element.331, ...), kind=kOutput, calls=%fused_computation.14.clone.1 | convolution fusion | flops 415346688 | bytes 4804096 | tf_op jit(solution)/shard_map/while/body/eval_jaxpr/dk,edr->ekr/dot_general | solution.py:53
  24.6 6.5 %fusion.110 = bf16[4,40,128]{2,1,0:T(8,128)(2,1)S(1)} fusion(f32[8192,128]{1,0:T(8,128)} %get-tuple-element.334, s32[]{:T(128)} %get-tuple-element.338, s32[]{:T(128)} %get-tuple-element.337, s32[40]{0:T(128)S(1)} %get-tuple-element.335, s32[8192]{0:T(1024)S(1)} %get-tuple-element.336, bf16[4,4,8,8192]{3,2,1,0:T(8,128)(2,1)} %get-tuple-element.331, ...), kind=kOutput, calls=%fused_computation.14.clone.1 | convolution fusion | flops 415346688 | bytes 4804096 | tf_op jit(solution)/shard_map/while/body/eval_jaxpr/dk,edr->ekr/dot_general | solution.py:53
  31.1 6.5 %fusion.110 = bf16[4,40,128]{2,1,0:T(8,128)(2,1)S(1)} fusion(f32[8192,128]{1,0:T(8,128)} %get-tuple-element.334, s32[]{:T(128)} %get-tuple-element.338, s32[]{:T(128)} %get-tuple-element.337, s32[40]{0:T(128)S(1)} %get-tuple-element.335, s32[8192]{0:T(1024)S(1)} %get-tuple-element.336, bf16[4,4,8,8192]{3,2,1,0:T(8,128)(2,1)} %get-tuple-element.331, ...), kind=kOutput, calls=%fused_computation.14.clone.1 | convolution fusion | flops 415346688 | bytes 4804096 | tf_op jit(solution)/shard_map/while/body/eval_jaxpr/dk,edr->ekr/dot_general | solution.py:53
  37.7 6.5 %fusion.110 = bf16[4,40,128]{2,1,0:T(8,128)(2,1)S(1)} fusion(f32[8192,128]{1,0:T(8,128)} %get-tuple-element.334, s32[]{:T(128)} %get-tuple-element.338, s32[]{:T(128)} %get-tuple-element.337, s32[40]{0:T(128)S(1)} %get-tuple-element.335, s32[8192]{0:T(1024)S(1)} %get-tuple-element.336, bf16[4,4,8,8192]{3,2,1,0:T(8,128)(2,1)} %get-tuple-element.331, ...), kind=kOutput, calls=%fused_computation.14.clone.1 | convolution fusion | flops 415346688 | bytes 4804096 | tf_op jit(solution)/shard_map/while/body/eval_jaxpr/dk,edr->ekr/dot_general | solution.py:53
  44.2 0.0 copy-start.5
  44.3 0.0 copy-start.3
  44.3 25.5 %while.23 = (s32[]{:T(128)}, bf16[4,4,5120]{2,1,0:T(4,128)(2,1)S(1)}, bf16[4,4,8,8192]{3,2,1,0:T(8,128)(2,1)S(1)}, bf16[4,4,8,128]{3,2,1,0:T(8,128)(2,1)S(1)}, b...) while((s32[]{:T(128)}, ...), condition=%wide.region_3.4_spmd.clone, body=%wide.region_2.3_spmd.clone.sunk | while | flops 415346688 | bytes 4968181 | solution.py:70
  44.3 6.3 %fusion.114 = bf16[4,40,128]{2,1,0:T(8,128)(2,1)S(1)} fusion(f32[8192,128]{1,0:T(8,128)} %get-tuple-element.367, s32[]{:T(128)} %get-tuple-element.371, s32[]{:T(128)} %get-tuple-element.370, s32[40]{0:T(128)S(1)} %get-tuple-element.368, s32[8192]{0:T(1024)S(1)} %get-tuple-element.369, bf16[4,4,8,8192]{3,2,1,0:T(8,128)(2,1)S(1)} %get-tuple-element.364, ...), kind=kOutput, calls=%fused_computation.55.clone.1 | convolution fusion | flops 415346688 | bytes 4804096 | tf_op jit(solution)/shard_map/while/body/eval_jaxpr/dk,edr->ekr/dot_general | solution.py:53
  50.7 6.3 %fusion.114 = bf16[4,40,128]{2,1,0:T(8,128)(2,1)S(1)} fusion(f32[8192,128]{1,0:T(8,128)} %get-tuple-element.367, s32[]{:T(128)} %get-tuple-element.371, s32[]{:T(128)} %get-tuple-element.370, s32[40]{0:T(128)S(1)} %get-tuple-element.368, s32[8192]{0:T(1024)S(1)} %get-tuple-element.369, bf16[4,4,8,8192]{3,2,1,0:T(8,128)(2,1)S(1)} %get-tuple-element.364, ...), kind=kOutput, calls=%fused_computation.55.clone.1 | convolution fusion | flops 415346688 | bytes 4804096 | tf_op jit(solution)/shard_map/while/body/eval_jaxpr/dk,edr->ekr/dot_general | solution.py:53
  57.0 6.3 %fusion.114 = bf16[4,40,128]{2,1,0:T(8,128)(2,1)S(1)} fusion(f32[8192,128]{1,0:T(8,128)} %get-tuple-element.367, s32[]{:T(128)} %get-tuple-element.371, s32[]{:T(128)} %get-tuple-element.370, s32[40]{0:T(128)S(1)} %get-tuple-element.368, s32[8192]{0:T(1024)S(1)} %get-tuple-element.369, bf16[4,4,8,8192]{3,2,1,0:T(8,128)(2,1)S(1)} %get-tuple-element.364, ...), kind=kOutput, calls=%fused_computation.55.clone.1 | convolution fusion | flops 415346688 | bytes 4804096 | tf_op jit(solution)/shard_map/while/body/eval_jaxpr/dk,edr->ekr/dot_general | solution.py:53
  63.4 6.3 %fusion.114 = bf16[4,40,128]{2,1,0:T(8,128)(2,1)S(1)} fusion(f32[8192,128]{1,0:T(8,128)} %get-tuple-element.367, s32[]{:T(128)} %get-tuple-element.371, s32[]{:T(128)} %get-tuple-element.370, s32[40]{0:T(128)S(1)} %get-tuple-element.368, s32[8192]{0:T(1024)S(1)} %get-tuple-element.369, bf16[4,4,8,8192]{3,2,1,0:T(8,128)(2,1)S(1)} %get-tuple-element.364, ...), kind=kOutput, calls=%fused_computation.55.clone.1 | convolution fusion | flops 415346688 | bytes 4804096 | tf_op jit(solution)/shard_map/while/body/eval_jaxpr/dk,edr->ekr/dot_general | solution.py:53
  69.9 0.6 dynamic-slice
  71.1 0.6 fusion.98
  71.8 0.1 multiply_reduce_fusion
  71.9 1.8 %fusion.86 = f32[2,16,64]{2,1,0:T(8,128)S(1)} fusion(bf16[2,1,64,5120]{3,2,0,1:T(8,128)(2,1)} %all-gather.2.cloned.1.call-done, bf16[2,1,16,5120]{3,2,0,1:T(8,128)(2,1)S(1)} %constant_dynamic-update-slice_fusion.2), kind=kOutput, calls=%fused_computation.86 | convolution fusion | flops 20971520 | bytes 1646592 | tf_op jit(solution)/shard_map/clek,clvk->cev/dot_general | solution.py:76
  73.7 20.6 %all-reduce.2 = (f32[2,16,64]{2,1,0:T(8,128)S(1)}, f32[2,16]{1,0:T(2,128)S(1)}) all-reduce(f32[2,16,64]{2,1,0:T(8,128)S(1)} %fusion.86, f32[2,16]{1,0:T(2,128)S(1)} %multiply_reduce_fusion), channel_id=2, replica_groups=mesh['dp'=8,'layer'=4] {'layer'}, use_global_device_ids=true, to_apply=%region_4.5.clone | all-reduce | flops 2080 | bytes 16640
  94.3 0.1 constant_dynamic-slice_fusion.2
  94.4 1.9 %fusion.93 = f32[4,64]{1,0:T(4,128)} fusion(f32[2,16,64]{2,1,0:T(8,128)S(1)} %get-tuple-element.173, u32[]{:T(128)S(6)} %convert.1, u32[]{:T(128)S(6)} %multiply.1, f32[4]{0:T(128)S(1)} %get-tuple-element.182, f32[]{:T(128)} %bitcast.14, f32[4]{0:T(128)S(1)} %get-tuple-element.181, f32[]{:T(128)} %bitcast), kind=kLoop, calls=%fused_computation.99 | loop fusion | flops 1280 | bytes 3120 | tf_op jit(solution)/shard_map/add | solution.py:89
  (46 shorter events, 0.7 us)
Async XLA Ops:
  6.5 65.4 %all-gather.2.cloned.1.call-start = ((), (), s32[]{:S(2)}) async-start(), calls=%async_computation | async-start | bytes 1474560 | tf_op jit(solution)/shard_map/all_gather | solution.py:79
  7.3 8.0 %copy-start = (bf16[2,1,16,8,8192]{4,3,2,1,0:T(8,128)(2,1)S(1)}, bf16[2,1,16,8,8192]{4,3,2,1,0:T(8,128)(2,1)}, u32[]{:S(2)}) copy-start(bf16[2,1,16,8,8192]{4,3,2,1,0:T(8,128)(2,1)} %param.12) | copy-start | bytes 12582916
  15.3 1.7 %copy-start.1 = (bf16[2,1,16,8,128]{4,3,2,1,0:T(8,128)(2,1)S(1)}, bf16[2,1,16,8,128]{4,3,2,1,0:T(8,128)(2,1)}, u32[]{:S(2)}) copy-start(bf16[2,1,16,8,128]{4,3,2,1,0:T(8,128)(2,1)} %param.13) | copy-start | bytes 196612
  15.3 1.7 %copy-start.2 = (s32[16,8]{0,1:T(8,128)S(1)}, s32[16,8]{0,1:T(8,128)}, u32[]{:S(2)}) copy-start(s32[16,8]{0,1:T(8,128)} %param.17) | copy-start | bytes 1540
  15.3 2.4 %copy-start.4 = (s32[16]{0:T(128)S(1)}, s32[16]{0:T(128)}, u32[]{:S(2)}) copy-start(s32[16]{0:T(128)} %param.16) | copy-start | bytes 196
  44.2 25.7 %copy-start.5 = (u32[32]{0:T(128)S(1)}, u32[32]{0:T(128)}, u32[]{:S(2)}) copy-start(u32[32]{0:T(128)} %constant.70) | copy-start | bytes 388
  44.3 26.9 %copy-start.3 = (f32[2]{0:T(128)S(1)}, f32[2]{0:T(128)}, u32[]{:S(2)}) copy-start(f32[2]{0:T(128)} %param.19) | copy-start | bytes 28
Sparse Core Ops, SparseCore 0:
  9.3 27.2 all-gather.1
where the time goes:
time: 104 us; the launch traced here: 103 us
  matrix products  52.8 us (51%)
  blocking collectives  20.6 us (20%)
  between operations  14.8 us (14%)
  other arithmetic  10.2 us (10%)
  local copies, waits for them, and re-layouts  3.68 us (4%)
    dot_general x8, matrix products, one_group(): jnp.einsum('dk,edr->ekr', signs_table, scaled, preferred_element_type=jnp...  51.1 us
    unnamed x1, blocking collectives  20.6 us
    add x1, other arithmetic, local(): jnp.sqrt(adaptive_variance[snapshot_index, 0].astype(jnp.float32)) + 1e-08  8.02 us
  transfers between devices with their start and end apart: 1, of which 0 were waited for; matrix products, arithmetic and copies ran while one was open for 61% of the time, Pallas kernels for 0%

commit v1 on v0

v1 whole, which is shorter than its diff:
```python
import functools
import math

import jax
import jax.numpy as jnp
from jax import lax
from jax.experimental import pallas as pl
from jax.experimental.pallas import tpu as pltpu
from jax.sharding import PartitionSpec as P

F32 = jnp.float32
BF16 = jnp.bfloat16
TILE = 256
LANES = 128
AHEAD = 2


def feature_kernel(
    seed_ref,
    len_ref,
    mask_ref,
    act_ref,
    grad_hbm,
    var_hbm,
    out_ref,
    grad_raw,
    var_raw,
    lhs_ring,
    scale_ring,
    sign_ring,
    act_blocks,
    feat_buf,
    sems,
    *,
    ckpts,
    examples,
    slots,
    width,
    cols,
    tiles,
):
    chunk = tiles * TILE
    chunks = width // chunk
    total = ckpts * chunks
    rows = examples * slots
    pairs = examples // 2
    per_unit = pairs // 2
    sign_rows = sign_ring.shape[0]
    inv_root = 1.0 / math.sqrt(width)

    def copies(it):
        c, q = it // chunks, it % chunks
        at = pl.ds(pl.multiple_of(q * chunk, chunk), chunk)
        return (
            pltpu.make_async_copy(grad_hbm.at[c, :, at], grad_raw.at[c, :, at], sems.at[0, it]),
            pltpu.make_async_copy(var_hbm.at[c, at, :], var_raw.at[c, at, :], sems.at[1, it]),
        )

    for it in range(total):
        for copy in copies(it):
            copy.start()

    hash_base = (
        lax.axis_index("layer") * jnp.int32(668265263) + seed_ref[0] * jnp.int32(374761393)
    )

    act_blocks[...] = jnp.zeros_like(act_blocks)
    lhs_ring[:, LANES:] = jnp.zeros((chunk, TILE - LANES), BF16)
    slot_ids = lax.broadcasted_iota(jnp.int32, (slots, slots), 0)
    diagonal = slot_ids == lax.broadcasted_iota(jnp.int32, (slots, slots), 1)
    for pair in range(pairs):
        marks = []
        for e in (2 * pair, 2 * pair + 1):
            spread = jnp.where(diagonal, jnp.broadcast_to(mask_ref[e : e + 1, :], (slots, slots)), 0)
            marked = jnp.sum(spread.astype(F32), axis=1, keepdims=True) == 1.0
            marks.append(marked & (slot_ids[:, :1] < len_ref[e]))
        for c in range(ckpts):
            at = 2 * pair * slots
            first = jnp.where(marks[0], act_ref[c, at : at + slots, :].astype(F32), 0.0)
            second = jnp.where(marks[1], act_ref[c, at + slots : at + 2 * slots, :].astype(F32), 0.0)
            blank = jnp.zeros_like(first)
            act_blocks[c * pairs + pair, at : at + 2 * slots, :] = jnp.concatenate(
                [jnp.concatenate([first, blank], 1), jnp.concatenate([blank, second], 1)], 0
            ).astype(BF16)

    def prepare(it, t, part):
        c, q = it // chunks, it % chunks
        base = q * chunk + t * TILE
        here = t * TILE
        if part < 2:
            half = part * LANES
            src = grad_raw[c, :, pl.ds(pl.multiple_of(base + half, LANES), LANES)]
            lhs_ring[here + half : here + half + LANES, :LANES] = jnp.transpose(src)
        elif part == 2:
            moment = var_raw[c, pl.ds(pl.multiple_of(base, TILE), TILE), :].astype(F32)
            scale_ring[here : here + TILE, :] = 1.0 / (jnp.sqrt(moment) + 1e-08)
        else:
            d = lax.broadcasted_iota(jnp.int32, (sign_rows, TILE), 1) + base
            k = lax.broadcasted_iota(jnp.int32, (sign_rows, TILE), 0)
            m = d * jnp.int32(1103515245) + k * jnp.int32(12345) + hash_base
            m = m ^ (m >> 15)
            m = m * jnp.int32(747796405)
            m = m ^ (m >> 13)
            sign = (2 * ((m >> 7) & 1) - 1).astype(F32)
            sign_ring[:, here : here + TILE] = jnp.where(k < cols, sign, 0.0).astype(BF16)

    for copy in copies(0):
        copy.wait()
    for t in range(tiles - 1):
        for part in range(4):
            prepare(0, t, part)

    def scoped(*accs):
        depth = AHEAD + 1
        outer_acc = [accs[m * depth : (m + 1) * depth] for m in (0, 1)]
        proj_acc = [accs[2 * depth + m * per_unit : 2 * depth + (m + 1) * per_unit] for m in (0, 1)]
        steps = [(t, j) for t in range(tiles) for j in range(per_unit)]

        def outer(c, m, n):
            t, j = steps[n]
            pltpu.matmul_push_rhs(act_blocks[c * pairs + m * per_unit + j], 0, m)
            pltpu.matmul_acc_lhs(
                outer_acc[m][n % depth], lhs_ring[t * TILE : (t + 1) * TILE, :], load_staged_rhs=0
            )

        def project(m, n):
            t, j = steps[n]
            at = slice(t * TILE, (t + 1) * TILE)
            summed = pltpu.matmul_pop(outer_acc[m][n % depth])
            scale = scale_ring[at, :]
            scaled = (summed * jnp.concatenate([scale, scale], 1)).astype(BF16)
            pltpu.matmul_push_rhs(scaled, 1, m)
            pltpu.matmul_acc_lhs(proj_acc[m][j], sign_ring[:, at], load_staged_rhs=1)

        def one_chunk(c, q):
            it = c * chunks + q
            following = jnp.minimum(it + 1, total - 1)

            @pl.when(it + 1 < total)
            def _():
                for copy in copies(it + 1):
                    copy.wait()

            for n in range(AHEAD):
                for m in (0, 1):
                    outer(c, m, n)
            for n in range(len(steps)):
                for m in (0, 1):
                    if n + AHEAD < len(steps):
                        outer(c, m, n + AHEAD)
                    project(m, n)
                t, j = steps[n]
                for part in range(j * 4 // per_unit, (j + 1) * 4 // per_unit):
                    if t == 0:
                        prepare(it, tiles - 1, part)
                    else:
                        prepare(following, t - 1, part)

        def one_ckpt(c, carry):
            def body(q, inner):
                one_chunk(c, q)
                return inner

            lax.fori_loop(0, chunks, body, 0)
            for m in (0, 1):
                for j in range(per_unit):
                    total_sum = pltpu.matmul_pop(proj_acc[m][j])
                    for half in range(2):
                        e = 2 * (m * per_unit + j) + half
                        feat_buf[e] = total_sum[:cols, half * LANES : (half + 1) * LANES] * inv_root
            for k in range(cols):
                out_ref[c, :, k * LANES : (k + 1) * LANES] = feat_buf[:, k, :].astype(BF16)
            return carry

        lax.fori_loop(0, ckpts, one_ckpt, 0)

    pl.run_scoped(
        scoped,
        *[pltpu.ACC(m)((TILE, TILE), F32) for m in (0, 1) for _ in range(AHEAD + 1)],
        *[pltpu.ACC(m)((sign_rows, TILE), F32) for m in (0, 1) for _ in range(per_unit)],
    )


def features_of(seed, lengths, mask, act, grad, var, cols):
    ckpts, rows, width = grad.shape
    examples, slots = mask.shape
    tiles = 8
    chunk = tiles * TILE
    pairs = examples // 2
    sign_rows = -(-cols // 16) * 16
    vmem = pl.BlockSpec(memory_space=pltpu.VMEM)
    smem = pl.BlockSpec(memory_space=pltpu.SMEM)
    hbm = pl.BlockSpec(memory_space=pl.ANY)
    kernel = functools.partial(
        feature_kernel,
        ckpts=ckpts,
        examples=examples,
        slots=slots,
        width=width,
        cols=cols,
        tiles=tiles,
    )
    return pl.pallas_call(
        kernel,
        out_shape=jax.ShapeDtypeStruct((ckpts, examples, cols * LANES), BF16),
        in_specs=[smem, smem, vmem, vmem, hbm, hbm],
        out_specs=vmem,
        scratch_shapes=[
            pltpu.VMEM((ckpts, rows, width), BF16),
            pltpu.VMEM((ckpts, width, LANES), BF16),
            pltpu.VMEM((chunk, TILE), BF16),
            pltpu.VMEM((chunk, LANES), F32),
            pltpu.VMEM((sign_rows, chunk), BF16),
            pltpu.VMEM((ckpts * pairs, TILE, TILE), BF16),
            pltpu.VMEM((examples, cols, LANES), F32),
            pltpu.SemaphoreType.DMA((2, ckpts * width // chunk)),
        ],
        compiler_params=pltpu.CompilerParams(vmem_limit_bytes=40 << 20),
        cost_estimate=pl.CostEstimate(
            flops=40_000_000_000, bytes_accessed=9_000_000, transcendentals=0
        ),
        name="features",
    )(seed, lengths, mask, act, grad, var)


def score_kernel(feat_ref, hold_ref, out_ref, sums, *, parts):
    ckpts, examples, _ = feat_ref.shape
    held = hold_ref.shape[1]
    share = examples // parts
    me = lax.axis_index("layer")
    for c in range(ckpts):
        feat = feat_ref[c]
        sums[c, :, :held] = lax.dot_general(
            feat, hold_ref[c], (((1,), (1,)), ((), ())), preferred_element_type=F32
        )
        wide = feat.astype(F32)
        norm = jnp.sum(wide * wide, axis=1, keepdims=True)
        sums[c, :, held:] = jnp.broadcast_to(norm, (examples, sums.shape[2] - held))
        for step in range(parts):
            owner = lax.rem(me + step, parts)
            out_ref[step, c] = sums[c, pl.ds(owner * share, share), :]


def scores_of(feat, hold, parts):
    ckpts, examples, _ = feat.shape
    held = hold.shape[1]
    lanes = (held // LANES + 1) * LANES
    vmem = pl.BlockSpec(memory_space=pltpu.VMEM)
    return pl.pallas_call(
        functools.partial(score_kernel, parts=parts),
        out_shape=jax.ShapeDtypeStruct((parts, ckpts, examples // parts, lanes), F32),
        in_specs=[vmem, vmem],
        out_specs=vmem,
        scratch_shapes=[pltpu.VMEM((ckpts, examples, lanes), F32)],
        name="scores",
    )(feat, hold)


def solution(mesh):
    parts = mesh.shape["layer"]

    def local(grad, act, var, hold, lengths, mask, seed, weight):
        ckpts, _, examples, slots, width = grad.shape
        rank = act.shape[-1]
        cols = hold.shape[-1] // rank
        everyone = lax.all_gather(hold[:, 0], "dp", axis=1, tiled=True)
        feat = features_of(
            seed,
            lengths,
            mask,
            act.reshape(ckpts, examples * slots, rank),
            grad.reshape(ckpts, examples * slots, width),
            var[:, 0],
            cols,
        )
        pieces = scores_of(feat, everyone, parts)
        total = pieces[0]
        for step in range(1, parts):
            total = total + lax.ppermute(
                pieces[step], "layer", [(i, (i + step) % parts) for i in range(parts)]
            )
        held = everyone.shape[1]
        common, norm = total[:, :, :held], total[:, :, held : held + 1]
        return jnp.sum(weight[:, None, None] * common * lax.rsqrt(norm + 1e-06), axis=0)

    placed = (
        P(None, "layer", "dp", None, None),
        P(None, "layer", "dp", None, None),
        P(None, "layer", None, None),
        P(None, "layer", "dp", None),
        P("dp"),
        P("dp", None),
        P(),
        P(),
    )
    return jax.shard_map(
        local, mesh=mesh, in_specs=placed, out_specs=P(("dp", "layer"), None), check_vma=False
    )
```

time: 104 us -> 62.5 us (0.60)
  matrix products: 52.8 us -> 0 us
  Pallas kernels: 0 us -> 28.2 us
  blocking collectives: 20.6 us -> 0 us
  other arithmetic: 10.2 us -> 1.51 us
  starting transfers between devices: 0.01 us -> 6.07 us
  local copies, waits for them, and re-layouts: 3.68 us -> 8.04 us
  waiting for transfers between devices: 0.71 us -> 4.21 us
    dot_general x9 -> x0, matrix products: 52.8 us -> none  [the longest x8 51.1 us: one_group(): jnp.einsum('dk,edr->ekr', signs_table, scaled, preferred_element_type=jnp...]
    pallas_call x0 -> x2, Pallas kernels: none -> 28.2 us  [the longest x1 25.7 us: features_of(): pl.pallas_call(kernel, out_shape=jax.ShapeDtypeStruct((ckpts, examples, c...]
    unnamed x1 -> x0, blocking collectives: 20.6 us -> none
    add x2 -> x1, other arithmetic: 9.93 us -> 0.68 us  [local(): total + lax.ppermute(pieces[step], 'layer', [(i, (i + step) % parts) for...]
    unnamed x16 -> x13, local copies, waits for them, and re-layouts: 0.78 us -> 7.35 us
    ppermute x0 -> x3, starting transfers between devices: none -> 6.07 us  [local(): lax.ppermute(pieces[step], 'layer', [(i, (i + step) % parts) for i in ran...]
    ppermute x0 -> x3, waiting for transfers between devices: none -> 3.49 us  [local(): lax.ppermute(pieces[step], 'layer', [(i, (i + step) % parts) for i in ran...]
    slice x3 -> x0, local copies, waits for them, and re-layouts: 2.26 us -> none  [the longest x1 1.65 us: local(): output_gradient[snapshot_index, 0]]
  transfers between devices with their start and end apart: 1 -> 4, of which waited for: 0 -> 2; matrix products, arithmetic and copies ran while one was open for 61% -> 1% of each run, Pallas kernels for 0% -> 41%
where the time goes in v1:
time: 62.5 us; the launch traced here: 62.1 us
  Pallas kernels  28.2 us (45%)
  between operations  14.1 us (23%)
  local copies, waits for them, and re-layouts  8.04 us (13%)
  starting transfers between devices  6.07 us (10%)
  waiting for transfers between devices  4.21 us (7%)
  other arithmetic  1.51 us (2%)
    pallas_call x1, Pallas kernels, features_of(): pl.pallas_call(kernel, out_shape=jax.ShapeDtypeStruct((ckpts, examples, c...  25.7 us
    unnamed x13, local copies, waits for them, and re-layouts  7.35 us
    ppermute x3, starting transfers between devices, local(): lax.ppermute(pieces[step], 'layer', [(i, (i + step) % parts) for i in ran...  6.07 us
    ppermute x3, waiting for transfers between devices, local(): lax.ppermute(pieces[step], 'layer', [(i, (i + step) % parts) for i in ran...  3.49 us
    pallas_call x1, Pallas kernels, scores_of(): pl.pallas_call(functools.partial(score_kernel, parts=parts), out_shape=ja...  2.48 us
  transfers between devices with their start and end apart: 4, of which 2 were waited for; matrix products, arithmetic and copies ran while one was open for 1% of the time, Pallas kernels for 41%

profile of v1, /device:TPU:0, one launch (start us, length us, event | category | flops | bytes accessed | tf_op | source)
XLA Modules:
  0.0 62.1 jit_solution(2801569210977285669)
XLA Ops:
  6.5 0.0 all-gather.3.cloned.1.call-start
  6.5 0.7 %all-gather.3.cloned.1.call-update = ((bf16[2,1,8,5120]{3,2,0,1:T(8,128)(2,1)}), bf16[2,1,64,5120]{3,2,0,1:T(8,128)(2,1)}) async-update(((), (), s32[]{:S(2)}) %all-gather.3.cloned.1.call-start, bf16[2,1,8,5120]{3,2,0,1:T(8,128)(2,1)} %bitcast.23) | async-update | bytes 1638424
  7.9 0.8 %copy.11.mask_ref = s32[16,8]{1,0:T(8,128)S(1)} copy(s32[16,8]{0,1:T(8,128)} %param.13) | data formatting | bytes 1024 | tf_op args[5]
  8.7 0.0 copy-start.1
  8.7 2.2 %copy-done.1 = bf16[2,1,16,8,8192]{4,3,2,1,0:T(8,128)(2,1)S(1)} copy-done((bf16[2,1,16,8,8192]{4,3,2,1,0:T(8,128)(2,1)S(1)}, bf16[2,1,16,8,8192]{4,3,2,1,0:T(8,128)(2,1)}, u32[]{:S(2)}) %copy-start.1) | copy-done | bytes 4194328
  10.8 0.0 copy-start.2
  10.9 2.2 %copy-done.2 = bf16[2,1,8192,128]{3,2,1,0:T(8,128)(2,1)S(1)} copy-done((bf16[2,1,8192,128]{3,2,1,0:T(8,128)(2,1)S(1)}, bf16[2,1,8192,128]{3,2,1,0:T(8,128)(2,1)}, u32[]{:S(2)}) %copy-start.2) | copy-done | bytes 4194328
  13.0 0.8 %copy-done.3 = bf16[2,1,16,8,128]{4,3,2,1,0:T(8,128)(2,1)S(1)} copy-done((bf16[2,1,16,8,128]{4,3,2,1,0:T(8,128)(2,1)S(1)}, bf16[2,1,16,8,128]{4,3,2,1,0:T(8,128)(2,1)}, u32[]{:S(2)}) %copy-start.3) | copy-done | bytes 65560
  13.9 0.7 %copy-done.4 = s32[16]{0:T(128)S(1)} copy-done((s32[16]{0:T(128)S(1)}, s32[16]{0:T(128)}, u32[]{:S(2)}) %copy-start.4) | copy-done | bytes 88
  14.5 25.7 %features.1.feat_ref = bf16[2,16,5120]{2,1,0:T(8,128)(2,1)S(1)} custom-call(s32[1]{0:T(128)S(6)} %copy.13.seed_ref, s32[16]{0:T(128)S(1)} %copy-done.4, s32[16,8]{1,0:T(8,128)S(1)} %copy.11.mask_ref, bf16[2,128,128]{2,1,0:T(8,128)(2,1)S(1)} %bitcast.21, bf16[2,128,8192]{2,1,0:T(8,128)(2,1)S(1)} %bitcast.19, bf16[2,8192,128]{2,1,0:T(8,128)(2,1)S(1)} %bitcast.20), custom_call_target="tpu_custom_call" | custom-call | flops 40000000000 | bytes 9000000 | tf_op jit(solution)/shard_map/features/pallas_call | solution.py:203
  40.3 0.0 copy-start
  40.3 0.7 %copy-done = bf16[2,16,5120]{2,1,0:T(8,128)(2,1)} copy-done((bf16[2,16,5120]{2,1,0:T(8,128)(2,1)}, bf16[2,16,5120]{2,1,0:T(8,128)(2,1)S(1)}, u32[]{:S(2)}) %copy-start) | copy-done | bytes 327704
  41.0 2.5 %scores.1 = f32[4,2,4,128]{3,2,1,0:T(4,128)} custom-call(bf16[2,16,5120]{2,1,0:T(8,128)(2,1)} %copy-done, bf16[2,64,5120]{2,1,0:T(8,128)(2,1)} %bitcast.22), custom_call_target="tpu_custom_call" | custom-call | tf_op jit(solution)/shard_map/scores/pallas_call | solution.py:249
  43.5 0.7 %slice_bitcast_fusion.2 = (f32[2,4,128]{2,1,0:T(4,128)S(1)}, f32[2,4,128]{2,1,0:T(4,128)S(1)}, f32[2,4,128]{2,1,0:T(4,128)S(1)}) fusion(f32[4,2,4,128]{3,2,1,0:T(4,128)} %scores.1), kind=kLoop, calls=%fused_computation.8 | loop fusion | bytes 24576 | tf_op jit(solution)/shard_map/squeeze | solution.py:280
  44.2 3.0 %collective-permute-start = (f32[2,4,128]{2,1,0:T(4,128)S(1)}, f32[2,4,128]{2,1,0:T(4,128)S(1)}, u32[]{:S(2)}, u32[]{:S(2)}) collective-permute-start(f32[2,4,128]{2,1,0:T(4,128)S(1)} %get-tuple-element.5), channel_id=1, source_target_pairs={{0,1},{1,2},{2,3},{3,0},{4,5},{5,6},{6,7},{7,4},{8,9},{9,10},{10,1... | collective-permute-start | bytes 12296 | tf_op jit(solution)/shard_map/ppermute | solution.py:279
  47.2 2.0 %collective-permute-start.2 = (f32[2,4,128]{2,1,0:T(4,128)S(1)}, f32[2,4,128]{2,1,0:T(4,128)S(1)}, u32[]{:S(2)}, u32[]{:S(2)}) collective-permute-start(f32[2,4,128]{2,1,0:T(4,128)S(1)} %get-tuple-element.6), channel_id=1, source_target_pairs={{0,3},{1,0},{2,1},{3,2},{4,7},{5,4},{6,5},{7,6},{8,11},{9,8},{10,9... | collective-permute-start | bytes 12296 | tf_op jit(solution)/shard_map/ppermute | solution.py:279
  49.2 1.0 %collective-permute-start.1 = (f32[2,4,128]{2,1,0:T(4,128)S(1)}, f32[2,4,128]{2,1,0:T(4,128)S(1)}, u32[]{:S(2)}, u32[]{:S(2)}) collective-permute-start(f32[2,4,128]{2,1,0:T(4,128)S(1)} %get-tuple-element.7), channel_id=1, source_target_pairs={{0,2},{1,3},{2,0},{3,1},{4,6},{5,7},{6,4},{7,5},{8,10},{9,11},{10,... | collective-permute-start | bytes 12296 | tf_op jit(solution)/shard_map/ppermute | solution.py:279
  50.2 0.6 collective-permute-done
  50.8 0.0 collective-permute-done.2
  50.9 2.9 %collective-permute-done.1 = f32[2,4,128]{2,1,0:T(4,128)S(1)} collective-permute-done((f32[2,4,128]{2,1,0:T(4,128)S(1)}, f32[2,4,128]{2,1,0:T(4,128)S(1)}, u32[]{:S(2)}, u32[]{:S(2)}) %collective-permute-start.1) | collective-permute-done | bytes 4128 | tf_op jit(solution)/shard_map/ppermute | solution.py:279
  53.7 0.7 %fusion.6 = f32[2,4,128]{2,1,0:T(4,128)S(1)} fusion(f32[2,4,128]{2,1,0:T(4,128)S(1)} %collective-permute-done.2, f32[2,4,128]{2,1,0:T(4,128)S(1)} %collective-permute-done.1, f32[2,4,128]{2,1,0:T(4,128)S(1)} %collective-permute-done, f32[4,2,4,128]{3,2,1,0:T(4,128)} %scores.1), kind=kLoop, calls=%fused_computation.12 | loop fusion | flops 3072 | bytes 20480 | tf_op jit(solution)/shard_map/add | solution.py:279
  54.4 0.2 fusion.1
  54.6 0.0 copy-done.5
  54.6 0.7 %fusion.3 = f32[4,64]{1,0:T(4,128)} fusion(f32[2,4,128]{2,1,0:T(4,128)S(1)} %fusion.6, f32[2,4]{1,0:T(2,128)S(1)} %fusion.1, f32[2]{0:T(128)S(1)} %copy-done.5), kind=kLoop, calls=%fused_computation.5 | loop fusion | flops 1280 | bytes 3112 | tf_op jit(solution)/shard_map/reduce_sum | solution.py:284
  (4 shorter events, 0.0 us)
Async XLA Ops:
  6.5 34.5 %all-gather.3.cloned.1.call-start = ((), (), s32[]{:S(2)}) async-start(), calls=%async_computation | async-start | bytes 1474560 | tf_op jit(solution)/shard_map/all_gather | solution.py:266
  8.7 2.2 %copy-start.1 = (bf16[2,1,16,8,8192]{4,3,2,1,0:T(8,128)(2,1)S(1)}, bf16[2,1,16,8,8192]{4,3,2,1,0:T(8,128)(2,1)}, u32[]{:S(2)}) copy-start(bf16[2,1,16,8,8192]{4,3,2,1,0:T(8,128)(2,1)} %param.8) | copy-start | bytes 12582916
  10.8 2.2 %copy-start.2 = (bf16[2,1,8192,128]{3,2,1,0:T(8,128)(2,1)S(1)}, bf16[2,1,8192,128]{3,2,1,0:T(8,128)(2,1)}, u32[]{:S(2)}) copy-start(bf16[2,1,8192,128]{3,2,1,0:T(8,128)(2,1)} %param.10) | copy-start | bytes 12582916
  13.0 0.8 %copy-start.3 = (bf16[2,1,16,8,128]{4,3,2,1,0:T(8,128)(2,1)S(1)}, bf16[2,1,16,8,128]{4,3,2,1,0:T(8,128)(2,1)}, u32[]{:S(2)}) copy-start(bf16[2,1,16,8,128]{4,3,2,1,0:T(8,128)(2,1)} %param.9) | copy-start | bytes 196612
  13.9 0.7 %copy-start.4 = (s32[16]{0:T(128)S(1)}, s32[16]{0:T(128)}, u32[]{:S(2)}) copy-start(s32[16]{0:T(128)} %len_ref.1) | copy-start | bytes 196
  14.5 40.0 %copy-start.5 = (f32[2]{0:T(128)S(1)}, f32[2]{0:T(128)}, u32[]{:S(2)}) copy-start(f32[2]{0:T(128)} %param.15) | copy-start | bytes 28
  40.3 0.7 %copy-start = (bf16[2,16,5120]{2,1,0:T(8,128)(2,1)}, bf16[2,16,5120]{2,1,0:T(8,128)(2,1)S(1)}, u32[]{:S(2)}) copy-start(bf16[2,16,5120]{2,1,0:T(8,128)(2,1)S(1)} %features.1.feat_ref) | copy-start | bytes 983044
  44.2 6.7 %collective-permute-start = (f32[2,4,128]{2,1,0:T(4,128)S(1)}, f32[2,4,128]{2,1,0:T(4,128)S(1)}, u32[]{:S(2)}, u32[]{:S(2)}) collective-permute-start(f32[2,4,128]{2,1,0:T(4,128)S(1)} %get-tuple-element.5), channel_id=1, source_target_pairs={{0,1},{1,2},{2,3},{3,0},{4,5},{5,6},{6,7},{7,4},{8,9},{9,10},{10,1... | collective-permute-start | bytes 12296 | tf_op jit(solution)/shard_map/ppermute | solution.py:279
  47.2 3.7 %collective-permute-start.2 = (f32[2,4,128]{2,1,0:T(4,128)S(1)}, f32[2,4,128]{2,1,0:T(4,128)S(1)}, u32[]{:S(2)}, u32[]{:S(2)}) collective-permute-start(f32[2,4,128]{2,1,0:T(4,128)S(1)} %get-tuple-element.6), channel_id=1, source_target_pairs={{0,3},{1,0},{2,1},{3,2},{4,7},{5,4},{6,5},{7,6},{8,11},{9,8},{10,9... | collective-permute-start | bytes 12296 | tf_op jit(solution)/shard_map/ppermute | solution.py:279
  49.2 4.5 %collective-permute-start.1 = (f32[2,4,128]{2,1,0:T(4,128)S(1)}, f32[2,4,128]{2,1,0:T(4,128)S(1)}, u32[]{:S(2)}, u32[]{:S(2)}) collective-permute-start(f32[2,4,128]{2,1,0:T(4,128)S(1)} %get-tuple-element.7), channel_id=1, source_target_pairs={{0,2},{1,3},{2,0},{3,1},{4,6},{5,7},{6,4},{7,5},{8,10},{9,11},{10,... | collective-permute-start | bytes 12296 | tf_op jit(solution)/shard_map/ppermute | solution.py:279
Sparse Core Ops, SparseCore 0:
  9.3 27.2 all-gather.2

commit v2 on v1

--- a/solution.py
+++ b/solution.py
@@ -16,13 +16,17 @@
 
 
 def feature_kernel(
+    seed_hbm,
+    len_hbm,
+    mask_hbm,
+    act_hbm,
+    grad_hbm,
+    var_hbm,
+    out_ref,
     seed_ref,
     len_ref,
     mask_ref,
     act_ref,
-    grad_hbm,
-    var_hbm,
-    out_ref,
     grad_raw,
     var_raw,
     lhs_ring,
@@ -30,6 +34,7 @@
     sign_ring,
     act_blocks,
     feat_buf,
+    small_sems,
     sems,
     *,
     ckpts,
@@ -56,24 +61,37 @@
             pltpu.make_async_copy(var_hbm.at[c, at, :], var_raw.at[c, at, :], sems.at[1, it]),
         )
 
+    small = [
+        pltpu.make_async_copy(src, dst, small_sems.at[i])
+        for i, (src, dst) in enumerate(
+            (
+                (seed_hbm, seed_ref),
+                (len_hbm, len_ref),
+                (mask_hbm, mask_ref),
+                (act_hbm, act_ref),
+            )
+        )
+    ]
+    for copy in small:
+        copy.start()
     for it in range(total):
         for copy in copies(it):
             copy.start()
+    act_blocks[...] = jnp.zeros_like(act_blocks)
+    lhs_ring[:, LANES:] = jnp.zeros((chunk, TILE - LANES), BF16)
+    for copy in small:
+        copy.wait()
 
     hash_base = (
         lax.axis_index("layer") * jnp.int32(668265263) + seed_ref[0] * jnp.int32(374761393)
     )
 
-    act_blocks[...] = jnp.zeros_like(act_blocks)
-    lhs_ring[:, LANES:] = jnp.zeros((chunk, TILE - LANES), BF16)
-    slot_ids = lax.broadcasted_iota(jnp.int32, (slots, slots), 0)
-    diagonal = slot_ids == lax.broadcasted_iota(jnp.int32, (slots, slots), 1)
+    slot_ids = lax.broadcasted_iota(jnp.int32, (slots, 1), 0)
     for pair in range(pairs):
-        marks = []
-        for e in (2 * pair, 2 * pair + 1):
-            spread = jnp.where(diagonal, jnp.broadcast_to(mask_ref[e : e + 1, :], (slots, slots)), 0)
-            marked = jnp.sum(spread.astype(F32), axis=1, keepdims=True) == 1.0
-            marks.append(marked & (slot_ids[:, :1] < len_ref[e]))
+        marks = [
+            (mask_ref[:, e : e + 1] == 1) & (slot_ids < len_ref[e])
+            for e in (2 * pair, 2 * pair + 1)
+        ]
         for c in range(ckpts):
             at = 2 * pair * slots
             first = jnp.where(marks[0], act_ref[c, at : at + slots, :].astype(F32), 0.0)
@@ -183,14 +201,13 @@
 
 def features_of(seed, lengths, mask, act, grad, var, cols):
     ckpts, rows, width = grad.shape
-    examples, slots = mask.shape
+    slots, examples = mask.shape
     tiles = 8
     chunk = tiles * TILE
     pairs = examples // 2
     sign_rows = -(-cols // 16) * 16
     vmem = pl.BlockSpec(memory_space=pltpu.VMEM)
-    smem = pl.BlockSpec(memory_space=pltpu.SMEM)
-    hbm = pl.BlockSpec(memory_space=pl.ANY)
+    hbm = pl.BlockSpec(memory_space=pltpu.HBM)
     kernel = functools.partial(
         feature_kernel,
         ckpts=ckpts,
@@ -203,9 +220,13 @@
     return pl.pallas_call(
         kernel,
         out_shape=jax.ShapeDtypeStruct((ckpts, examples, cols * LANES), BF16),
-        in_specs=[smem, smem, vmem, vmem, hbm, hbm],
+        in_specs=[hbm] * 6,
         out_specs=vmem,
         scratch_shapes=[
+            pltpu.SMEM(seed.shape, jnp.int32),
+            pltpu.SMEM(lengths.shape, jnp.int32),
+            pltpu.VMEM(mask.shape, jnp.int32),
+            pltpu.VMEM(act.shape, BF16),
             pltpu.VMEM((ckpts, rows, width), BF16),
             pltpu.VMEM((ckpts, width, LANES), BF16),
             pltpu.VMEM((chunk, TILE), BF16),
@@ -213,9 +234,10 @@
             pltpu.VMEM((sign_rows, chunk), BF16),
             pltpu.VMEM((ckpts * pairs, TILE, TILE), BF16),
             pltpu.VMEM((examples, cols, LANES), F32),
+            pltpu.SemaphoreType.DMA((4,)),
             pltpu.SemaphoreType.DMA((2, ckpts * width // chunk)),
         ],
-        compiler_params=pltpu.CompilerParams(vmem_limit_bytes=40 << 20),
+        compiler_params=pltpu.CompilerParams(vmem_limit_bytes=57 << 20),
         cost_estimate=pl.CostEstimate(
             flops=40_000_000_000, bytes_accessed=9_000_000, transcendentals=0
         ),
@@ -223,65 +245,126 @@
     )(seed, lengths, mask, act, grad, var)
 
 
-def score_kernel(feat_ref, hold_ref, out_ref, sums, *, parts):
-    ckpts, examples, _ = feat_ref.shape
-    held = hold_ref.shape[1]
+def score_kernel(*refs, groups, parts):
+    feat_ref, holds, outs = refs[0], refs[1 : 1 + groups], refs[1 + groups : 1 + groups + parts]
+    hold_ref, sums, sems = refs[1 + groups + parts :]
+    ckpts, examples, width = feat_ref.shape
+    peers, block = hold_ref.shape[1:3]
+    members = peers // groups
+    held = peers * block
     share = examples // parts
+    mine = lax.axis_index("dp")
     me = lax.axis_index("layer")
+    group, member = mine // members, lax.rem(mine, members)
+    copies = []
+    for step in range(groups):
+        source = lax.rem(group + groups - step, groups) * members
+        for turn in range(members):
+            index = source + lax.rem(member + turn, members)
+            copies.append(
+                pltpu.make_async_copy(
+                    holds[step].at[:, turn], hold_ref.at[:, index], sems.at[step, turn]
+                )
+            )
+    for copy in copies:
+        copy.start()
     for c in range(ckpts):
-        feat = feat_ref[c]
-        sums[c, :, :held] = lax.dot_general(
-            feat, hold_ref[c], (((1,), (1,)), ((), ())), preferred_element_type=F32
-        )
-        wide = feat.astype(F32)
+        wide = feat_ref[c].astype(F32)
         norm = jnp.sum(wide * wide, axis=1, keepdims=True)
         sums[c, :, held:] = jnp.broadcast_to(norm, (examples, sums.shape[2] - held))
+    for copy in copies:
+        copy.wait()
+    for c in range(ckpts):
+        sums[c, :, :held] = lax.dot_general(
+            feat_ref[c],
+            hold_ref[c].reshape(held, width),
+            (((1,), (1,)), ((), ())),
+            preferred_element_type=F32,
+        )
         for step in range(parts):
             owner = lax.rem(me + step, parts)
-            out_ref[step, c] = sums[c, pl.ds(owner * share, share), :]
-
-
-def scores_of(feat, hold, parts):
-    ckpts, examples, _ = feat.shape
-    held = hold.shape[1]
-    lanes = (held // LANES + 1) * LANES
+            outs[step][c] = sums[c, pl.ds(owner * share, share), :]
+
+
+def scores_of(feat, holds, parts):
+    ckpts, examples, width = feat.shape
+    groups = len(holds)
+    members, block = holds[0].shape[1:3]
+    peers = groups * members
+    lanes = (peers * block // LANES + 1) * LANES
     vmem = pl.BlockSpec(memory_space=pltpu.VMEM)
+    anywhere = pl.BlockSpec(memory_space=pl.ANY)
     return pl.pallas_call(
-        functools.partial(score_kernel, parts=parts),
-        out_shape=jax.ShapeDtypeStruct((parts, ckpts, examples // parts, lanes), F32),
-        in_specs=[vmem, vmem],
-        out_specs=vmem,
-        scratch_shapes=[pltpu.VMEM((ckpts, examples, lanes), F32)],
+        functools.partial(score_kernel, groups=groups, parts=parts),
+        out_shape=[jax.ShapeDtypeStruct((ckpts, examples // parts, lanes), F32)] * parts,
+        in_specs=[vmem] + [anywhere] * groups,
+        out_specs=[vmem] * parts,
+        scratch_shapes=[
+            pltpu.VMEM((ckpts, peers, block, width), BF16),
+            pltpu.VMEM((ckpts, examples, lanes), F32),
+            pltpu.SemaphoreType.DMA((groups, members)),
+        ],
+        compiler_params=pltpu.CompilerParams(vmem_limit_bytes=12 << 20),
         name="scores",
-    )(feat, hold)
+    )(feat, *holds)
+
+
+def finish_kernel(*refs):
+    weight_ref, pieces, out_ref = refs[0], refs[1:-1], refs[-1]
+    held = out_ref.shape[1]
+    result = jnp.zeros(out_ref.shape, F32)
+    for c in range(pieces[0].shape[0]):
+        total = pieces[0][c]
+        for piece in pieces[1:]:
+            total = total + piece[c]
+        scale = weight_ref[c] * lax.rsqrt(total[:, held : held + 1] + 1e-06)
+        result = result + total[:, :held] * scale
+    out_ref[...] = result
 
 
 def solution(mesh):
     parts = mesh.shape["layer"]
+    peers = mesh.shape["dp"]
 
     def local(grad, act, var, hold, lengths, mask, seed, weight):
         ckpts, _, examples, slots, width = grad.shape
         rank = act.shape[-1]
         cols = hold.shape[-1] // rank
-        everyone = lax.all_gather(hold[:, 0], "dp", axis=1, tiled=True)
+        members = 2 if peers % 2 == 0 else 1
+        groups = peers // members
+        gathered = [hold[:, 0]]
+        for turn in range(1, members):
+            ring = [
+                (i, i // members * members + (i + members - turn) % members) for i in range(peers)
+            ]
+            gathered.append(lax.ppermute(hold[:, 0], "dp", ring))
+        own = jnp.stack(gathered, axis=1)
+        holds = [own]
+        for step in range(1, groups):
+            ring = [(i, (i + step * members) % peers) for i in range(peers)]
+            holds.append(lax.ppermute(own, "dp", ring))
         feat = features_of(
             seed,
             lengths,
-            mask,
+            mask.T,
             act.reshape(ckpts, examples * slots, rank),
             grad.reshape(ckpts, examples * slots, width),
             var[:, 0],
             cols,
         )
-        pieces = scores_of(feat, everyone, parts)
-        total = pieces[0]
+        pieces = list(scores_of(feat, holds, parts))
         for step in range(1, parts):
-            total = total + lax.ppermute(
-                pieces[step], "layer", [(i, (i + step) % parts) for i in range(parts)]
-            )
-        held = everyone.shape[1]
-        common, norm = total[:, :, :held], total[:, :, held : held + 1]
-        return jnp.sum(weight[:, None, None] * common * lax.rsqrt(norm + 1e-06), axis=0)
+            ring = [(i, (i + step) % parts) for i in range(parts)]
+            pieces[step] = lax.ppermute(pieces[step], "layer", ring)
+        vmem = pl.BlockSpec(memory_space=pltpu.VMEM)
+        return pl.pallas_call(
+            finish_kernel,
+            out_shape=jax.ShapeDtypeStruct((examples // parts, peers * hold.shape[2]), F32),
+            in_specs=[pl.BlockSpec(memory_space=pltpu.SMEM)] + [vmem] * parts,
+            out_specs=vmem,
+            compiler_params=pltpu.CompilerParams(vmem_limit_bytes=12 << 20),
+            name="finish",
+        )(weight, *pieces)
 
     placed = (
         P(None, "layer", "dp", None, None),

time: 62.5 us -> 48.3 us (0.77)
  between operations: 14.1 us -> 0.71 us
  local copies, waits for them, and re-layouts: 8.04 us -> 0.97 us
  starting transfers between devices: 6.07 us -> 11 us
  Pallas kernels: 28.2 us -> 31.6 us
  waiting for transfers between devices: 4.21 us -> 2.86 us
    unnamed x13 -> x4, local copies, waits for them, and re-layouts: 7.35 us -> 0.97 us
    ppermute x3 -> x7, starting transfers between devices: 6.07 us -> 11 us  [the longest x3 5.57 us: local(): pieces[step] = lax.ppermute(pieces[step], 'layer', ring)]
    pallas_call x1, Pallas kernels: 25.7 us -> 28.9 us  [features_of(): pl.pallas_call(kernel, out_shape=jax.ShapeDtypeStruct((ckpts, examples, c...]
    another operation x0 -> x1, other arithmetic: none -> 0.95 us  [local(): own = jnp.stack(gathered, axis=1)]
    unnamed x1 -> x0, waiting for transfers between devices: 0.71 us -> none
    squeeze x1 -> x0, local copies, waits for them, and re-layouts: 0.69 us -> none  [local(): pieces[step]]
    add x1 -> x0, other arithmetic: 0.68 us -> none  [local(): total + lax.ppermute(pieces[step], 'layer', [(i, (i + step) % parts) for...]
    reduce_sum x1 -> x0, other arithmetic: 0.66 us -> none  [local(): jnp.sum(weight[:, None, None] * common * lax.rsqrt(norm + 1e-06), axis=0)]
  transfers between devices with their start and end apart: 4 -> 7, of which waited for: 2 -> 3; matrix products, arithmetic and copies ran while one was open for 1% -> 0% of each run, Pallas kernels for 41% -> 60%
where the time goes in v2:
time: 48.3 us; the launch traced here: 48.1 us
  Pallas kernels  31.6 us (65%)
  starting transfers between devices  11 us (23%)
  waiting for transfers between devices  2.86 us (6%)
  local copies, waits for them, and re-layouts  0.97 us (2%)
  other arithmetic  0.95 us (2%)
  between operations  0.71 us (1%)
    pallas_call x1, Pallas kernels, features_of(): pl.pallas_call(kernel, out_shape=jax.ShapeDtypeStruct((ckpts, examples, c...  28.9 us
    ppermute x3, starting transfers between devices, local(): pieces[step] = lax.ppermute(pieces[step], 'layer', ring)  5.57 us
    ppermute x3, starting transfers between devices, local(): holds.append(lax.ppermute(own, 'dp', ring))  4.96 us
    ppermute x3, waiting for transfers between devices, local(): pieces[step] = lax.ppermute(pieces[step], 'layer', ring)  2.27 us
    pallas_call x1, Pallas kernels, scores_of(): pl.pallas_call(functools.partial(score_kernel, groups=groups, parts=parts...  1.53 us
    pallas_call x1, Pallas kernels, local(): pl.pallas_call(finish_kernel, out_shape=jax.ShapeDtypeStruct((examples //...  1.2 us
    unnamed x4, local copies, waits for them, and re-layouts  0.97 us
  transfers between devices with their start and end apart: 7, of which 3 were waited for; matrix products, arithmetic and copies ran while one was open for 0% of the time, Pallas kernels for 60%

profile of v2, /device:TPU:0, one launch (start us, length us, event | category | flops | bytes accessed | tf_op | source)
XLA Modules:
  0.0 48.1 jit_solution(11681749948153759334)
XLA Ops:
  0.0 0.5 collective-permute-start
  1.1 0.6 %collective-permute-done = bf16[2,8,5120]{2,1,0:T(8,128)(2,1)S(1)} collective-permute-done((bf16[2,8,5120]{2,1,0:T(8,128)(2,1)}, bf16[2,8,5120]{2,1,0:T(8,128)(2,1)S(1)}, u32[]{:S(2)}, u32[]{:S(2)}) %collective-permute-start) | collective-permute-done | bytes 163872 | tf_op jit(solution)/shard_map/ppermute | solution.py:340
  1.7 0.9 %pad_maximum_fusion.refs_1_ = bf16[2,2,8,5120]{3,2,1,0:T(8,128)(2,1)S(1)} fusion(bf16[2,1,8,5120]{3,2,1,0:T(8,128)(2,1)S(1)} %bitcast.7, bf16[2,1,8,5120]{3,2,1,0:T(8,128)(2,1)} %param.11), kind=kLoop, calls=%fused_computation | loop fusion | flops 163840 | bytes 655360 | tf_op jit(solution)/shard_map/stack | solution.py:341
  2.6 3.9 %collective-permute-start.3 = (bf16[2,2,8,5120]{3,2,1,0:T(8,128)(2,1)S(1)}, bf16[2,2,8,5120]{3,2,1,0:T(8,128)(2,1)S(1)}, u32[]{:S(2)}, u32[]{:S(2)}) collective-permute-start(bf16[2,2,8,5120]{3,2,1,0:T(8,128)(2,1)S(1)} %pad_maximum_fusion.refs_1_), channel_id=1, source_target_pairs={{0,24},{4,28},{8,0},{12,4},{16,8},{20,12},{24,16},{28,20},{1,25},{... | collective-permute-start | bytes 983048 | tf_op jit(solution)/shard_map/ppermute | solution.py:345
  6.5 0.5 %collective-permute-start.2 = (bf16[2,2,8,5120]{3,2,1,0:T(8,128)(2,1)S(1)}, bf16[2,2,8,5120]{3,2,1,0:T(8,128)(2,1)S(1)}, u32[]{:S(2)}, u32[]{:S(2)}) collective-permute-start(bf16[2,2,8,5120]{3,2,1,0:T(8,128)(2,1)S(1)} %pad_maximum_fusion.refs_1_), channel_id=1, source_target_pairs={{0,16},{4,20},{8,24},{12,28},{16,0},{20,4},{24,8},{28,12},{1,17},{... | collective-permute-start | bytes 983048 | tf_op jit(solution)/shard_map/ppermute | solution.py:345
  7.0 0.6 %collective-permute-start.1 = (bf16[2,2,8,5120]{3,2,1,0:T(8,128)(2,1)S(1)}, bf16[2,2,8,5120]{3,2,1,0:T(8,128)(2,1)S(1)}, u32[]{:S(2)}, u32[]{:S(2)}) collective-permute-start(bf16[2,2,8,5120]{3,2,1,0:T(8,128)(2,1)S(1)} %pad_maximum_fusion.refs_1_), channel_id=1, source_target_pairs={{0,8},{4,12},{8,16},{12,20},{16,24},{20,28},{24,0},{28,4},{1,9},{5... | collective-permute-start | bytes 983048 | tf_op jit(solution)/shard_map/ppermute | solution.py:345
  7.6 0.0 copy-start.1
  7.6 28.9 %features.1.refs_0_ = bf16[2,16,5120]{2,1,0:T(8,128)(2,1)} custom-call(s32[1]{0:T(128)S(6)} %copy.9.seed_hbm, s32[16]{0:T(128)} %len_hbm.1, s32[8,16]{1,0:T(8,128)} %bitcast.11, bf16[2,128,128]{2,1,0:T(8,128)(2,1)} %bitcast.10, bf16[2,128,8192]{2,1,0:T(8,128)(2,1)} %bitcast.8, bf16[2,8192,128]{2,1,0:T(8,128)(2,1)} %bitcast.9), custom_call_target="tpu_custom_call" | custom-call | flops 40000000000 | bytes 9000000 | tf_op jit(solution)/shard_map/features/pallas_call | solution.py:220
  36.5 0.0 collective-permute-done.3.refs_4_
  36.5 0.0 collective-permute-done.2.refs_3_
  36.6 0.0 collective-permute-done.1.refs_2_
  36.6 0.0 copy-start
  36.6 1.0 %copy-done = bf16[2,16,5120]{2,1,0:T(8,128)(2,1)S(1)} copy-done((bf16[2,16,5120]{2,1,0:T(8,128)(2,1)S(1)}, bf16[2,16,5120]{2,1,0:T(8,128)(2,1)}, u32[]{:S(2)}) %copy-start) | copy-done | bytes 327704
  37.5 1.5 %scores.1 = (f32[2,4,128]{2,1,0:T(4,128)S(1)}, f32[2,4,128]{2,1,0:T(4,128)S(1)}, f32[2,4,128]{2,1,0:T(4,128)S(1)}, f32[2,4,128]{2,1,0:T(4,128)S(1)}) custom-call(bf16[2,16,5120]{2,1,0:T(8,128)(2,1)S(1)} %copy-done, bf16[2,2,8,5120]{3,2,1,0:T(8,128)(2,1)S(1)} %pad_maximum_fusion.refs_1_, bf16[2,2,8,5120]{3,2,1,0:T(8,128)(2,1)S(1)} %collective-permute-done.1.refs_2_, ...), custom_call_target="tpu_custom_call" | custom-call | tf_op jit(solution)/shard_map/scores/pallas_call | solution.py:297
  39.1 1.6 %collective-permute-start.4 = (f32[2,4,128]{2,1,0:T(4,128)S(1)}, f32[2,4,128]{2,1,0:T(4,128)S(1)}, u32[]{:S(2)}, u32[]{:S(2)}) collective-permute-start(f32[2,4,128]{2,1,0:T(4,128)S(1)} %get-tuple-element.10), channel_id=1, source_target_pairs={{0,1},{1,2},{2,3},{3,0},{4,5},{5,6},{6,7},{7,4},{8,9},{9,10},{10,1... | collective-permute-start | bytes 12296 | tf_op jit(solution)/shard_map/ppermute | solution.py:358
  40.7 2.6 %collective-permute-start.5 = (f32[2,4,128]{2,1,0:T(4,128)S(1)}, f32[2,4,128]{2,1,0:T(4,128)S(1)}, u32[]{:S(2)}, u32[]{:S(2)}) collective-permute-start(f32[2,4,128]{2,1,0:T(4,128)S(1)} %get-tuple-element.11), channel_id=1, source_target_pairs={{0,2},{1,3},{2,0},{3,1},{4,6},{5,7},{6,4},{7,5},{8,10},{9,11},{10,... | collective-permute-start | bytes 12296 | tf_op jit(solution)/shard_map/ppermute | solution.py:358
  43.3 1.3 %collective-permute-start.6 = (f32[2,4,128]{2,1,0:T(4,128)S(1)}, f32[2,4,128]{2,1,0:T(4,128)S(1)}, u32[]{:S(2)}, u32[]{:S(2)}) collective-permute-start(f32[2,4,128]{2,1,0:T(4,128)S(1)} %get-tuple-element.12), channel_id=1, source_target_pairs={{0,3},{1,0},{2,1},{3,2},{4,7},{5,4},{6,5},{7,6},{8,11},{9,8},{10,9... | collective-permute-start | bytes 12296 | tf_op jit(solution)/shard_map/ppermute | solution.py:358
  44.6 0.0 collective-permute-done.4.refs_2_
  44.6 0.6 %collective-permute-done.5.refs_3_ = f32[2,4,128]{2,1,0:T(4,128)S(1)} collective-permute-done((f32[2,4,128]{2,1,0:T(4,128)S(1)}, f32[2,4,128]{2,1,0:T(4,128)S(1)}, u32[]{:S(2)}, u32[]{:S(2)}) %collective-permute-start.5) | collective-permute-done | bytes 4128 | tf_op jit(solution)/shard_map/ppermute | solution.py:358
  45.2 1.7 %collective-permute-done.6.refs_4_ = f32[2,4,128]{2,1,0:T(4,128)S(1)} collective-permute-done((f32[2,4,128]{2,1,0:T(4,128)S(1)}, f32[2,4,128]{2,1,0:T(4,128)S(1)}, u32[]{:S(2)}, u32[]{:S(2)}) %collective-permute-start.6) | collective-permute-done | bytes 4128 | tf_op jit(solution)/shard_map/ppermute | solution.py:358
  46.9 0.0 copy-done.1
  46.9 1.2 %finish.1 = f32[4,64]{1,0:T(4,128)} custom-call(f32[2]{0:T(128)S(1)} %copy-done.1, f32[2,4,128]{2,1,0:T(4,128)S(1)} %get-tuple-element.9.refs_1_, f32[2,4,128]{2,1,0:T(4,128)S(1)} %collective-permute-done.4.refs_2_, f32[2,4,128]{2,1,0:T(4,128)S(1)} %collective-permute-done.5.refs_3_, f32[2,4,128]{2,1,0:T(4,128)S(1)} %collective-permute-done.6.refs_4_), custom_call_target="tpu_custom_call" | custom-call | tf_op jit(solution)/shard_map/finish/pallas_call | solution.py:360
Async XLA Ops:
  0.0 1.7 %collective-permute-start = (bf16[2,8,5120]{2,1,0:T(8,128)(2,1)}, bf16[2,8,5120]{2,1,0:T(8,128)(2,1)S(1)}, u32[]{:S(2)}, u32[]{:S(2)}) collective-permute-start(bf16[2,8,5120]{2,1,0:T(8,128)(2,1)} %bitcast.6), channel_id=1, source_target_pairs={{0,4},{4,0},{8,12},{12,8},{16,20},{20,16},{24,28},{28,24},{1,5},{5... | collective-permute-start | bytes 491528 | tf_op jit(solution)/shard_map/ppermute | solution.py:340
  2.6 33.9 %collective-permute-start.3 = (bf16[2,2,8,5120]{3,2,1,0:T(8,128)(2,1)S(1)}, bf16[2,2,8,5120]{3,2,1,0:T(8,128)(2,1)S(1)}, u32[]{:S(2)}, u32[]{:S(2)}) collective-permute-start(bf16[2,2,8,5120]{3,2,1,0:T(8,128)(2,1)S(1)} %pad_maximum_fusion.refs_1_), channel_id=1, source_target_pairs={{0,24},{4,28},{8,0},{12,4},{16,8},{20,12},{24,16},{28,20},{1,25},{... | collective-permute-start | bytes 983048 | tf_op jit(solution)/shard_map/ppermute | solution.py:345
  6.5 30.0 %collective-permute-start.2 = (bf16[2,2,8,5120]{3,2,1,0:T(8,128)(2,1)S(1)}, bf16[2,2,8,5120]{3,2,1,0:T(8,128)(2,1)S(1)}, u32[]{:S(2)}, u32[]{:S(2)}) collective-permute-start(bf16[2,2,8,5120]{3,2,1,0:T(8,128)(2,1)S(1)} %pad_maximum_fusion.refs_1_), channel_id=1, source_target_pairs={{0,16},{4,20},{8,24},{12,28},{16,0},{20,4},{24,8},{28,12},{1,17},{... | collective-permute-start | bytes 983048 | tf_op jit(solution)/shard_map/ppermute | solution.py:345
  7.0 29.5 %collective-permute-start.1 = (bf16[2,2,8,5120]{3,2,1,0:T(8,128)(2,1)S(1)}, bf16[2,2,8,5120]{3,2,1,0:T(8,128)(2,1)S(1)}, u32[]{:S(2)}, u32[]{:S(2)}) collective-permute-start(bf16[2,2,8,5120]{3,2,1,0:T(8,128)(2,1)S(1)} %pad_maximum_fusion.refs_1_), channel_id=1, source_target_pairs={{0,8},{4,12},{8,16},{12,20},{16,24},{20,28},{24,0},{28,4},{1,9},{5... | collective-permute-start | bytes 983048 | tf_op jit(solution)/shard_map/ppermute | solution.py:345
  7.6 39.3 %copy-start.1 = (f32[2]{0:T(128)S(1)}, f32[2]{0:T(128)}, u32[]{:S(2)}) copy-start(f32[2]{0:T(128)} %refs_0_.1) | copy-start | bytes 28
  36.6 1.0 %copy-start = (bf16[2,16,5120]{2,1,0:T(8,128)(2,1)S(1)}, bf16[2,16,5120]{2,1,0:T(8,128)(2,1)}, u32[]{:S(2)}) copy-start(bf16[2,16,5120]{2,1,0:T(8,128)(2,1)} %features.1.refs_0_) | copy-start | bytes 983044
  39.1 5.6 %collective-permute-start.4 = (f32[2,4,128]{2,1,0:T(4,128)S(1)}, f32[2,4,128]{2,1,0:T(4,128)S(1)}, u32[]{:S(2)}, u32[]{:S(2)}) collective-permute-start(f32[2,4,128]{2,1,0:T(4,128)S(1)} %get-tuple-element.10), channel_id=1, source_target_pairs={{0,1},{1,2},{2,3},{3,0},{4,5},{5,6},{6,7},{7,4},{8,9},{9,10},{10,1... | collective-permute-start | bytes 12296 | tf_op jit(solution)/shard_map/ppermute | solution.py:358
  40.7 4.5 %collective-permute-start.5 = (f32[2,4,128]{2,1,0:T(4,128)S(1)}, f32[2,4,128]{2,1,0:T(4,128)S(1)}, u32[]{:S(2)}, u32[]{:S(2)}) collective-permute-start(f32[2,4,128]{2,1,0:T(4,128)S(1)} %get-tuple-element.11), channel_id=1, source_target_pairs={{0,2},{1,3},{2,0},{3,1},{4,6},{5,7},{6,4},{7,5},{8,10},{9,11},{10,... | collective-permute-start | bytes 12296 | tf_op jit(solution)/shard_map/ppermute | solution.py:358
  43.3 3.6 %collective-permute-start.6 = (f32[2,4,128]{2,1,0:T(4,128)S(1)}, f32[2,4,128]{2,1,0:T(4,128)S(1)}, u32[]{:S(2)}, u32[]{:S(2)}) collective-permute-start(f32[2,4,128]{2,1,0:T(4,128)S(1)} %get-tuple-element.12), channel_id=1, source_target_pairs={{0,3},{1,0},{2,1},{3,2},{4,7},{5,4},{6,5},{7,6},{8,11},{9,8},{10,9... | collective-permute-start | bytes 12296 | tf_op jit(solution)/shard_map/ppermute | solution.py:358

commit v3 on v2

--- a/solution.py
+++ b/solution.py
@@ -13,6 +13,7 @@
 TILE = 256
 LANES = 128
 AHEAD = 2
+READY = 2
 
 
 def feature_kernel(
@@ -35,7 +36,8 @@
     act_blocks,
     feat_buf,
     small_sems,
-    sems,
+    grad_sems,
+    var_sems,
     *,
     ckpts,
     examples,
@@ -47,7 +49,6 @@
     chunk = tiles * TILE
     chunks = width // chunk
     total = ckpts * chunks
-    rows = examples * slots
     pairs = examples // 2
     per_unit = pairs // 2
     sign_rows = sign_ring.shape[0]
@@ -57,9 +58,10 @@
         c, q = it // chunks, it % chunks
         at = pl.ds(pl.multiple_of(q * chunk, chunk), chunk)
         return (
-            pltpu.make_async_copy(grad_hbm.at[c, :, at], grad_raw.at[c, :, at], sems.at[0, it]),
-            pltpu.make_async_copy(var_hbm.at[c, at, :], var_raw.at[c, at, :], sems.at[1, it]),
+            pltpu.make_async_copy(grad_hbm.at[c, :, at], grad_raw.at[c, :, at], grad_sems.at[it]),
+            pltpu.make_async_copy(var_hbm.at[c, at, :], var_raw.at[c, at, :], var_sems.at[it]),
         )
+
 
     small = [
         pltpu.make_async_copy(src, dst, small_sems.at[i])
@@ -72,21 +74,16 @@
             )
         )
     ]
-    for copy in small:
+    for copy in (*copies(0), *small, *copies(1)):
         copy.start()
-    for it in range(total):
-        for copy in copies(it):
-            copy.start()
     act_blocks[...] = jnp.zeros_like(act_blocks)
-    lhs_ring[:, LANES:] = jnp.zeros((chunk, TILE - LANES), BF16)
     for copy in small:
         copy.wait()
-
     hash_base = (
         lax.axis_index("layer") * jnp.int32(668265263) + seed_ref[0] * jnp.int32(374761393)
     )
-
     slot_ids = lax.broadcasted_iota(jnp.int32, (slots, 1), 0)
+
     for pair in range(pairs):
         marks = [
             (mask_ref[:, e : e + 1] == 1) & (slot_ids < len_ref[e])
@@ -108,7 +105,7 @@
         if part < 2:
             half = part * LANES
             src = grad_raw[c, :, pl.ds(pl.multiple_of(base + half, LANES), LANES)]
-            lhs_ring[here + half : here + half + LANES, :LANES] = jnp.transpose(src)
+            lhs_ring[here + half : here + half + LANES, :] = jnp.transpose(src)
         elif part == 2:
             moment = var_raw[c, pl.ds(pl.multiple_of(base, TILE), TILE), :].astype(F32)
             scale_ring[here : here + TILE, :] = 1.0 / (jnp.sqrt(moment) + 1e-08)
@@ -124,7 +121,10 @@
 
     for copy in copies(0):
         copy.wait()
-    for t in range(tiles - 1):
+    for it in range(2, total):
+        for copy in copies(it):
+            copy.start()
+    for t in range(READY):
         for part in range(4):
             prepare(0, t, part)
 
@@ -136,9 +136,10 @@
 
         def outer(c, m, n):
             t, j = steps[n]
+            tokens = lhs_ring[t * TILE : (t + 1) * TILE, :]
             pltpu.matmul_push_rhs(act_blocks[c * pairs + m * per_unit + j], 0, m)
             pltpu.matmul_acc_lhs(
-                outer_acc[m][n % depth], lhs_ring[t * TILE : (t + 1) * TILE, :], load_staged_rhs=0
+                outer_acc[m][n % depth], jnp.concatenate([tokens, tokens], 1), load_staged_rhs=0
             )
 
         def project(m, n):
@@ -159,7 +160,7 @@
                 for copy in copies(it + 1):
                     copy.wait()
 
-            for n in range(AHEAD):
+            for n in range(1, AHEAD):
                 for m in (0, 1):
                     outer(c, m, n)
             for n in range(len(steps)):
@@ -167,12 +168,14 @@
                     if n + AHEAD < len(steps):
                         outer(c, m, n + AHEAD)
                     project(m, n)
+                    if n == len(steps) - 2:
+                        outer(following // chunks, m, 0)
                 t, j = steps[n]
                 for part in range(j * 4 // per_unit, (j + 1) * 4 // per_unit):
-                    if t == 0:
-                        prepare(it, tiles - 1, part)
+                    if t + READY < tiles:
+                        prepare(it, t + READY, part)
                     else:
-                        prepare(following, t - 1, part)
+                        prepare(following, t + READY - tiles, part)
 
         def one_ckpt(c, carry):
             def body(q, inner):
@@ -190,7 +193,11 @@
                 out_ref[c, :, k * LANES : (k + 1) * LANES] = feat_buf[:, k, :].astype(BF16)
             return carry
 
+        for m in (0, 1):
+            outer(0, m, 0)
         lax.fori_loop(0, ckpts, one_ckpt, 0)
+        for m in (0, 1):
+            pltpu.matmul_pop(outer_acc[m][0])
 
     pl.run_scoped(
         scoped,
@@ -229,13 +236,14 @@
             pltpu.VMEM(act.shape, BF16),
             pltpu.VMEM((ckpts, rows, width), BF16),
             pltpu.VMEM((ckpts, width, LANES), BF16),
-            pltpu.VMEM((chunk, TILE), BF16),
+            pltpu.VMEM((chunk, LANES), BF16),
             pltpu.VMEM((chunk, LANES), F32),
             pltpu.VMEM((sign_rows, chunk), BF16),
             pltpu.VMEM((ckpts * pairs, TILE, TILE), BF16),
             pltpu.VMEM((examples, cols, LANES), F32),
             pltpu.SemaphoreType.DMA((4,)),
-            pltpu.SemaphoreType.DMA((2, ckpts * width // chunk)),
+            pltpu.SemaphoreType.DMA((ckpts * width // chunk,)),
+            pltpu.SemaphoreType.DMA((ckpts * width // chunk,)),
         ],
         compiler_params=pltpu.CompilerParams(vmem_limit_bytes=57 << 20),
         cost_estimate=pl.CostEstimate(
@@ -246,8 +254,10 @@
 
 
 def score_kernel(*refs, groups, parts):
-    feat_ref, holds, outs = refs[0], refs[1 : 1 + groups], refs[1 + groups : 1 + groups + parts]
-    hold_ref, sums, sems = refs[1 + groups + parts :]
+    feat_hbm, holds, outs = refs[0], refs[1 : 1 + groups], refs[1 + groups : 1 + groups + parts]
+    feat_ref, hold_ref, sums, sems, feat_sem = refs[1 + groups + parts :]
+    feat_copy = pltpu.make_async_copy(feat_hbm, feat_ref, feat_sem)
+    feat_copy.start()
     ckpts, examples, width = feat_ref.shape
     peers, block = hold_ref.shape[1:3]
     members = peers // groups
@@ -268,6 +278,7 @@
             )
     for copy in copies:
         copy.start()
+    feat_copy.wait()
     for c in range(ckpts):
         wide = feat_ref[c].astype(F32)
         norm = jnp.sum(wide * wide, axis=1, keepdims=True)
@@ -297,12 +308,14 @@
     return pl.pallas_call(
         functools.partial(score_kernel, groups=groups, parts=parts),
         out_shape=[jax.ShapeDtypeStruct((ckpts, examples // parts, lanes), F32)] * parts,
-        in_specs=[vmem] + [anywhere] * groups,
+        in_specs=[anywhere] * (1 + groups),
         out_specs=[vmem] * parts,
         scratch_shapes=[
+            pltpu.VMEM(feat.shape, BF16),
             pltpu.VMEM((ckpts, peers, block, width), BF16),
             pltpu.VMEM((ckpts, examples, lanes), F32),
             pltpu.SemaphoreType.DMA((groups, members)),
+            pltpu.SemaphoreType.DMA,
         ],
         compiler_params=pltpu.CompilerParams(vmem_limit_bytes=12 << 20),
         name="scores",

time: 48.3 us -> 45.6 us (0.944)
  Pallas kernels: 31.6 us -> 29 us
    pallas_call x1, Pallas kernels: 28.9 us -> 26.1 us  [features_of(): pl.pallas_call(kernel, out_shape=jax.ShapeDtypeStruct((ckpts, examples, c...]
  transfers between devices with their start and end apart: 7 -> 7, of which waited for: 3 -> 3; matrix products, arithmetic and copies ran while one was open for 0% -> 0% of each run, Pallas kernels for 60% -> 57%
where the time goes in v3:
time: 45.6 us; the launch traced here: 45.4 us
  Pallas kernels  29 us (64%)
  starting transfers between devices  11 us (24%)
  waiting for transfers between devices  2.85 us (6%)
  local copies, waits for them, and re-layouts  0.97 us (2%)
  other arithmetic  0.95 us (2%)
  between operations  0.71 us (2%)
    pallas_call x1, Pallas kernels, features_of(): pl.pallas_call(kernel, out_shape=jax.ShapeDtypeStruct((ckpts, examples, c...  26.1 us
    ppermute x3, starting transfers between devices, local(): pieces[step] = lax.ppermute(pieces[step], 'layer', ring)  5.56 us
    ppermute x3, starting transfers between devices, local(): holds.append(lax.ppermute(own, 'dp', ring))  4.96 us
    ppermute x3, waiting for transfers between devices, local(): pieces[step] = lax.ppermute(pieces[step], 'layer', ring)  2.26 us
    pallas_call x1, Pallas kernels, scores_of(): pl.pallas_call(functools.partial(score_kernel, groups=groups, parts=parts...  1.69 us
    pallas_call x1, Pallas kernels, local(): pl.pallas_call(finish_kernel, out_shape=jax.ShapeDtypeStruct((examples //...  1.2 us
    unnamed x4, local copies, waits for them, and re-layouts  0.97 us
    another operation x1, other arithmetic, local(): own = jnp.stack(gathered, axis=1)  0.95 us
  transfers between devices with their start and end apart: 7, of which 3 were waited for; matrix products, arithmetic and copies ran while one was open for 0% of the time, Pallas kernels for 57%

profile of v3, /device:TPU:0, one launch (start us, length us, event | category | flops | bytes accessed | tf_op | source)
XLA Modules:
  0.0 45.4 jit_solution(5035523563016565783)
XLA Ops:
  0.0 0.5 collective-permute-start
  1.1 0.6 %collective-permute-done = bf16[2,8,5120]{2,1,0:T(8,128)(2,1)S(1)} collective-permute-done((bf16[2,8,5120]{2,1,0:T(8,128)(2,1)}, bf16[2,8,5120]{2,1,0:T(8,128)(2,1)S(1)}, u32[]{:S(2)}, u32[]{:S(2)}) %collective-permute-start) | collective-permute-done | bytes 163872 | tf_op jit(solution)/shard_map/ppermute | solution.py:353
  1.7 0.9 %pad_maximum_fusion.refs_1_ = bf16[2,2,8,5120]{3,2,1,0:T(8,128)(2,1)S(1)} fusion(bf16[2,1,8,5120]{3,2,1,0:T(8,128)(2,1)S(1)} %bitcast.7, bf16[2,1,8,5120]{3,2,1,0:T(8,128)(2,1)} %param.11), kind=kLoop, calls=%fused_computation | loop fusion | flops 163840 | bytes 655360 | tf_op jit(solution)/shard_map/stack | solution.py:354
  2.6 3.9 %collective-permute-start.3 = (bf16[2,2,8,5120]{3,2,1,0:T(8,128)(2,1)S(1)}, bf16[2,2,8,5120]{3,2,1,0:T(8,128)(2,1)S(1)}, u32[]{:S(2)}, u32[]{:S(2)}) collective-permute-start(bf16[2,2,8,5120]{3,2,1,0:T(8,128)(2,1)S(1)} %pad_maximum_fusion.refs_1_), channel_id=1, source_target_pairs={{0,24},{4,28},{8,0},{12,4},{16,8},{20,12},{24,16},{28,20},{1,25},{... | collective-permute-start | bytes 983048 | tf_op jit(solution)/shard_map/ppermute | solution.py:358
  6.5 0.5 %collective-permute-start.2 = (bf16[2,2,8,5120]{3,2,1,0:T(8,128)(2,1)S(1)}, bf16[2,2,8,5120]{3,2,1,0:T(8,128)(2,1)S(1)}, u32[]{:S(2)}, u32[]{:S(2)}) collective-permute-start(bf16[2,2,8,5120]{3,2,1,0:T(8,128)(2,1)S(1)} %pad_maximum_fusion.refs_1_), channel_id=1, source_target_pairs={{0,16},{4,20},{8,24},{12,28},{16,0},{20,4},{24,8},{28,12},{1,17},{... | collective-permute-start | bytes 983048 | tf_op jit(solution)/shard_map/ppermute | solution.py:358
  7.0 0.6 %collective-permute-start.1 = (bf16[2,2,8,5120]{3,2,1,0:T(8,128)(2,1)S(1)}, bf16[2,2,8,5120]{3,2,1,0:T(8,128)(2,1)S(1)}, u32[]{:S(2)}, u32[]{:S(2)}) collective-permute-start(bf16[2,2,8,5120]{3,2,1,0:T(8,128)(2,1)S(1)} %pad_maximum_fusion.refs_1_), channel_id=1, source_target_pairs={{0,8},{4,12},{8,16},{12,20},{16,24},{20,28},{24,0},{28,4},{1,9},{5... | collective-permute-start | bytes 983048 | tf_op jit(solution)/shard_map/ppermute | solution.py:358
  7.6 0.0 copy-start.1
  7.6 26.1 %features.1.refs_0_ = bf16[2,16,5120]{2,1,0:T(8,128)(2,1)} custom-call(s32[1]{0:T(128)S(6)} %copy.9.seed_hbm, s32[16]{0:T(128)} %len_hbm.1, s32[8,16]{1,0:T(8,128)} %bitcast.11, bf16[2,128,128]{2,1,0:T(8,128)(2,1)} %bitcast.10, bf16[2,128,8192]{2,1,0:T(8,128)(2,1)} %bitcast.8, bf16[2,8192,128]{2,1,0:T(8,128)(2,1)} %bitcast.9), custom_call_target="tpu_custom_call" | custom-call | flops 40000000000 | bytes 9000000 | tf_op jit(solution)/shard_map/features/pallas_call | solution.py:227
  33.7 0.0 collective-permute-done.3.refs_4_
  33.7 0.0 collective-permute-done.2.refs_3_
  33.7 0.0 collective-permute-done.1.refs_2_
  33.7 0.0 copy-start
  33.8 1.0 %copy-done = bf16[2,16,5120]{2,1,0:T(8,128)(2,1)S(1)} copy-done((bf16[2,16,5120]{2,1,0:T(8,128)(2,1)S(1)}, bf16[2,16,5120]{2,1,0:T(8,128)(2,1)}, u32[]{:S(2)}) %copy-start) | copy-done | bytes 327704
  34.7 1.7 %scores.1 = (f32[2,4,128]{2,1,0:T(4,128)S(1)}, f32[2,4,128]{2,1,0:T(4,128)S(1)}, f32[2,4,128]{2,1,0:T(4,128)S(1)}, f32[2,4,128]{2,1,0:T(4,128)S(1)}) custom-call(bf16[2,16,5120]{2,1,0:T(8,128)(2,1)S(1)} %copy-done, bf16[2,2,8,5120]{3,2,1,0:T(8,128)(2,1)S(1)} %pad_maximum_fusion.refs_1_, bf16[2,2,8,5120]{3,2,1,0:T(8,128)(2,1)S(1)} %collective-permute-done.1.refs_2_, ...), custom_call_target="tpu_custom_call" | custom-call | tf_op jit(solution)/shard_map/scores/pallas_call | solution.py:308
  36.4 1.6 %collective-permute-start.4 = (f32[2,4,128]{2,1,0:T(4,128)S(1)}, f32[2,4,128]{2,1,0:T(4,128)S(1)}, u32[]{:S(2)}, u32[]{:S(2)}) collective-permute-start(f32[2,4,128]{2,1,0:T(4,128)S(1)} %get-tuple-element.10), channel_id=1, source_target_pairs={{0,1},{1,2},{2,3},{3,0},{4,5},{5,6},{6,7},{7,4},{8,9},{9,10},{10,1... | collective-permute-start | bytes 12296 | tf_op jit(solution)/shard_map/ppermute | solution.py:371
  38.0 2.6 %collective-permute-start.5 = (f32[2,4,128]{2,1,0:T(4,128)S(1)}, f32[2,4,128]{2,1,0:T(4,128)S(1)}, u32[]{:S(2)}, u32[]{:S(2)}) collective-permute-start(f32[2,4,128]{2,1,0:T(4,128)S(1)} %get-tuple-element.11), channel_id=1, source_target_pairs={{0,2},{1,3},{2,0},{3,1},{4,6},{5,7},{6,4},{7,5},{8,10},{9,11},{10,... | collective-permute-start | bytes 12296 | tf_op jit(solution)/shard_map/ppermute | solution.py:371
  40.6 1.3 %collective-permute-start.6 = (f32[2,4,128]{2,1,0:T(4,128)S(1)}, f32[2,4,128]{2,1,0:T(4,128)S(1)}, u32[]{:S(2)}, u32[]{:S(2)}) collective-permute-start(f32[2,4,128]{2,1,0:T(4,128)S(1)} %get-tuple-element.12), channel_id=1, source_target_pairs={{0,3},{1,0},{2,1},{3,2},{4,7},{5,4},{6,5},{7,6},{8,11},{9,8},{10,9... | collective-permute-start | bytes 12296 | tf_op jit(solution)/shard_map/ppermute | solution.py:371
  42.0 0.0 collective-permute-done.4.refs_2_
  42.0 0.6 %collective-permute-done.5.refs_3_ = f32[2,4,128]{2,1,0:T(4,128)S(1)} collective-permute-done((f32[2,4,128]{2,1,0:T(4,128)S(1)}, f32[2,4,128]{2,1,0:T(4,128)S(1)}, u32[]{:S(2)}, u32[]{:S(2)}) %collective-permute-start.5) | collective-permute-done | bytes 4128 | tf_op jit(solution)/shard_map/ppermute | solution.py:371
  42.6 1.7 %collective-permute-done.6.refs_4_ = f32[2,4,128]{2,1,0:T(4,128)S(1)} collective-permute-done((f32[2,4,128]{2,1,0:T(4,128)S(1)}, f32[2,4,128]{2,1,0:T(4,128)S(1)}, u32[]{:S(2)}, u32[]{:S(2)}) %collective-permute-start.6) | collective-permute-done | bytes 4128 | tf_op jit(solution)/shard_map/ppermute | solution.py:371
  44.2 0.0 copy-done.1
  44.2 1.2 %finish.1 = f32[4,64]{1,0:T(4,128)} custom-call(f32[2]{0:T(128)S(1)} %copy-done.1, f32[2,4,128]{2,1,0:T(4,128)S(1)} %get-tuple-element.9.refs_1_, f32[2,4,128]{2,1,0:T(4,128)S(1)} %collective-permute-done.4.refs_2_, f32[2,4,128]{2,1,0:T(4,128)S(1)} %collective-permute-done.5.refs_3_, f32[2,4,128]{2,1,0:T(4,128)S(1)} %collective-permute-done.6.refs_4_), custom_call_target="tpu_custom_call" | custom-call | tf_op jit(solution)/shard_map/finish/pallas_call | solution.py:373
Async XLA Ops:
  0.0 1.7 %collective-permute-start = (bf16[2,8,5120]{2,1,0:T(8,128)(2,1)}, bf16[2,8,5120]{2,1,0:T(8,128)(2,1)S(1)}, u32[]{:S(2)}, u32[]{:S(2)}) collective-permute-start(bf16[2,8,5120]{2,1,0:T(8,128)(2,1)} %bitcast.6), channel_id=1, source_target_pairs={{0,4},{4,0},{8,12},{12,8},{16,20},{20,16},{24,28},{28,24},{1,5},{5... | collective-permute-start | bytes 491528 | tf_op jit(solution)/shard_map/ppermute | solution.py:353
  2.6 31.1 %collective-permute-start.3 = (bf16[2,2,8,5120]{3,2,1,0:T(8,128)(2,1)S(1)}, bf16[2,2,8,5120]{3,2,1,0:T(8,128)(2,1)S(1)}, u32[]{:S(2)}, u32[]{:S(2)}) collective-permute-start(bf16[2,2,8,5120]{3,2,1,0:T(8,128)(2,1)S(1)} %pad_maximum_fusion.refs_1_), channel_id=1, source_target_pairs={{0,24},{4,28},{8,0},{12,4},{16,8},{20,12},{24,16},{28,20},{1,25},{... | collective-permute-start | bytes 983048 | tf_op jit(solution)/shard_map/ppermute | solution.py:358
  6.5 27.2 %collective-permute-start.2 = (bf16[2,2,8,5120]{3,2,1,0:T(8,128)(2,1)S(1)}, bf16[2,2,8,5120]{3,2,1,0:T(8,128)(2,1)S(1)}, u32[]{:S(2)}, u32[]{:S(2)}) collective-permute-start(bf16[2,2,8,5120]{3,2,1,0:T(8,128)(2,1)S(1)} %pad_maximum_fusion.refs_1_), channel_id=1, source_target_pairs={{0,16},{4,20},{8,24},{12,28},{16,0},{20,4},{24,8},{28,12},{1,17},{... | collective-permute-start | bytes 983048 | tf_op jit(solution)/shard_map/ppermute | solution.py:358
  7.0 26.7 %collective-permute-start.1 = (bf16[2,2,8,5120]{3,2,1,0:T(8,128)(2,1)S(1)}, bf16[2,2,8,5120]{3,2,1,0:T(8,128)(2,1)S(1)}, u32[]{:S(2)}, u32[]{:S(2)}) collective-permute-start(bf16[2,2,8,5120]{3,2,1,0:T(8,128)(2,1)S(1)} %pad_maximum_fusion.refs_1_), channel_id=1, source_target_pairs={{0,8},{4,12},{8,16},{12,20},{16,24},{20,28},{24,0},{28,4},{1,9},{5... | collective-permute-start | bytes 983048 | tf_op jit(solution)/shard_map/ppermute | solution.py:358
  7.6 36.6 %copy-start.1 = (f32[2]{0:T(128)S(1)}, f32[2]{0:T(128)}, u32[]{:S(2)}) copy-start(f32[2]{0:T(128)} %refs_0_.1) | copy-start | bytes 28
  33.7 1.0 %copy-start = (bf16[2,16,5120]{2,1,0:T(8,128)(2,1)S(1)}, bf16[2,16,5120]{2,1,0:T(8,128)(2,1)}, u32[]{:S(2)}) copy-start(bf16[2,16,5120]{2,1,0:T(8,128)(2,1)} %features.1.refs_0_) | copy-start | bytes 983044
  36.4 5.6 %collective-permute-start.4 = (f32[2,4,128]{2,1,0:T(4,128)S(1)}, f32[2,4,128]{2,1,0:T(4,128)S(1)}, u32[]{:S(2)}, u32[]{:S(2)}) collective-permute-start(f32[2,4,128]{2,1,0:T(4,128)S(1)} %get-tuple-element.10), channel_id=1, source_target_pairs={{0,1},{1,2},{2,3},{3,0},{4,5},{5,6},{6,7},{7,4},{8,9},{9,10},{10,1... | collective-permute-start | bytes 12296 | tf_op jit(solution)/shard_map/ppermute | solution.py:371
  38.0 4.5 %collective-permute-start.5 = (f32[2,4,128]{2,1,0:T(4,128)S(1)}, f32[2,4,128]{2,1,0:T(4,128)S(1)}, u32[]{:S(2)}, u32[]{:S(2)}) collective-permute-start(f32[2,4,128]{2,1,0:T(4,128)S(1)} %get-tuple-element.11), channel_id=1, source_target_pairs={{0,2},{1,3},{2,0},{3,1},{4,6},{5,7},{6,4},{7,5},{8,10},{9,11},{10,... | collective-permute-start | bytes 12296 | tf_op jit(solution)/shard_map/ppermute | solution.py:371
  40.6 3.6 %collective-permute-start.6 = (f32[2,4,128]{2,1,0:T(4,128)S(1)}, f32[2,4,128]{2,1,0:T(4,128)S(1)}, u32[]{:S(2)}, u32[]{:S(2)}) collective-permute-start(f32[2,4,128]{2,1,0:T(4,128)S(1)} %get-tuple-element.12), channel_id=1, source_target_pairs={{0,3},{1,0},{2,1},{3,2},{4,7},{5,4},{6,5},{7,6},{8,11},{9,8},{10,9... | collective-permute-start | bytes 12296 | tf_op jit(solution)/shard_map/ppermute | solution.py:371

commit v4 on v3

--- a/solution.py
+++ b/solution.py
@@ -16,18 +16,20 @@
 READY = 2
 
 
+def target(index, step, size):
+    return index ^ step if size & (size - 1) == 0 else (index + step) % size
+
+
+def source(index, step, size):
+    return index ^ step if size & (size - 1) == 0 else (index + size - step) % size
+
+
 def feature_kernel(
-    seed_hbm,
-    len_hbm,
-    mask_hbm,
-    act_hbm,
+    seed_ref,
+    act_ref,
     grad_hbm,
     var_hbm,
     out_ref,
-    seed_ref,
-    len_ref,
-    mask_ref,
-    act_ref,
     grad_raw,
     var_raw,
     lhs_ring,
@@ -35,7 +37,6 @@
     sign_ring,
     act_blocks,
     feat_buf,
-    small_sems,
     grad_sems,
     var_sems,
     *,
@@ -63,36 +64,17 @@
         )
 
 
-    small = [
-        pltpu.make_async_copy(src, dst, small_sems.at[i])
-        for i, (src, dst) in enumerate(
-            (
-                (seed_hbm, seed_ref),
-                (len_hbm, len_ref),
-                (mask_hbm, mask_ref),
-                (act_hbm, act_ref),
-            )
-        )
-    ]
-    for copy in (*copies(0), *small, *copies(1)):
+    for copy in (*copies(0), *copies(1)):
         copy.start()
     act_blocks[...] = jnp.zeros_like(act_blocks)
-    for copy in small:
-        copy.wait()
     hash_base = (
         lax.axis_index("layer") * jnp.int32(668265263) + seed_ref[0] * jnp.int32(374761393)
     )
-    slot_ids = lax.broadcasted_iota(jnp.int32, (slots, 1), 0)
-
     for pair in range(pairs):
-        marks = [
-            (mask_ref[:, e : e + 1] == 1) & (slot_ids < len_ref[e])
-            for e in (2 * pair, 2 * pair + 1)
-        ]
         for c in range(ckpts):
             at = 2 * pair * slots
-            first = jnp.where(marks[0], act_ref[c, at : at + slots, :].astype(F32), 0.0)
-            second = jnp.where(marks[1], act_ref[c, at + slots : at + 2 * slots, :].astype(F32), 0.0)
+            first = act_ref[c, at : at + slots, :].astype(F32)
+            second = act_ref[c, at + slots : at + 2 * slots, :].astype(F32)
             blank = jnp.zeros_like(first)
             act_blocks[c * pairs + pair, at : at + 2 * slots, :] = jnp.concatenate(
                 [jnp.concatenate([first, blank], 1), jnp.concatenate([blank, second], 1)], 0
@@ -206,9 +188,9 @@
     )
 
 
-def features_of(seed, lengths, mask, act, grad, var, cols):
+def features_of(seed, act, grad, var, slots, cols):
     ckpts, rows, width = grad.shape
-    slots, examples = mask.shape
+    examples = rows // slots
     tiles = 8
     chunk = tiles * TILE
     pairs = examples // 2
@@ -227,13 +209,9 @@
     return pl.pallas_call(
         kernel,
         out_shape=jax.ShapeDtypeStruct((ckpts, examples, cols * LANES), BF16),
-        in_specs=[hbm] * 6,
+        in_specs=[pl.BlockSpec(memory_space=pltpu.SMEM), vmem, hbm, hbm],
         out_specs=vmem,
         scratch_shapes=[
-            pltpu.SMEM(seed.shape, jnp.int32),
-            pltpu.SMEM(lengths.shape, jnp.int32),
-            pltpu.VMEM(mask.shape, jnp.int32),
-            pltpu.VMEM(act.shape, BF16),
             pltpu.VMEM((ckpts, rows, width), BF16),
             pltpu.VMEM((ckpts, width, LANES), BF16),
             pltpu.VMEM((chunk, LANES), BF16),
@@ -241,97 +219,80 @@
             pltpu.VMEM((sign_rows, chunk), BF16),
             pltpu.VMEM((ckpts * pairs, TILE, TILE), BF16),
             pltpu.VMEM((examples, cols, LANES), F32),
-            pltpu.SemaphoreType.DMA((4,)),
             pltpu.SemaphoreType.DMA((ckpts * width // chunk,)),
             pltpu.SemaphoreType.DMA((ckpts * width // chunk,)),
         ],
-        compiler_params=pltpu.CompilerParams(vmem_limit_bytes=57 << 20),
+        compiler_params=pltpu.CompilerParams(vmem_limit_bytes=53 << 20),
         cost_estimate=pl.CostEstimate(
             flops=40_000_000_000, bytes_accessed=9_000_000, transcendentals=0
         ),
         name="features",
-    )(seed, lengths, mask, act, grad, var)
+    )(seed, act, grad, var)
 
 
 def score_kernel(*refs, groups, parts):
-    feat_hbm, holds, outs = refs[0], refs[1 : 1 + groups], refs[1 + groups : 1 + groups + parts]
-    feat_ref, hold_ref, sums, sems, feat_sem = refs[1 + groups + parts :]
-    feat_copy = pltpu.make_async_copy(feat_hbm, feat_ref, feat_sem)
-    feat_copy.start()
+    weight_ref, feat_ref, holds = refs[0], refs[1], refs[2 : 2 + groups]
+    outs, (turned, sums) = refs[2 + groups : 2 + groups + parts], refs[2 + groups + parts :]
     ckpts, examples, width = feat_ref.shape
-    peers, block = hold_ref.shape[1:3]
-    members = peers // groups
-    held = peers * block
+    members, block = holds[0].shape[1:3]
+    held = groups * members * block
     share = examples // parts
     mine = lax.axis_index("dp")
     me = lax.axis_index("layer")
     group, member = mine // members, lax.rem(mine, members)
-    copies = []
-    for step in range(groups):
-        source = lax.rem(group + groups - step, groups) * members
-        for turn in range(members):
-            index = source + lax.rem(member + turn, members)
-            copies.append(
-                pltpu.make_async_copy(
-                    holds[step].at[:, turn], hold_ref.at[:, index], sems.at[step, turn]
-                )
-            )
-    for copy in copies:
-        copy.start()
-    feat_copy.wait()
     for c in range(ckpts):
-        wide = feat_ref[c].astype(F32)
+        feat = feat_ref[c]
+        stack = jnp.concatenate([hold[c].reshape(members * block, width) for hold in holds], 0)
+        found = lax.dot_general(
+            stack, feat, (((1,), (1,)), ((), ())), preferred_element_type=F32
+        )
+        for step in range(groups):
+            first = source(group, step, groups) * members
+            for turn in range(members):
+                index = first + lax.rem(member + turn, members)
+                at = (step * members + turn) * block
+                turned[c, pl.ds(pl.multiple_of(index * block, block), block), :] = found[
+                    at : at + block
+                ]
+        wide = feat.astype(F32)
         norm = jnp.sum(wide * wide, axis=1, keepdims=True)
+        sums[c, :, :held] = jnp.transpose(turned[c]) * weight_ref[c]
         sums[c, :, held:] = jnp.broadcast_to(norm, (examples, sums.shape[2] - held))
-    for copy in copies:
-        copy.wait()
-    for c in range(ckpts):
-        sums[c, :, :held] = lax.dot_general(
-            feat_ref[c],
-            hold_ref[c].reshape(held, width),
-            (((1,), (1,)), ((), ())),
-            preferred_element_type=F32,
-        )
         for step in range(parts):
             owner = lax.rem(me + step, parts)
             outs[step][c] = sums[c, pl.ds(owner * share, share), :]
 
 
-def scores_of(feat, holds, parts):
+def scores_of(weight, feat, holds, parts):
     ckpts, examples, width = feat.shape
     groups = len(holds)
     members, block = holds[0].shape[1:3]
-    peers = groups * members
-    lanes = (peers * block // LANES + 1) * LANES
+    held = groups * members * block
+    lanes = (held // LANES + 1) * LANES
     vmem = pl.BlockSpec(memory_space=pltpu.VMEM)
-    anywhere = pl.BlockSpec(memory_space=pl.ANY)
     return pl.pallas_call(
         functools.partial(score_kernel, groups=groups, parts=parts),
         out_shape=[jax.ShapeDtypeStruct((ckpts, examples // parts, lanes), F32)] * parts,
-        in_specs=[anywhere] * (1 + groups),
+        in_specs=[pl.BlockSpec(memory_space=pltpu.SMEM)] + [vmem] * (1 + groups),
         out_specs=[vmem] * parts,
         scratch_shapes=[
-            pltpu.VMEM(feat.shape, BF16),
-            pltpu.VMEM((ckpts, peers, block, width), BF16),
+            pltpu.VMEM((ckpts, held, examples), F32),
             pltpu.VMEM((ckpts, examples, lanes), F32),
-            pltpu.SemaphoreType.DMA((groups, members)),
-            pltpu.SemaphoreType.DMA,
         ],
         compiler_params=pltpu.CompilerParams(vmem_limit_bytes=12 << 20),
         name="scores",
-    )(feat, *holds)
+    )(weight, feat, *holds)
 
 
 def finish_kernel(*refs):
-    weight_ref, pieces, out_ref = refs[0], refs[1:-1], refs[-1]
+    pieces, out_ref = refs[:-1], refs[-1]
     held = out_ref.shape[1]
     result = jnp.zeros(out_ref.shape, F32)
     for c in range(pieces[0].shape[0]):
         total = pieces[0][c]
         for piece in pieces[1:]:
             total = total + piece[c]
-        scale = weight_ref[c] * lax.rsqrt(total[:, held : held + 1] + 1e-06)
-        result = result + total[:, :held] * scale
+        result = result + total[:, :held] * lax.rsqrt(total[:, held : held + 1] + 1e-06)
     out_ref[...] = result
 
 
@@ -354,18 +315,21 @@
         own = jnp.stack(gathered, axis=1)
         holds = [own]
         for step in range(1, groups):
-            ring = [(i, (i + step * members) % peers) for i in range(peers)]
+            ring = [
+                (i, target(i // members, step, groups) * members + i % members) for i in range(peers)
+            ]
             holds.append(lax.ppermute(own, "dp", ring))
+        valid = (mask == 1) & (jnp.arange(slots, dtype=jnp.int32) < lengths[:, None])
+        valid = valid[None, :, :, None]
         feat = features_of(
             seed,
-            lengths,
-            mask.T,
-            act.reshape(ckpts, examples * slots, rank),
+            jnp.where(valid, act[:, 0], 0).reshape(ckpts, examples * slots, rank),
             grad.reshape(ckpts, examples * slots, width),
             var[:, 0],
+            slots,
             cols,
         )
-        pieces = list(scores_of(feat, holds, parts))
+        pieces = list(scores_of(weight, feat, holds, parts))
         for step in range(1, parts):
             ring = [(i, (i + step) % parts) for i in range(parts)]
             pieces[step] = lax.ppermute(pieces[step], "layer", ring)
@@ -373,11 +337,11 @@
         return pl.pallas_call(
             finish_kernel,
             out_shape=jax.ShapeDtypeStruct((examples // parts, peers * hold.shape[2]), F32),
-            in_specs=[pl.BlockSpec(memory_space=pltpu.SMEM)] + [vmem] * parts,
+            in_specs=[vmem] * parts,
             out_specs=vmem,
             compiler_params=pltpu.CompilerParams(vmem_limit_bytes=12 << 20),
             name="finish",
-        )(weight, *pieces)
+        )(*pieces)
 
     placed = (
         P(None, "layer", "dp", None, None),

time: 45.6 us -> 43.1 us (0.945)
  Pallas kernels: 29 us -> 26.5 us
  other arithmetic: 0.95 us -> 2.57 us
  local copies, waits for them, and re-layouts: 0.97 us -> 0.19 us
  waiting for transfers between devices: 2.85 us -> 2.27 us
    pallas_call x1, Pallas kernels: 26.1 us -> 24.7 us  [features_of(): pl.pallas_call(kernel, out_shape=jax.ShapeDtypeStruct((ckpts, examples, c...]
    unnamed x4 -> x2, local copies, waits for them, and re-layouts: 0.97 us -> 0.01 us
    select_n x0 -> x1, other arithmetic: none -> 0.93 us  [local(): jnp.where(valid, act[:, 0], 0).reshape(ckpts, examples * slots, rank)]
    ppermute x3, starting transfers between devices: 4.96 us -> 4.15 us  [local(): holds.append(lax.ppermute(own, 'dp', ring))]
    and x0 -> x1, other arithmetic: none -> 0.7 us  [local(): (mask == 1) & (jnp.arange(slots, dtype=jnp.int32) < lengths[:, None])]
    ppermute x1, waiting for transfers between devices: 0.59 us -> 0.01 us  [local(): gathered.append(lax.ppermute(hold[:, 0], 'dp', ring))]
    pallas_call x1, Pallas kernels: 1.69 us -> 1.1 us  [scores_of(): pl.pallas_call(functools.partial(score_kernel, groups=groups, parts=parts...]
    pallas_call x1, Pallas kernels: 1.2 us -> 0.66 us  [local(): pl.pallas_call(finish_kernel, out_shape=jax.ShapeDtypeStruct((examples //...]
  transfers between devices with their start and end apart: 7 -> 7, of which waited for: 3 -> 2; matrix products, arithmetic and copies ran while one was open for 0% -> 4% of each run, Pallas kernels for 57% -> 58%
where the time goes in v4:
time: 43.1 us; the launch traced here: 42.8 us
  Pallas kernels  26.5 us (61%)
  starting transfers between devices  10.6 us (25%)
  other arithmetic  2.57 us (6%)
  waiting for transfers between devices  2.27 us (5%)
  between operations  0.73 us (2%)
    pallas_call x1, Pallas kernels, features_of(): pl.pallas_call(kernel, out_shape=jax.ShapeDtypeStruct((ckpts, examples, c...  24.7 us
    ppermute x3, starting transfers between devices, local(): pieces[step] = lax.ppermute(pieces[step], 'layer', ring)  5.95 us
    ppermute x3, starting transfers between devices, local(): holds.append(lax.ppermute(own, 'dp', ring))  4.15 us
    ppermute x3, waiting for transfers between devices, local(): pieces[step] = lax.ppermute(pieces[step], 'layer', ring)  2.26 us
    pallas_call x1, Pallas kernels, scores_of(): pl.pallas_call(functools.partial(score_kernel, groups=groups, parts=parts...  1.1 us
    another operation x1, other arithmetic, local(): own = jnp.stack(gathered, axis=1)  0.95 us
    select_n x1, other arithmetic, local(): jnp.where(valid, act[:, 0], 0).reshape(ckpts, examples * slots, rank)  0.93 us
  transfers between devices with their start and end apart: 7, of which 2 were waited for; matrix products, arithmetic and copies ran while one was open for 4% of the time, Pallas kernels for 58%

profile of v4, /device:TPU:0, one launch (start us, length us, event | category | flops | bytes accessed | tf_op | source)
XLA Modules:
  0.0 42.8 jit_solution(15110273494703782852)
XLA Ops:
  0.0 0.5 %collective-permute-start = (bf16[2,8,5120]{2,1,0:T(8,128)(2,1)}, bf16[2,8,5120]{2,1,0:T(8,128)(2,1)S(1)}, u32[]{:S(2)}, u32[]{:S(2)}) collective-permute-start(bf16[2,8,5120]{2,1,0:T(8,128)(2,1)} %bitcast.6), channel_id=1, source_target_pairs={{0,4},{4,0},{8,12},{12,8},{16,20},{20,16},{24,28},{28,24},{1,5},{5... | collective-permute-start | bytes 491528 | tf_op jit(solution)/shard_map/ppermute | solution.py:314
  1.1 0.7 %fusion = pred[16,8]{0,1:T(8,128)(4,1)S(1)} fusion(s32[16,8]{0,1:T(8,128)} %param.13, s32[16]{0:T(128)} %param.12), kind=kLoop, calls=%fused_computation.3 | loop fusion | flops 384 | bytes 704 | tf_op jit(solution)/shard_map/and | solution.py:322
  1.8 0.1 copy.10
  1.9 0.1 broadcast_in_dim.17
  2.0 0.9 %bitcast_select_fusion.act_ref = bf16[2,128,128]{2,1,0:T(8,128)(2,1)S(1)} fusion(bf16[2,1,16,8,128]{4,3,2,1,0:T(8,128)(2,1)} %param.9, pred[128]{0:T(512)(128)(4,1)S(1)} %broadcast_in_dim.17), kind=kLoop, calls=%fused_computation.1 | loop fusion | flops 32768 | bytes 131200 | tf_op jit(solution)/shard_map/jit(_where)/select_n | solution.py:326
  2.9 0.0 collective-permute-done
  2.9 1.0 %pad_maximum_fusion.refs_2_ = bf16[2,2,8,5120]{3,2,1,0:T(8,128)(2,1)S(1)} fusion(bf16[2,1,8,5120]{3,2,1,0:T(8,128)(2,1)S(1)} %bitcast.7, bf16[2,1,8,5120]{3,2,1,0:T(8,128)(2,1)} %param.11), kind=kLoop, calls=%fused_computation | loop fusion | flops 163840 | bytes 655360 | tf_op jit(solution)/shard_map/stack | solution.py:315
  3.9 3.5 %collective-permute-start.3 = (bf16[2,2,8,5120]{3,2,1,0:T(8,128)(2,1)S(1)}, bf16[2,2,8,5120]{3,2,1,0:T(8,128)(2,1)S(1)}, u32[]{:S(2)}, u32[]{:S(2)}) collective-permute-start(bf16[2,2,8,5120]{3,2,1,0:T(8,128)(2,1)S(1)} %pad_maximum_fusion.refs_2_), channel_id=1, source_target_pairs={{0,24},{4,28},{8,16},{12,20},{16,8},{20,12},{24,0},{28,4},{1,25},{... | collective-permute-start | bytes 983048 | tf_op jit(solution)/shard_map/ppermute | solution.py:321
  7.4 0.5 %collective-permute-start.2 = (bf16[2,2,8,5120]{3,2,1,0:T(8,128)(2,1)S(1)}, bf16[2,2,8,5120]{3,2,1,0:T(8,128)(2,1)S(1)}, u32[]{:S(2)}, u32[]{:S(2)}) collective-permute-start(bf16[2,2,8,5120]{3,2,1,0:T(8,128)(2,1)S(1)} %pad_maximum_fusion.refs_2_), channel_id=1, source_target_pairs={{0,16},{4,20},{8,24},{12,28},{16,0},{20,4},{24,8},{28,12},{1,17},{... | collective-permute-start | bytes 983048 | tf_op jit(solution)/shard_map/ppermute | solution.py:321
  7.9 0.1 collective-permute-start.1
  8.0 0.0 copy-start
  8.0 24.7 %features.1.refs_1_ = bf16[2,16,5120]{2,1,0:T(8,128)(2,1)S(1)} custom-call(s32[1]{0:T(128)S(6)} %copy.11.seed_ref, bf16[2,128,128]{2,1,0:T(8,128)(2,1)S(1)} %bitcast_select_fusion.act_ref, bf16[2,128,8192]{2,1,0:T(8,128)(2,1)} %bitcast.8, bf16[2,8192,128]{2,1,0:T(8,128)(2,1)} %bitcast.9), custom_call_target="tpu_custom_call" | custom-call | flops 40000000000 | bytes 9000000 | tf_op jit(solution)/shard_map/features/pallas_call | solution.py:209
  32.8 0.0 collective-permute-done.3.refs_5_
  32.8 0.0 collective-permute-done.2.refs_4_
  32.8 0.0 collective-permute-done.1.refs_3_
  32.8 0.0 copy-done
  32.8 1.1 %scores.1 = (f32[2,4,128]{2,1,0:T(4,128)S(1)}, f32[2,4,128]{2,1,0:T(4,128)S(1)}, f32[2,4,128]{2,1,0:T(4,128)S(1)}, f32[2,4,128]{2,1,0:T(4,128)S(1)}) custom-call(f32[2]{0:T(128)S(1)} %copy-done, bf16[2,16,5120]{2,1,0:T(8,128)(2,1)S(1)} %features.1.refs_1_, bf16[2,2,8,5120]{3,2,1,0:T(8,128)(2,1)S(1)} %pad_maximum_fusion.refs_2_, ...), custom_call_target="tpu_custom_call" | custom-call | tf_op jit(solution)/shard_map/scores/pallas_call | solution.py:273
  34.0 2.0 %collective-permute-start.4 = (f32[2,4,128]{2,1,0:T(4,128)S(1)}, f32[2,4,128]{2,1,0:T(4,128)S(1)}, u32[]{:S(2)}, u32[]{:S(2)}) collective-permute-start(f32[2,4,128]{2,1,0:T(4,128)S(1)} %get-tuple-element.10), channel_id=1, source_target_pairs={{0,1},{1,2},{2,3},{3,0},{4,5},{5,6},{6,7},{7,4},{8,9},{9,10},{10,1... | collective-permute-start | bytes 12296 | tf_op jit(solution)/shard_map/ppermute | solution.py:335
  36.0 2.6 %collective-permute-start.5 = (f32[2,4,128]{2,1,0:T(4,128)S(1)}, f32[2,4,128]{2,1,0:T(4,128)S(1)}, u32[]{:S(2)}, u32[]{:S(2)}) collective-permute-start(f32[2,4,128]{2,1,0:T(4,128)S(1)} %get-tuple-element.11), channel_id=1, source_target_pairs={{0,2},{1,3},{2,0},{3,1},{4,6},{5,7},{6,4},{7,5},{8,10},{9,11},{10,... | collective-permute-start | bytes 12296 | tf_op jit(solution)/shard_map/ppermute | solution.py:335
  38.6 1.3 %collective-permute-start.6 = (f32[2,4,128]{2,1,0:T(4,128)S(1)}, f32[2,4,128]{2,1,0:T(4,128)S(1)}, u32[]{:S(2)}, u32[]{:S(2)}) collective-permute-start(f32[2,4,128]{2,1,0:T(4,128)S(1)} %get-tuple-element.12), channel_id=1, source_target_pairs={{0,3},{1,0},{2,1},{3,2},{4,7},{5,4},{6,5},{7,6},{8,11},{9,8},{10,9... | collective-permute-start | bytes 12296 | tf_op jit(solution)/shard_map/ppermute | solution.py:335
  39.9 0.0 collective-permute-done.4.refs_1_
  39.9 0.6 %collective-permute-done.5.refs_2_ = f32[2,4,128]{2,1,0:T(4,128)S(1)} collective-permute-done((f32[2,4,128]{2,1,0:T(4,128)S(1)}, f32[2,4,128]{2,1,0:T(4,128)S(1)}, u32[]{:S(2)}, u32[]{:S(2)}) %collective-permute-start.5) | collective-permute-done | bytes 4128 | tf_op jit(solution)/shard_map/ppermute | solution.py:335
  40.5 1.7 %collective-permute-done.6.refs_3_ = f32[2,4,128]{2,1,0:T(4,128)S(1)} collective-permute-done((f32[2,4,128]{2,1,0:T(4,128)S(1)}, f32[2,4,128]{2,1,0:T(4,128)S(1)}, u32[]{:S(2)}, u32[]{:S(2)}) %collective-permute-start.6) | collective-permute-done | bytes 4128 | tf_op jit(solution)/shard_map/ppermute | solution.py:335
  42.2 0.7 %finish.1 = f32[4,64]{1,0:T(4,128)} custom-call(f32[2,4,128]{2,1,0:T(4,128)S(1)} %get-tuple-element.9.refs_0_, f32[2,4,128]{2,1,0:T(4,128)S(1)} %collective-permute-done.4.refs_1_, f32[2,4,128]{2,1,0:T(4,128)S(1)} %collective-permute-done.5.refs_2_, f32[2,4,128]{2,1,0:T(4,128)S(1)} %collective-permute-done.6.refs_3_), custom_call_target="tpu_custom_call" | custom-call | tf_op jit(solution)/shard_map/finish/pallas_call | solution.py:337
Async XLA Ops:
  0.0 2.9 %collective-permute-start = (bf16[2,8,5120]{2,1,0:T(8,128)(2,1)}, bf16[2,8,5120]{2,1,0:T(8,128)(2,1)S(1)}, u32[]{:S(2)}, u32[]{:S(2)}) collective-permute-start(bf16[2,8,5120]{2,1,0:T(8,128)(2,1)} %bitcast.6), channel_id=1, source_target_pairs={{0,4},{4,0},{8,12},{12,8},{16,20},{20,16},{24,28},{28,24},{1,5},{5... | collective-permute-start | bytes 491528 | tf_op jit(solution)/shard_map/ppermute | solution.py:314
  3.9 28.9 %collective-permute-start.3 = (bf16[2,2,8,5120]{3,2,1,0:T(8,128)(2,1)S(1)}, bf16[2,2,8,5120]{3,2,1,0:T(8,128)(2,1)S(1)}, u32[]{:S(2)}, u32[]{:S(2)}) collective-permute-start(bf16[2,2,8,5120]{3,2,1,0:T(8,128)(2,1)S(1)} %pad_maximum_fusion.refs_2_), channel_id=1, source_target_pairs={{0,24},{4,28},{8,16},{12,20},{16,8},{20,12},{24,0},{28,4},{1,25},{... | collective-permute-start | bytes 983048 | tf_op jit(solution)/shard_map/ppermute | solution.py:321
  7.4 25.4 %collective-permute-start.2 = (bf16[2,2,8,5120]{3,2,1,0:T(8,128)(2,1)S(1)}, bf16[2,2,8,5120]{3,2,1,0:T(8,128)(2,1)S(1)}, u32[]{:S(2)}, u32[]{:S(2)}) collective-permute-start(bf16[2,2,8,5120]{3,2,1,0:T(8,128)(2,1)S(1)} %pad_maximum_fusion.refs_2_), channel_id=1, source_target_pairs={{0,16},{4,20},{8,24},{12,28},{16,0},{20,4},{24,8},{28,12},{1,17},{... | collective-permute-start | bytes 983048 | tf_op jit(solution)/shard_map/ppermute | solution.py:321
  7.9 24.9 %collective-permute-start.1 = (bf16[2,2,8,5120]{3,2,1,0:T(8,128)(2,1)S(1)}, bf16[2,2,8,5120]{3,2,1,0:T(8,128)(2,1)S(1)}, u32[]{:S(2)}, u32[]{:S(2)}) collective-permute-start(bf16[2,2,8,5120]{3,2,1,0:T(8,128)(2,1)S(1)} %pad_maximum_fusion.refs_2_), channel_id=1, source_target_pairs={{0,8},{4,12},{8,0},{12,4},{16,24},{20,28},{24,16},{28,20},{1,9},{5... | collective-permute-start | bytes 983048 | tf_op jit(solution)/shard_map/ppermute | solution.py:321
  8.0 24.8 %copy-start = (f32[2]{0:T(128)S(1)}, f32[2]{0:T(128)}, u32[]{:S(2)}) copy-start(f32[2]{0:T(128)} %refs_0_.1) | copy-start | bytes 28
  34.0 6.0 %collective-permute-start.4 = (f32[2,4,128]{2,1,0:T(4,128)S(1)}, f32[2,4,128]{2,1,0:T(4,128)S(1)}, u32[]{:S(2)}, u32[]{:S(2)}) collective-permute-start(f32[2,4,128]{2,1,0:T(4,128)S(1)} %get-tuple-element.10), channel_id=1, source_target_pairs={{0,1},{1,2},{2,3},{3,0},{4,5},{5,6},{6,7},{7,4},{8,9},{9,10},{10,1... | collective-permute-start | bytes 12296 | tf_op jit(solution)/shard_map/ppermute | solution.py:335
  36.0 4.5 %collective-permute-start.5 = (f32[2,4,128]{2,1,0:T(4,128)S(1)}, f32[2,4,128]{2,1,0:T(4,128)S(1)}, u32[]{:S(2)}, u32[]{:S(2)}) collective-permute-start(f32[2,4,128]{2,1,0:T(4,128)S(1)} %get-tuple-element.11), channel_id=1, source_target_pairs={{0,2},{1,3},{2,0},{3,1},{4,6},{5,7},{6,4},{7,5},{8,10},{9,11},{10,... | collective-permute-start | bytes 12296 | tf_op jit(solution)/shard_map/ppermute | solution.py:335
  38.6 3.6 %collective-permute-start.6 = (f32[2,4,128]{2,1,0:T(4,128)S(1)}, f32[2,4,128]{2,1,0:T(4,128)S(1)}, u32[]{:S(2)}, u32[]{:S(2)}) collective-permute-start(f32[2,4,128]{2,1,0:T(4,128)S(1)} %get-tuple-element.12), channel_id=1, source_target_pairs={{0,3},{1,0},{2,1},{3,2},{4,7},{5,4},{6,5},{7,6},{8,11},{9,8},{10,9... | collective-permute-start | bytes 12296 | tf_op jit(solution)/shard_map/ppermute | solution.py:335

commit v5 on v4

--- a/solution.py
+++ b/solution.py
@@ -26,10 +26,15 @@
 
 def feature_kernel(
     seed_ref,
-    act_ref,
+    len_hbm,
+    mask_hbm,
+    act_hbm,
     grad_hbm,
     var_hbm,
     out_ref,
+    len_ref,
+    mask_ref,
+    act_ref,
     grad_raw,
     var_raw,
     lhs_ring,
@@ -37,6 +42,7 @@
     sign_ring,
     act_blocks,
     feat_buf,
+    small_sems,
     grad_sems,
     var_sems,
     *,
@@ -64,17 +70,30 @@
         )
 
 
-    for copy in (*copies(0), *copies(1)):
+    small = [
+        pltpu.make_async_copy(src, dst, small_sems.at[i])
+        for i, (src, dst) in enumerate(
+            ((len_hbm, len_ref), (mask_hbm, mask_ref), (act_hbm, act_ref))
+        )
+    ]
+    for copy in (*small, *copies(0), *copies(1)):
         copy.start()
     act_blocks[...] = jnp.zeros_like(act_blocks)
+    for copy in small:
+        copy.wait()
     hash_base = (
         lax.axis_index("layer") * jnp.int32(668265263) + seed_ref[0] * jnp.int32(374761393)
     )
+    slot_ids = lax.broadcasted_iota(jnp.int32, (slots, 1), 0)
     for pair in range(pairs):
+        marks = [
+            (mask_ref[:, e : e + 1] == 1) & (slot_ids < len_ref[e])
+            for e in (2 * pair, 2 * pair + 1)
+        ]
         for c in range(ckpts):
             at = 2 * pair * slots
-            first = act_ref[c, at : at + slots, :].astype(F32)
-            second = act_ref[c, at + slots : at + 2 * slots, :].astype(F32)
+            first = jnp.where(marks[0], act_ref[c, at : at + slots, :].astype(F32), 0.0)
+            second = jnp.where(marks[1], act_ref[c, at + slots : at + 2 * slots, :].astype(F32), 0.0)
             blank = jnp.zeros_like(first)
             act_blocks[c * pairs + pair, at : at + 2 * slots, :] = jnp.concatenate(
                 [jnp.concatenate([first, blank], 1), jnp.concatenate([blank, second], 1)], 0
@@ -188,9 +207,12 @@
     )
 
 
-def features_of(seed, act, grad, var, slots, cols):
+def features_of(seed, lengths, mask, act, grad, var, cols):
     ckpts, rows, width = grad.shape
-    examples = rows // slots
+    slots, examples = mask.shape
+    stay = [
+        pltpu.with_memory_space_constraint(x, pltpu.HBM) for x in (lengths, mask, act, grad, var)
+    ]
     tiles = 8
     chunk = tiles * TILE
     pairs = examples // 2
@@ -209,9 +231,12 @@
     return pl.pallas_call(
         kernel,
         out_shape=jax.ShapeDtypeStruct((ckpts, examples, cols * LANES), BF16),
-        in_specs=[pl.BlockSpec(memory_space=pltpu.SMEM), vmem, hbm, hbm],
+        in_specs=[pl.BlockSpec(memory_space=pltpu.SMEM)] + [hbm] * 5,
         out_specs=vmem,
         scratch_shapes=[
+            pltpu.SMEM(lengths.shape, jnp.int32),
+            pltpu.VMEM(mask.shape, jnp.int32),
+            pltpu.VMEM(act.shape, BF16),
             pltpu.VMEM((ckpts, rows, width), BF16),
             pltpu.VMEM((ckpts, width, LANES), BF16),
             pltpu.VMEM((chunk, LANES), BF16),
@@ -219,15 +244,16 @@
             pltpu.VMEM((sign_rows, chunk), BF16),
             pltpu.VMEM((ckpts * pairs, TILE, TILE), BF16),
             pltpu.VMEM((examples, cols, LANES), F32),
+            pltpu.SemaphoreType.DMA((3,)),
             pltpu.SemaphoreType.DMA((ckpts * width // chunk,)),
             pltpu.SemaphoreType.DMA((ckpts * width // chunk,)),
         ],
-        compiler_params=pltpu.CompilerParams(vmem_limit_bytes=53 << 20),
+        compiler_params=pltpu.CompilerParams(vmem_limit_bytes=40 << 20),
         cost_estimate=pl.CostEstimate(
             flops=40_000_000_000, bytes_accessed=9_000_000, transcendentals=0
         ),
         name="features",
-    )(seed, act, grad, var)
+    )(seed, *stay)
 
 
 def score_kernel(*refs, groups, parts):
@@ -296,6 +322,35 @@
     out_ref[...] = result
 
 
+def place_kernel(*refs, turn):
+    block_ref, out_ref, sem = refs[0], refs[-2], refs[-1]
+    copy = pltpu.make_async_copy(block_ref, out_ref.at[:, turn], sem)
+    copy.start()
+    copy.wait()
+
+
+def together(blocks):
+    ckpts, *rest = blocks[0].shape
+    anywhere = pl.BlockSpec(memory_space=pl.ANY)
+    joined = ()
+    for turn, block in enumerate(blocks):
+        if turn == 0:
+            block = pltpu.with_memory_space_constraint(block, pltpu.HBM)
+        joined = (
+            pl.pallas_call(
+                functools.partial(place_kernel, turn=turn),
+                out_shape=jax.ShapeDtypeStruct((ckpts, len(blocks), *rest), block.dtype),
+                in_specs=[anywhere] * (1 + len(joined)),
+                out_specs=anywhere,
+                scratch_shapes=[pltpu.SemaphoreType.DMA],
+                input_output_aliases={1: 0} if joined else {},
+                compiler_params=pltpu.CompilerParams(vmem_limit_bytes=12 << 20),
+                name=f"place{turn}",
+            )(block, *joined),
+        )
+    return joined[0]
+
+
 def solution(mesh):
     parts = mesh.shape["layer"]
     peers = mesh.shape["dp"]
@@ -312,21 +367,20 @@
                 (i, i // members * members + (i + members - turn) % members) for i in range(peers)
             ]
             gathered.append(lax.ppermute(hold[:, 0], "dp", ring))
-        own = jnp.stack(gathered, axis=1)
+        own = together(gathered)
         holds = [own]
         for step in range(1, groups):
             ring = [
                 (i, target(i // members, step, groups) * members + i % members) for i in range(peers)
             ]
             holds.append(lax.ppermute(own, "dp", ring))
-        valid = (mask == 1) & (jnp.arange(slots, dtype=jnp.int32) < lengths[:, None])
-        valid = valid[None, :, :, None]
         feat = features_of(
             seed,
-            jnp.where(valid, act[:, 0], 0).reshape(ckpts, examples * slots, rank),
+            lengths,
+            mask.T,
+            act.reshape(ckpts, examples * slots, rank),
             grad.reshape(ckpts, examples * slots, width),
             var[:, 0],
-            slots,
             cols,
         )
         pieces = list(scores_of(weight, feat, holds, parts))

time: 43.1 us -> 41.9 us (0.972)
  other arithmetic: 2.57 us -> 0 us
  Pallas kernels: 26.5 us -> 28.2 us
    pallas_call x0 -> x2, Pallas kernels: none -> 1.04 us  [together(): pl.pallas_call(functools.partial(place_kernel, turn=turn), out_shape=jax....]
    another operation x1 -> x0, other arithmetic: 0.95 us -> none  [local(): own = jnp.stack(gathered, axis=1)]
    select_n x1 -> x0, other arithmetic: 0.93 us -> none  [local(): jnp.where(valid, act[:, 0], 0).reshape(ckpts, examples * slots, rank)]
    and x1 -> x0, other arithmetic: 0.7 us -> none  [local(): (mask == 1) & (jnp.arange(slots, dtype=jnp.int32) < lengths[:, None])]
    pallas_call x1, Pallas kernels: 24.7 us -> 25.4 us  [features_of(): pl.pallas_call(kernel, out_shape=jax.ShapeDtypeStruct((ckpts, examples, c...]
  transfers between devices with their start and end apart: 7 -> 7, of which waited for: 2 -> 2; matrix products, arithmetic and copies ran while one was open for 4% -> 0% of each run, Pallas kernels for 58% -> 63%
where the time goes in v5:
time: 41.9 us; the launch traced here: 41.7 us
  Pallas kernels  28.2 us (67%)
  starting transfers between devices  10.6 us (25%)
  waiting for transfers between devices  2.27 us (5%)
  between operations  0.73 us (2%)
    pallas_call x1, Pallas kernels, features_of(): pl.pallas_call(kernel, out_shape=jax.ShapeDtypeStruct((ckpts, examples, c...  25.4 us
    ppermute x3, starting transfers between devices, local(): pieces[step] = lax.ppermute(pieces[step], 'layer', ring)  5.96 us
    ppermute x3, starting transfers between devices, local(): holds.append(lax.ppermute(own, 'dp', ring))  4.15 us
    ppermute x3, waiting for transfers between devices, local(): pieces[step] = lax.ppermute(pieces[step], 'layer', ring)  2.26 us
    pallas_call x1, Pallas kernels, scores_of(): pl.pallas_call(functools.partial(score_kernel, groups=groups, parts=parts...  1.1 us
    pallas_call x2, Pallas kernels, together(): pl.pallas_call(functools.partial(place_kernel, turn=turn), out_shape=jax....  1.04 us
  transfers between devices with their start and end apart: 7, of which 2 were waited for; matrix products, arithmetic and copies ran while one was open for 0% of the time, Pallas kernels for 63%

profile of v5, /device:TPU:0, one launch (start us, length us, event | category | flops | bytes accessed | tf_op | source)
XLA Modules:
  0.0 41.7 jit_solution(10793760402173704080)
XLA Ops:
  0.0 0.5 %collective-permute-start = (bf16[2,8,5120]{2,1,0:T(8,128)(2,1)}, bf16[2,8,5120]{2,1,0:T(8,128)(2,1)S(1)}, u32[]{:S(2)}, u32[]{:S(2)}) collective-permute-start(bf16[2,8,5120]{2,1,0:T(8,128)(2,1)} %bitcast.5), channel_id=1, source_target_pairs={{0,4},{4,0},{8,12},{12,8},{16,20},{20,16},{24,28},{28,24},{1,5},{5... | collective-permute-start | bytes 491528 | tf_op jit(solution)/shard_map/ppermute | solution.py:369
  0.5 0.9 %place0.1.refs_1_ = bf16[2,2,8,5120]{3,2,1,0:T(8,128)(2,1)S(1)} custom-call(bf16[2,8,5120]{2,1,0:T(8,128)(2,1)} %bitcast.6), custom_call_target="tpu_custom_call" | custom-call | tf_op jit(solution)/shard_map/place0/pallas_call | solution.py:340
  2.0 0.0 collective-permute-done.refs_0_
  2.0 0.1 place1.1.refs_2_
  2.2 3.5 %collective-permute-start.3 = (bf16[2,2,8,5120]{3,2,1,0:T(8,128)(2,1)S(1)}, bf16[2,2,8,5120]{3,2,1,0:T(8,128)(2,1)S(1)}, u32[]{:S(2)}, u32[]{:S(2)}) collective-permute-start(bf16[2,2,8,5120]{3,2,1,0:T(8,128)(2,1)S(1)} %place1.1.refs_2_), channel_id=1, source_target_pairs={{0,24},{4,28},{8,16},{12,20},{16,8},{20,12},{24,0},{28,4},{1,25},{... | collective-permute-start | bytes 983048 | tf_op jit(solution)/shard_map/ppermute | solution.py:376
  5.7 0.5 %collective-permute-start.2 = (bf16[2,2,8,5120]{3,2,1,0:T(8,128)(2,1)S(1)}, bf16[2,2,8,5120]{3,2,1,0:T(8,128)(2,1)S(1)}, u32[]{:S(2)}, u32[]{:S(2)}) collective-permute-start(bf16[2,2,8,5120]{3,2,1,0:T(8,128)(2,1)S(1)} %place1.1.refs_2_), channel_id=1, source_target_pairs={{0,16},{4,20},{8,24},{12,28},{16,0},{20,4},{24,8},{28,12},{1,17},{... | collective-permute-start | bytes 983048 | tf_op jit(solution)/shard_map/ppermute | solution.py:376
  6.2 0.1 collective-permute-start.1
  6.3 0.0 copy-start
  6.3 25.4 %features.1.refs_1_ = bf16[2,16,5120]{2,1,0:T(8,128)(2,1)S(1)} custom-call(s32[1]{0:T(128)S(6)} %copy.11.seed_ref, s32[16]{0:T(128)} %len_hbm.1, s32[8,16]{1,0:T(8,128)} %bitcast.10, bf16[2,128,128]{2,1,0:T(8,128)(2,1)} %bitcast.9, bf16[2,128,8192]{2,1,0:T(8,128)(2,1)} %bitcast.7, bf16[2,8192,128]{2,1,0:T(8,128)(2,1)} %bitcast.8), custom_call_target="tpu_custom_call" | custom-call | flops 40000000000 | bytes 9000000 | tf_op jit(solution)/shard_map/features/pallas_call | solution.py:231
  31.7 0.0 collective-permute-done.3.refs_5_
  31.7 0.0 collective-permute-done.2.refs_4_
  31.7 0.0 collective-permute-done.1.refs_3_
  31.7 0.0 copy-done
  31.7 1.1 %scores.1 = (f32[2,4,128]{2,1,0:T(4,128)S(1)}, f32[2,4,128]{2,1,0:T(4,128)S(1)}, f32[2,4,128]{2,1,0:T(4,128)S(1)}, f32[2,4,128]{2,1,0:T(4,128)S(1)}) custom-call(f32[2]{0:T(128)S(1)} %copy-done, bf16[2,16,5120]{2,1,0:T(8,128)(2,1)S(1)} %features.1.refs_1_, bf16[2,2,8,5120]{3,2,1,0:T(8,128)(2,1)S(1)} %place1.1.refs_2_, ...), custom_call_target="tpu_custom_call" | custom-call | tf_op jit(solution)/shard_map/scores/pallas_call | solution.py:299
  32.8 2.0 %collective-permute-start.4 = (f32[2,4,128]{2,1,0:T(4,128)S(1)}, f32[2,4,128]{2,1,0:T(4,128)S(1)}, u32[]{:S(2)}, u32[]{:S(2)}) collective-permute-start(f32[2,4,128]{2,1,0:T(4,128)S(1)} %get-tuple-element.10), channel_id=1, source_target_pairs={{0,1},{1,2},{2,3},{3,0},{4,5},{5,6},{6,7},{7,4},{8,9},{9,10},{10,1... | collective-permute-start | bytes 12296 | tf_op jit(solution)/shard_map/ppermute | solution.py:389
  34.9 2.6 %collective-permute-start.5 = (f32[2,4,128]{2,1,0:T(4,128)S(1)}, f32[2,4,128]{2,1,0:T(4,128)S(1)}, u32[]{:S(2)}, u32[]{:S(2)}) collective-permute-start(f32[2,4,128]{2,1,0:T(4,128)S(1)} %get-tuple-element.11), channel_id=1, source_target_pairs={{0,2},{1,3},{2,0},{3,1},{4,6},{5,7},{6,4},{7,5},{8,10},{9,11},{10,... | collective-permute-start | bytes 12296 | tf_op jit(solution)/shard_map/ppermute | solution.py:389
  37.5 1.3 %collective-permute-start.6 = (f32[2,4,128]{2,1,0:T(4,128)S(1)}, f32[2,4,128]{2,1,0:T(4,128)S(1)}, u32[]{:S(2)}, u32[]{:S(2)}) collective-permute-start(f32[2,4,128]{2,1,0:T(4,128)S(1)} %get-tuple-element.12), channel_id=1, source_target_pairs={{0,3},{1,0},{2,1},{3,2},{4,7},{5,4},{6,5},{7,6},{8,11},{9,8},{10,9... | collective-permute-start | bytes 12296 | tf_op jit(solution)/shard_map/ppermute | solution.py:389
  38.8 0.0 collective-permute-done.4.refs_1_
  38.8 0.6 %collective-permute-done.5.refs_2_ = f32[2,4,128]{2,1,0:T(4,128)S(1)} collective-permute-done((f32[2,4,128]{2,1,0:T(4,128)S(1)}, f32[2,4,128]{2,1,0:T(4,128)S(1)}, u32[]{:S(2)}, u32[]{:S(2)}) %collective-permute-start.5) | collective-permute-done | bytes 4128 | tf_op jit(solution)/shard_map/ppermute | solution.py:389
  39.4 1.7 %collective-permute-done.6.refs_3_ = f32[2,4,128]{2,1,0:T(4,128)S(1)} collective-permute-done((f32[2,4,128]{2,1,0:T(4,128)S(1)}, f32[2,4,128]{2,1,0:T(4,128)S(1)}, u32[]{:S(2)}, u32[]{:S(2)}) %collective-permute-start.6) | collective-permute-done | bytes 4128 | tf_op jit(solution)/shard_map/ppermute | solution.py:389
  41.1 0.7 %finish.1 = f32[4,64]{1,0:T(4,128)} custom-call(f32[2,4,128]{2,1,0:T(4,128)S(1)} %get-tuple-element.9.refs_0_, f32[2,4,128]{2,1,0:T(4,128)S(1)} %collective-permute-done.4.refs_1_, f32[2,4,128]{2,1,0:T(4,128)S(1)} %collective-permute-done.5.refs_2_, f32[2,4,128]{2,1,0:T(4,128)S(1)} %collective-permute-done.6.refs_3_), custom_call_target="tpu_custom_call" | custom-call | tf_op jit(solution)/shard_map/finish/pallas_call | solution.py:391
Async XLA Ops:
  0.0 2.0 %collective-permute-start = (bf16[2,8,5120]{2,1,0:T(8,128)(2,1)}, bf16[2,8,5120]{2,1,0:T(8,128)(2,1)S(1)}, u32[]{:S(2)}, u32[]{:S(2)}) collective-permute-start(bf16[2,8,5120]{2,1,0:T(8,128)(2,1)} %bitcast.5), channel_id=1, source_target_pairs={{0,4},{4,0},{8,12},{12,8},{16,20},{20,16},{24,28},{28,24},{1,5},{5... | collective-permute-start | bytes 491528 | tf_op jit(solution)/shard_map/ppermute | solution.py:369
  2.2 29.5 %collective-permute-start.3 = (bf16[2,2,8,5120]{3,2,1,0:T(8,128)(2,1)S(1)}, bf16[2,2,8,5120]{3,2,1,0:T(8,128)(2,1)S(1)}, u32[]{:S(2)}, u32[]{:S(2)}) collective-permute-start(bf16[2,2,8,5120]{3,2,1,0:T(8,128)(2,1)S(1)} %place1.1.refs_2_), channel_id=1, source_target_pairs={{0,24},{4,28},{8,16},{12,20},{16,8},{20,12},{24,0},{28,4},{1,25},{... | collective-permute-start | bytes 983048 | tf_op jit(solution)/shard_map/ppermute | solution.py:376
  5.7 26.0 %collective-permute-start.2 = (bf16[2,2,8,5120]{3,2,1,0:T(8,128)(2,1)S(1)}, bf16[2,2,8,5120]{3,2,1,0:T(8,128)(2,1)S(1)}, u32[]{:S(2)}, u32[]{:S(2)}) collective-permute-start(bf16[2,2,8,5120]{3,2,1,0:T(8,128)(2,1)S(1)} %place1.1.refs_2_), channel_id=1, source_target_pairs={{0,16},{4,20},{8,24},{12,28},{16,0},{20,4},{24,8},{28,12},{1,17},{... | collective-permute-start | bytes 983048 | tf_op jit(solution)/shard_map/ppermute | solution.py:376
  6.2 25.5 %collective-permute-start.1 = (bf16[2,2,8,5120]{3,2,1,0:T(8,128)(2,1)S(1)}, bf16[2,2,8,5120]{3,2,1,0:T(8,128)(2,1)S(1)}, u32[]{:S(2)}, u32[]{:S(2)}) collective-permute-start(bf16[2,2,8,5120]{3,2,1,0:T(8,128)(2,1)S(1)} %place1.1.refs_2_), channel_id=1, source_target_pairs={{0,8},{4,12},{8,0},{12,4},{16,24},{20,28},{24,16},{28,20},{1,9},{5... | collective-permute-start | bytes 983048 | tf_op jit(solution)/shard_map/ppermute | solution.py:376
  6.3 25.4 %copy-start = (f32[2]{0:T(128)S(1)}, f32[2]{0:T(128)}, u32[]{:S(2)}) copy-start(f32[2]{0:T(128)} %refs_0_.1) | copy-start | bytes 28
  32.8 6.0 %collective-permute-start.4 = (f32[2,4,128]{2,1,0:T(4,128)S(1)}, f32[2,4,128]{2,1,0:T(4,128)S(1)}, u32[]{:S(2)}, u32[]{:S(2)}) collective-permute-start(f32[2,4,128]{2,1,0:T(4,128)S(1)} %get-tuple-element.10), channel_id=1, source_target_pairs={{0,1},{1,2},{2,3},{3,0},{4,5},{5,6},{6,7},{7,4},{8,9},{9,10},{10,1... | collective-permute-start | bytes 12296 | tf_op jit(solution)/shard_map/ppermute | solution.py:389
  34.9 4.5 %collective-permute-start.5 = (f32[2,4,128]{2,1,0:T(4,128)S(1)}, f32[2,4,128]{2,1,0:T(4,128)S(1)}, u32[]{:S(2)}, u32[]{:S(2)}) collective-permute-start(f32[2,4,128]{2,1,0:T(4,128)S(1)} %get-tuple-element.11), channel_id=1, source_target_pairs={{0,2},{1,3},{2,0},{3,1},{4,6},{5,7},{6,4},{7,5},{8,10},{9,11},{10,... | collective-permute-start | bytes 12296 | tf_op jit(solution)/shard_map/ppermute | solution.py:389
  37.5 3.6 %collective-permute-start.6 = (f32[2,4,128]{2,1,0:T(4,128)S(1)}, f32[2,4,128]{2,1,0:T(4,128)S(1)}, u32[]{:S(2)}, u32[]{:S(2)}) collective-permute-start(f32[2,4,128]{2,1,0:T(4,128)S(1)} %get-tuple-element.12), channel_id=1, source_target_pairs={{0,3},{1,0},{2,1},{3,2},{4,7},{5,4},{6,5},{7,6},{8,11},{9,8},{10,9... | collective-permute-start | bytes 12296 | tf_op jit(solution)/shard_map/ppermute | solution.py:389

commit v6 on v5

--- a/solution.py
+++ b/solution.py
@@ -26,25 +26,17 @@
 
 def feature_kernel(
     seed_ref,
-    len_hbm,
-    mask_hbm,
-    act_hbm,
-    grad_hbm,
-    var_hbm,
-    out_ref,
     len_ref,
     mask_ref,
     act_ref,
     grad_raw,
     var_raw,
+    out_ref,
     lhs_ring,
     scale_ring,
     sign_ring,
     act_blocks,
     feat_buf,
-    small_sems,
-    grad_sems,
-    var_sems,
     *,
     ckpts,
     examples,
@@ -61,26 +53,7 @@
     sign_rows = sign_ring.shape[0]
     inv_root = 1.0 / math.sqrt(width)
 
-    def copies(it):
-        c, q = it // chunks, it % chunks
-        at = pl.ds(pl.multiple_of(q * chunk, chunk), chunk)
-        return (
-            pltpu.make_async_copy(grad_hbm.at[c, :, at], grad_raw.at[c, :, at], grad_sems.at[it]),
-            pltpu.make_async_copy(var_hbm.at[c, at, :], var_raw.at[c, at, :], var_sems.at[it]),
-        )
-
-
-    small = [
-        pltpu.make_async_copy(src, dst, small_sems.at[i])
-        for i, (src, dst) in enumerate(
-            ((len_hbm, len_ref), (mask_hbm, mask_ref), (act_hbm, act_ref))
-        )
-    ]
-    for copy in (*small, *copies(0), *copies(1)):
-        copy.start()
     act_blocks[...] = jnp.zeros_like(act_blocks)
-    for copy in small:
-        copy.wait()
     hash_base = (
         lax.axis_index("layer") * jnp.int32(668265263) + seed_ref[0] * jnp.int32(374761393)
     )
@@ -120,11 +93,6 @@
             sign = (2 * ((m >> 7) & 1) - 1).astype(F32)
             sign_ring[:, here : here + TILE] = jnp.where(k < cols, sign, 0.0).astype(BF16)
 
-    for copy in copies(0):
-        copy.wait()
-    for it in range(2, total):
-        for copy in copies(it):
-            copy.start()
     for t in range(READY):
         for part in range(4):
             prepare(0, t, part)
@@ -155,11 +123,6 @@
         def one_chunk(c, q):
             it = c * chunks + q
             following = jnp.minimum(it + 1, total - 1)
-
-            @pl.when(it + 1 < total)
-            def _():
-                for copy in copies(it + 1):
-                    copy.wait()
 
             for n in range(1, AHEAD):
                 for m in (0, 1):
@@ -210,15 +173,12 @@
 def features_of(seed, lengths, mask, act, grad, var, cols):
     ckpts, rows, width = grad.shape
     slots, examples = mask.shape
-    stay = [
-        pltpu.with_memory_space_constraint(x, pltpu.HBM) for x in (lengths, mask, act, grad, var)
-    ]
     tiles = 8
     chunk = tiles * TILE
     pairs = examples // 2
     sign_rows = -(-cols // 16) * 16
     vmem = pl.BlockSpec(memory_space=pltpu.VMEM)
-    hbm = pl.BlockSpec(memory_space=pltpu.HBM)
+    smem = pl.BlockSpec(memory_space=pltpu.SMEM)
     kernel = functools.partial(
         feature_kernel,
         ckpts=ckpts,
@@ -231,29 +191,21 @@
     return pl.pallas_call(
         kernel,
         out_shape=jax.ShapeDtypeStruct((ckpts, examples, cols * LANES), BF16),
-        in_specs=[pl.BlockSpec(memory_space=pltpu.SMEM)] + [hbm] * 5,
+        in_specs=[smem, smem] + [vmem] * 4,
         out_specs=vmem,
         scratch_shapes=[
-            pltpu.SMEM(lengths.shape, jnp.int32),
-            pltpu.VMEM(mask.shape, jnp.int32),
-            pltpu.VMEM(act.shape, BF16),
-            pltpu.VMEM((ckpts, rows, width), BF16),
-            pltpu.VMEM((ckpts, width, LANES), BF16),
             pltpu.VMEM((chunk, LANES), BF16),
             pltpu.VMEM((chunk, LANES), F32),
             pltpu.VMEM((sign_rows, chunk), BF16),
             pltpu.VMEM((ckpts * pairs, TILE, TILE), BF16),
             pltpu.VMEM((examples, cols, LANES), F32),
-            pltpu.SemaphoreType.DMA((3,)),
-            pltpu.SemaphoreType.DMA((ckpts * width // chunk,)),
-            pltpu.SemaphoreType.DMA((ckpts * width // chunk,)),
         ],
-        compiler_params=pltpu.CompilerParams(vmem_limit_bytes=40 << 20),
+        compiler_params=pltpu.CompilerParams(vmem_limit_bytes=24 << 20),
         cost_estimate=pl.CostEstimate(
             flops=40_000_000_000, bytes_accessed=9_000_000, transcendentals=0
         ),
         name="features",
-    )(seed, *stay)
+    )(seed, lengths, mask, act, grad, var)
 
 
 def score_kernel(*refs, groups, parts):
@@ -345,6 +297,9 @@
                 scratch_shapes=[pltpu.SemaphoreType.DMA],
                 input_output_aliases={1: 0} if joined else {},
                 compiler_params=pltpu.CompilerParams(vmem_limit_bytes=12 << 20),
+                cost_estimate=pl.CostEstimate(
+                    flops=10_000_000_000, bytes_accessed=700_000, transcendentals=0
+                ),
                 name=f"place{turn}",
             )(block, *joined),
         )

time: 41.9 us -> 40.6 us (0.969)
  Pallas kernels: 28.2 us -> 26.8 us
    pallas_call x1, Pallas kernels: 25.4 us -> 24 us  [features_of(): pl.pallas_call(kernel, out_shape=jax.ShapeDtypeStruct((ckpts, examples, c...]
  transfers between devices with their start and end apart: 7 -> 7, of which waited for: 2 -> 2; matrix products, arithmetic and copies ran while one was open for 0% -> 0% of each run, Pallas kernels for 63% -> 62%
where the time goes in v6:
time: 40.6 us; the launch traced here: 40.5 us
  Pallas kernels  26.8 us (66%)
  starting transfers between devices  10.6 us (26%)
  waiting for transfers between devices  2.27 us (6%)
  between operations  0.78 us (2%)
    pallas_call x1, Pallas kernels, features_of(): pl.pallas_call(kernel, out_shape=jax.ShapeDtypeStruct((ckpts, examples, c...  24 us
    ppermute x3, starting transfers between devices, local(): pieces[step] = lax.ppermute(pieces[step], 'layer', ring)  5.96 us
    ppermute x3, starting transfers between devices, local(): holds.append(lax.ppermute(own, 'dp', ring))  4.15 us
    ppermute x3, waiting for transfers between devices, local(): pieces[step] = lax.ppermute(pieces[step], 'layer', ring)  2.26 us
    pallas_call x1, Pallas kernels, scores_of(): pl.pallas_call(functools.partial(score_kernel, groups=groups, parts=parts...  1.1 us
    pallas_call x2, Pallas kernels, together(): pl.pallas_call(functools.partial(place_kernel, turn=turn), out_shape=jax....  1.04 us
  transfers between devices with their start and end apart: 7, of which 2 were waited for; matrix products, arithmetic and copies ran while one was open for 0% of the time, Pallas kernels for 62%

profile of v6, /device:TPU:0, one launch (start us, length us, event | category | flops | bytes accessed | tf_op | source)
XLA Modules:
  0.0 40.5 jit_solution(14271953300208159159)
XLA Ops:
  0.0 0.5 %collective-permute-start = (bf16[2,8,5120]{2,1,0:T(8,128)(2,1)}, bf16[2,8,5120]{2,1,0:T(8,128)(2,1)S(1)}, u32[]{:S(2)}, u32[]{:S(2)}) collective-permute-start(bf16[2,8,5120]{2,1,0:T(8,128)(2,1)} %bitcast.9), channel_id=1, source_target_pairs={{0,4},{4,0},{8,12},{12,8},{16,20},{20,16},{24,28},{28,24},{1,5},{5... | collective-permute-start | bytes 491528 | tf_op jit(solution)/shard_map/ppermute | solution.py:324
  0.5 0.9 %place0.1.refs_1_ = bf16[2,2,8,5120]{3,2,1,0:T(8,128)(2,1)S(1)} custom-call(bf16[2,8,5120]{2,1,0:T(8,128)(2,1)} %bitcast.10), custom_call_target="tpu_custom_call" | custom-call | flops 10000000000 | bytes 700000 | tf_op jit(solution)/shard_map/place0/pallas_call | solution.py:292
  2.0 0.0 copy-start.1
  2.0 0.0 copy-start.2
  2.1 0.0 copy-start.3
  2.1 0.0 copy-start.4
  2.1 0.0 copy-start.5
  2.1 0.0 collective-permute-done.refs_0_
  2.1 0.1 place1.1.refs_2_
  2.2 3.5 %collective-permute-start.3 = (bf16[2,2,8,5120]{3,2,1,0:T(8,128)(2,1)S(1)}, bf16[2,2,8,5120]{3,2,1,0:T(8,128)(2,1)S(1)}, u32[]{:S(2)}, u32[]{:S(2)}) collective-permute-start(bf16[2,2,8,5120]{3,2,1,0:T(8,128)(2,1)S(1)} %place1.1.refs_2_), channel_id=1, source_target_pairs={{0,24},{4,28},{8,16},{12,20},{16,8},{20,12},{24,0},{28,4},{1,25},{... | collective-permute-start | bytes 983048 | tf_op jit(solution)/shard_map/ppermute | solution.py:331
  5.7 0.5 %collective-permute-start.2 = (bf16[2,2,8,5120]{3,2,1,0:T(8,128)(2,1)S(1)}, bf16[2,2,8,5120]{3,2,1,0:T(8,128)(2,1)S(1)}, u32[]{:S(2)}, u32[]{:S(2)}) collective-permute-start(bf16[2,2,8,5120]{3,2,1,0:T(8,128)(2,1)S(1)} %place1.1.refs_2_), channel_id=1, source_target_pairs={{0,16},{4,20},{8,24},{12,28},{16,0},{20,4},{24,8},{28,12},{1,17},{... | collective-permute-start | bytes 983048 | tf_op jit(solution)/shard_map/ppermute | solution.py:331
  6.2 0.1 collective-permute-start.1
  6.4 0.0 copy-start
  6.4 24.0 %features.1.refs_1_ = bf16[2,16,5120]{2,1,0:T(8,128)(2,1)S(1)} custom-call(s32[1]{0:T(128)S(6)} %copy.11.seed_ref, s32[16]{0:T(128)S(1)} %copy-done.5, s32[8,16]{1,0:T(8,128)S(1)} %bitcast.8, bf16[2,128,128]{2,1,0:T(8,128)(2,1)S(1)} %bitcast.7, bf16[2,128,8192]{2,1,0:T(8,128)(2,1)S(1)} %bitcast.5, bf16[2,8192,128]{2,1,0:T(8,128)(2,1)S(1)} %bitcast.6), custom_call_target="tpu_custom_call" | custom-call | flops 40000000000 | bytes 9000000 | tf_op jit(solution)/shard_map/features/pallas_call | solution.py:191
  30.5 0.0 collective-permute-done.3.refs_5_
  30.5 0.0 collective-permute-done.2.refs_4_
  30.5 0.0 collective-permute-done.1.refs_3_
  30.5 1.1 %scores.1 = (f32[2,4,128]{2,1,0:T(4,128)S(1)}, f32[2,4,128]{2,1,0:T(4,128)S(1)}, f32[2,4,128]{2,1,0:T(4,128)S(1)}, f32[2,4,128]{2,1,0:T(4,128)S(1)}) custom-call(f32[2]{0:T(128)S(1)} %copy-done, bf16[2,16,5120]{2,1,0:T(8,128)(2,1)S(1)} %features.1.refs_1_, bf16[2,2,8,5120]{3,2,1,0:T(8,128)(2,1)S(1)} %place1.1.refs_2_, ...), custom_call_target="tpu_custom_call" | custom-call | tf_op jit(solution)/shard_map/scores/pallas_call | solution.py:251
  31.6 2.0 %collective-permute-start.4 = (f32[2,4,128]{2,1,0:T(4,128)S(1)}, f32[2,4,128]{2,1,0:T(4,128)S(1)}, u32[]{:S(2)}, u32[]{:S(2)}) collective-permute-start(f32[2,4,128]{2,1,0:T(4,128)S(1)} %get-tuple-element.10), channel_id=1, source_target_pairs={{0,1},{1,2},{2,3},{3,0},{4,5},{5,6},{6,7},{7,4},{8,9},{9,10},{10,1... | collective-permute-start | bytes 12296 | tf_op jit(solution)/shard_map/ppermute | solution.py:344
  33.6 2.6 %collective-permute-start.5 = (f32[2,4,128]{2,1,0:T(4,128)S(1)}, f32[2,4,128]{2,1,0:T(4,128)S(1)}, u32[]{:S(2)}, u32[]{:S(2)}) collective-permute-start(f32[2,4,128]{2,1,0:T(4,128)S(1)} %get-tuple-element.11), channel_id=1, source_target_pairs={{0,2},{1,3},{2,0},{3,1},{4,6},{5,7},{6,4},{7,5},{8,10},{9,11},{10,... | collective-permute-start | bytes 12296 | tf_op jit(solution)/shard_map/ppermute | solution.py:344
  36.2 1.3 %collective-permute-start.6 = (f32[2,4,128]{2,1,0:T(4,128)S(1)}, f32[2,4,128]{2,1,0:T(4,128)S(1)}, u32[]{:S(2)}, u32[]{:S(2)}) collective-permute-start(f32[2,4,128]{2,1,0:T(4,128)S(1)} %get-tuple-element.12), channel_id=1, source_target_pairs={{0,3},{1,0},{2,1},{3,2},{4,7},{5,4},{6,5},{7,6},{8,11},{9,8},{10,9... | collective-permute-start | bytes 12296 | tf_op jit(solution)/shard_map/ppermute | solution.py:344
  37.6 0.6 %collective-permute-done.5.refs_2_ = f32[2,4,128]{2,1,0:T(4,128)S(1)} collective-permute-done((f32[2,4,128]{2,1,0:T(4,128)S(1)}, f32[2,4,128]{2,1,0:T(4,128)S(1)}, u32[]{:S(2)}, u32[]{:S(2)}) %collective-permute-start.5) | collective-permute-done | bytes 4128 | tf_op jit(solution)/shard_map/ppermute | solution.py:344
  38.2 1.7 %collective-permute-done.6.refs_3_ = f32[2,4,128]{2,1,0:T(4,128)S(1)} collective-permute-done((f32[2,4,128]{2,1,0:T(4,128)S(1)}, f32[2,4,128]{2,1,0:T(4,128)S(1)}, u32[]{:S(2)}, u32[]{:S(2)}) %collective-permute-start.6) | collective-permute-done | bytes 4128 | tf_op jit(solution)/shard_map/ppermute | solution.py:344
  39.8 0.7 %finish.1 = f32[4,64]{1,0:T(4,128)} custom-call(f32[2,4,128]{2,1,0:T(4,128)S(1)} %get-tuple-element.9.refs_0_, f32[2,4,128]{2,1,0:T(4,128)S(1)} %collective-permute-done.4.refs_1_, f32[2,4,128]{2,1,0:T(4,128)S(1)} %collective-permute-done.5.refs_2_, f32[2,4,128]{2,1,0:T(4,128)S(1)} %collective-permute-done.6.refs_3_), custom_call_target="tpu_custom_call" | custom-call | tf_op jit(solution)/shard_map/finish/pallas_call | solution.py:346
  (7 shorter events, 0.0 us)
Async XLA Ops:
  0.0 2.1 %collective-permute-start = (bf16[2,8,5120]{2,1,0:T(8,128)(2,1)}, bf16[2,8,5120]{2,1,0:T(8,128)(2,1)S(1)}, u32[]{:S(2)}, u32[]{:S(2)}) collective-permute-start(bf16[2,8,5120]{2,1,0:T(8,128)(2,1)} %bitcast.9), channel_id=1, source_target_pairs={{0,4},{4,0},{8,12},{12,8},{16,20},{20,16},{24,28},{28,24},{1,5},{5... | collective-permute-start | bytes 491528 | tf_op jit(solution)/shard_map/ppermute | solution.py:324
  2.0 4.4 %copy-start.1 = (bf16[2,1,16,8,8192]{4,3,2,1,0:T(8,128)(2,1)S(1)}, bf16[2,1,16,8,8192]{4,3,2,1,0:T(8,128)(2,1)}, u32[]{:S(2)}) copy-start(bf16[2,1,16,8,8192]{4,3,2,1,0:T(8,128)(2,1)} %param.8) | copy-start | bytes 12582916
  2.0 4.3 %copy-start.2 = (bf16[2,1,8192,128]{3,2,1,0:T(8,128)(2,1)S(1)}, bf16[2,1,8192,128]{3,2,1,0:T(8,128)(2,1)}, u32[]{:S(2)}) copy-start(bf16[2,1,8192,128]{3,2,1,0:T(8,128)(2,1)} %param.10) | copy-start | bytes 12582916
  2.1 4.3 %copy-start.3 = (bf16[2,1,16,8,128]{4,3,2,1,0:T(8,128)(2,1)S(1)}, bf16[2,1,16,8,128]{4,3,2,1,0:T(8,128)(2,1)}, u32[]{:S(2)}) copy-start(bf16[2,1,16,8,128]{4,3,2,1,0:T(8,128)(2,1)} %param.9) | copy-start | bytes 196612
  2.1 4.3 %copy-start.4 = (s32[16,8]{0,1:T(8,128)S(1)}, s32[16,8]{0,1:T(8,128)}, u32[]{:S(2)}) copy-start(s32[16,8]{0,1:T(8,128)} %param.13) | copy-start | bytes 1540
  2.1 4.3 %copy-start.5 = (s32[16]{0:T(128)S(1)}, s32[16]{0:T(128)}, u32[]{:S(2)}) copy-start(s32[16]{0:T(128)} %len_ref.1) | copy-start | bytes 196
  2.2 28.2 %collective-permute-start.3 = (bf16[2,2,8,5120]{3,2,1,0:T(8,128)(2,1)S(1)}, bf16[2,2,8,5120]{3,2,1,0:T(8,128)(2,1)S(1)}, u32[]{:S(2)}, u32[]{:S(2)}) collective-permute-start(bf16[2,2,8,5120]{3,2,1,0:T(8,128)(2,1)S(1)} %place1.1.refs_2_), channel_id=1, source_target_pairs={{0,24},{4,28},{8,16},{12,20},{16,8},{20,12},{24,0},{28,4},{1,25},{... | collective-permute-start | bytes 983048 | tf_op jit(solution)/shard_map/ppermute | solution.py:331
  5.7 24.7 %collective-permute-start.2 = (bf16[2,2,8,5120]{3,2,1,0:T(8,128)(2,1)S(1)}, bf16[2,2,8,5120]{3,2,1,0:T(8,128)(2,1)S(1)}, u32[]{:S(2)}, u32[]{:S(2)}) collective-permute-start(bf16[2,2,8,5120]{3,2,1,0:T(8,128)(2,1)S(1)} %place1.1.refs_2_), channel_id=1, source_target_pairs={{0,16},{4,20},{8,24},{12,28},{16,0},{20,4},{24,8},{28,12},{1,17},{... | collective-permute-start | bytes 983048 | tf_op jit(solution)/shard_map/ppermute | solution.py:331
  6.2 24.2 %collective-permute-start.1 = (bf16[2,2,8,5120]{3,2,1,0:T(8,128)(2,1)S(1)}, bf16[2,2,8,5120]{3,2,1,0:T(8,128)(2,1)S(1)}, u32[]{:S(2)}, u32[]{:S(2)}) collective-permute-start(bf16[2,2,8,5120]{3,2,1,0:T(8,128)(2,1)S(1)} %place1.1.refs_2_), channel_id=1, source_target_pairs={{0,8},{4,12},{8,0},{12,4},{16,24},{20,28},{24,16},{28,20},{1,9},{5... | collective-permute-start | bytes 983048 | tf_op jit(solution)/shard_map/ppermute | solution.py:331
  6.4 24.1 %copy-start = (f32[2]{0:T(128)S(1)}, f32[2]{0:T(128)}, u32[]{:S(2)}) copy-start(f32[2]{0:T(128)} %refs_0_.1) | copy-start | bytes 28
  31.6 6.0 %collective-permute-start.4 = (f32[2,4,128]{2,1,0:T(4,128)S(1)}, f32[2,4,128]{2,1,0:T(4,128)S(1)}, u32[]{:S(2)}, u32[]{:S(2)}) collective-permute-start(f32[2,4,128]{2,1,0:T(4,128)S(1)} %get-tuple-element.10), channel_id=1, source_target_pairs={{0,1},{1,2},{2,3},{3,0},{4,5},{5,6},{6,7},{7,4},{8,9},{9,10},{10,1... | collective-permute-start | bytes 12296 | tf_op jit(solution)/shard_map/ppermute | solution.py:344
  33.6 4.5 %collective-permute-start.5 = (f32[2,4,128]{2,1,0:T(4,128)S(1)}, f32[2,4,128]{2,1,0:T(4,128)S(1)}, u32[]{:S(2)}, u32[]{:S(2)}) collective-permute-start(f32[2,4,128]{2,1,0:T(4,128)S(1)} %get-tuple-element.11), channel_id=1, source_target_pairs={{0,2},{1,3},{2,0},{3,1},{4,6},{5,7},{6,4},{7,5},{8,10},{9,11},{10,... | collective-permute-start | bytes 12296 | tf_op jit(solution)/shard_map/ppermute | solution.py:344
  36.2 3.6 %collective-permute-start.6 = (f32[2,4,128]{2,1,0:T(4,128)S(1)}, f32[2,4,128]{2,1,0:T(4,128)S(1)}, u32[]{:S(2)}, u32[]{:S(2)}) collective-permute-start(f32[2,4,128]{2,1,0:T(4,128)S(1)} %get-tuple-element.12), channel_id=1, source_target_pairs={{0,3},{1,0},{2,1},{3,2},{4,7},{5,4},{6,5},{7,6},{8,11},{9,8},{10,9... | collective-permute-start | bytes 12296 | tf_op jit(solution)/shard_map/ppermute | solution.py:344

commit v7 on v6

--- a/solution.py
+++ b/solution.py
@@ -53,7 +53,6 @@
     sign_rows = sign_ring.shape[0]
     inv_root = 1.0 / math.sqrt(width)
 
-    act_blocks[...] = jnp.zeros_like(act_blocks)
     hash_base = (
         lax.axis_index("layer") * jnp.int32(668265263) + seed_ref[0] * jnp.int32(374761393)
     )
@@ -68,7 +67,7 @@
             first = jnp.where(marks[0], act_ref[c, at : at + slots, :].astype(F32), 0.0)
             second = jnp.where(marks[1], act_ref[c, at + slots : at + 2 * slots, :].astype(F32), 0.0)
             blank = jnp.zeros_like(first)
-            act_blocks[c * pairs + pair, at : at + 2 * slots, :] = jnp.concatenate(
+            act_blocks[c * pairs + pair] = jnp.concatenate(
                 [jnp.concatenate([first, blank], 1), jnp.concatenate([blank, second], 1)], 0
             ).astype(BF16)
 
@@ -106,7 +105,11 @@
         def outer(c, m, n):
             t, j = steps[n]
             tokens = lhs_ring[t * TILE : (t + 1) * TILE, :]
-            pltpu.matmul_push_rhs(act_blocks[c * pairs + m * per_unit + j], 0, m)
+            pair = m * per_unit + j
+            sizes = (2 * slots * pair, TILE - 2 * slots * (pair + 1))
+            above, below = ([jnp.zeros((n, TILE), BF16)] if n else [] for n in sizes)
+            block = [*above, act_blocks[c * pairs + pair], *below]
+            pltpu.matmul_push_rhs(jnp.concatenate(block, 0), 0, m)
             pltpu.matmul_acc_lhs(
                 outer_acc[m][n % depth], jnp.concatenate([tokens, tokens], 1), load_staged_rhs=0
             )
@@ -197,7 +200,7 @@
             pltpu.VMEM((chunk, LANES), BF16),
             pltpu.VMEM((chunk, LANES), F32),
             pltpu.VMEM((sign_rows, chunk), BF16),
-            pltpu.VMEM((ckpts * pairs, TILE, TILE), BF16),
+            pltpu.VMEM((ckpts * pairs, 2 * slots, TILE), BF16),
             pltpu.VMEM((examples, cols, LANES), F32),
         ],
         compiler_params=pltpu.CompilerParams(vmem_limit_bytes=24 << 20),

time: 40.6 us -> 40.4 us (level)
  transfers between devices with their start and end apart: 7 -> 7, of which waited for: 2 -> 2; matrix products, arithmetic and copies ran while one was open for 0% -> 0% of each run, Pallas kernels for 62% -> 61%
where the time goes in v7:
time: 40.4 us; the launch traced here: 40.3 us
  Pallas kernels  26.6 us (66%)
  starting transfers between devices  10.6 us (26%)
  waiting for transfers between devices  2.26 us (6%)
  between operations  0.78 us (2%)
    pallas_call x1, Pallas kernels, features_of(): pl.pallas_call(kernel, out_shape=jax.ShapeDtypeStruct((ckpts, examples, c...  23.8 us
    ppermute x3, starting transfers between devices, local(): pieces[step] = lax.ppermute(pieces[step], 'layer', ring)  5.97 us
    ppermute x3, starting transfers between devices, local(): holds.append(lax.ppermute(own, 'dp', ring))  4.15 us
    ppermute x3, waiting for transfers between devices, local(): pieces[step] = lax.ppermute(pieces[step], 'layer', ring)  2.25 us
    pallas_call x1, Pallas kernels, scores_of(): pl.pallas_call(functools.partial(score_kernel, groups=groups, parts=parts...  1.1 us
    pallas_call x2, Pallas kernels, together(): pl.pallas_call(functools.partial(place_kernel, turn=turn), out_shape=jax....  1.04 us
  transfers between devices with their start and end apart: 7, of which 2 were waited for; matrix products, arithmetic and copies ran while one was open for 0% of the time, Pallas kernels for 61%

profile of v7, /device:TPU:0, one launch (start us, length us, event | category | flops | bytes accessed | tf_op | source)
XLA Modules:
  0.0 40.3 jit_solution(18005641315095766014)
XLA Ops:
  0.0 0.5 %collective-permute-start = (bf16[2,8,5120]{2,1,0:T(8,128)(2,1)}, bf16[2,8,5120]{2,1,0:T(8,128)(2,1)S(1)}, u32[]{:S(2)}, u32[]{:S(2)}) collective-permute-start(bf16[2,8,5120]{2,1,0:T(8,128)(2,1)} %bitcast.9), channel_id=1, source_target_pairs={{0,4},{4,0},{8,12},{12,8},{16,20},{20,16},{24,28},{28,24},{1,5},{5... | collective-permute-start | bytes 491528 | tf_op jit(solution)/shard_map/ppermute | solution.py:327
  0.5 0.9 %place0.1.refs_1_ = bf16[2,2,8,5120]{3,2,1,0:T(8,128)(2,1)S(1)} custom-call(bf16[2,8,5120]{2,1,0:T(8,128)(2,1)} %bitcast.10), custom_call_target="tpu_custom_call" | custom-call | flops 10000000000 | bytes 700000 | tf_op jit(solution)/shard_map/place0/pallas_call | solution.py:295
  2.0 0.0 copy-start.1
  2.0 0.0 copy-start.2
  2.1 0.0 copy-start.3
  2.1 0.0 copy-start.4
  2.1 0.0 copy-start.5
  2.1 0.0 collective-permute-done.refs_0_
  2.1 0.1 place1.1.refs_2_
  2.2 3.5 %collective-permute-start.3 = (bf16[2,2,8,5120]{3,2,1,0:T(8,128)(2,1)S(1)}, bf16[2,2,8,5120]{3,2,1,0:T(8,128)(2,1)S(1)}, u32[]{:S(2)}, u32[]{:S(2)}) collective-permute-start(bf16[2,2,8,5120]{3,2,1,0:T(8,128)(2,1)S(1)} %place1.1.refs_2_), channel_id=1, source_target_pairs={{0,24},{4,28},{8,16},{12,20},{16,8},{20,12},{24,0},{28,4},{1,25},{... | collective-permute-start | bytes 983048 | tf_op jit(solution)/shard_map/ppermute | solution.py:334
  5.7 0.5 %collective-permute-start.2 = (bf16[2,2,8,5120]{3,2,1,0:T(8,128)(2,1)S(1)}, bf16[2,2,8,5120]{3,2,1,0:T(8,128)(2,1)S(1)}, u32[]{:S(2)}, u32[]{:S(2)}) collective-permute-start(bf16[2,2,8,5120]{3,2,1,0:T(8,128)(2,1)S(1)} %place1.1.refs_2_), channel_id=1, source_target_pairs={{0,16},{4,20},{8,24},{12,28},{16,0},{20,4},{24,8},{28,12},{1,17},{... | collective-permute-start | bytes 983048 | tf_op jit(solution)/shard_map/ppermute | solution.py:334
  6.2 0.1 collective-permute-start.1
  6.4 0.0 copy-start
  6.4 23.8 %features.1.refs_1_ = bf16[2,16,5120]{2,1,0:T(8,128)(2,1)S(1)} custom-call(s32[1]{0:T(128)S(6)} %copy.11.seed_ref, s32[16]{0:T(128)S(1)} %copy-done.5, s32[8,16]{1,0:T(8,128)S(1)} %bitcast.8, bf16[2,128,128]{2,1,0:T(8,128)(2,1)S(1)} %bitcast.7, bf16[2,128,8192]{2,1,0:T(8,128)(2,1)S(1)} %bitcast.5, bf16[2,8192,128]{2,1,0:T(8,128)(2,1)S(1)} %bitcast.6), custom_call_target="tpu_custom_call" | custom-call | flops 40000000000 | bytes 9000000 | tf_op jit(solution)/shard_map/features/pallas_call | solution.py:194
  30.2 0.0 collective-permute-done.3.refs_5_
  30.2 0.0 collective-permute-done.2.refs_4_
  30.3 1.1 %scores.1 = (f32[2,4,128]{2,1,0:T(4,128)S(1)}, f32[2,4,128]{2,1,0:T(4,128)S(1)}, f32[2,4,128]{2,1,0:T(4,128)S(1)}, f32[2,4,128]{2,1,0:T(4,128)S(1)}) custom-call(f32[2]{0:T(128)S(1)} %copy-done, bf16[2,16,5120]{2,1,0:T(8,128)(2,1)S(1)} %features.1.refs_1_, bf16[2,2,8,5120]{3,2,1,0:T(8,128)(2,1)S(1)} %place1.1.refs_2_, ...), custom_call_target="tpu_custom_call" | custom-call | tf_op jit(solution)/shard_map/scores/pallas_call | solution.py:254
  31.4 2.0 %collective-permute-start.4 = (f32[2,4,128]{2,1,0:T(4,128)S(1)}, f32[2,4,128]{2,1,0:T(4,128)S(1)}, u32[]{:S(2)}, u32[]{:S(2)}) collective-permute-start(f32[2,4,128]{2,1,0:T(4,128)S(1)} %get-tuple-element.10), channel_id=1, source_target_pairs={{0,1},{1,2},{2,3},{3,0},{4,5},{5,6},{6,7},{7,4},{8,9},{9,10},{10,1... | collective-permute-start | bytes 12296 | tf_op jit(solution)/shard_map/ppermute | solution.py:347
  33.4 2.6 %collective-permute-start.5 = (f32[2,4,128]{2,1,0:T(4,128)S(1)}, f32[2,4,128]{2,1,0:T(4,128)S(1)}, u32[]{:S(2)}, u32[]{:S(2)}) collective-permute-start(f32[2,4,128]{2,1,0:T(4,128)S(1)} %get-tuple-element.11), channel_id=1, source_target_pairs={{0,2},{1,3},{2,0},{3,1},{4,6},{5,7},{6,4},{7,5},{8,10},{9,11},{10,... | collective-permute-start | bytes 12296 | tf_op jit(solution)/shard_map/ppermute | solution.py:347
  36.0 1.4 %collective-permute-start.6 = (f32[2,4,128]{2,1,0:T(4,128)S(1)}, f32[2,4,128]{2,1,0:T(4,128)S(1)}, u32[]{:S(2)}, u32[]{:S(2)}) collective-permute-start(f32[2,4,128]{2,1,0:T(4,128)S(1)} %get-tuple-element.12), channel_id=1, source_target_pairs={{0,3},{1,0},{2,1},{3,2},{4,7},{5,4},{6,5},{7,6},{8,11},{9,8},{10,9... | collective-permute-start | bytes 12296 | tf_op jit(solution)/shard_map/ppermute | solution.py:347
  37.3 0.0 collective-permute-done.4.refs_1_
  37.4 0.6 %collective-permute-done.5.refs_2_ = f32[2,4,128]{2,1,0:T(4,128)S(1)} collective-permute-done((f32[2,4,128]{2,1,0:T(4,128)S(1)}, f32[2,4,128]{2,1,0:T(4,128)S(1)}, u32[]{:S(2)}, u32[]{:S(2)}) %collective-permute-start.5) | collective-permute-done | bytes 4128 | tf_op jit(solution)/shard_map/ppermute | solution.py:347
  37.9 1.7 %collective-permute-done.6.refs_3_ = f32[2,4,128]{2,1,0:T(4,128)S(1)} collective-permute-done((f32[2,4,128]{2,1,0:T(4,128)S(1)}, f32[2,4,128]{2,1,0:T(4,128)S(1)}, u32[]{:S(2)}, u32[]{:S(2)}) %collective-permute-start.6) | collective-permute-done | bytes 4128 | tf_op jit(solution)/shard_map/ppermute | solution.py:347
  39.6 0.7 %finish.1 = f32[4,64]{1,0:T(4,128)} custom-call(f32[2,4,128]{2,1,0:T(4,128)S(1)} %get-tuple-element.9.refs_0_, f32[2,4,128]{2,1,0:T(4,128)S(1)} %collective-permute-done.4.refs_1_, f32[2,4,128]{2,1,0:T(4,128)S(1)} %collective-permute-done.5.refs_2_, f32[2,4,128]{2,1,0:T(4,128)S(1)} %collective-permute-done.6.refs_3_), custom_call_target="tpu_custom_call" | custom-call | tf_op jit(solution)/shard_map/finish/pallas_call | solution.py:349
  (7 shorter events, 0.0 us)
Async XLA Ops:
  0.0 2.1 %collective-permute-start = (bf16[2,8,5120]{2,1,0:T(8,128)(2,1)}, bf16[2,8,5120]{2,1,0:T(8,128)(2,1)S(1)}, u32[]{:S(2)}, u32[]{:S(2)}) collective-permute-start(bf16[2,8,5120]{2,1,0:T(8,128)(2,1)} %bitcast.9), channel_id=1, source_target_pairs={{0,4},{4,0},{8,12},{12,8},{16,20},{20,16},{24,28},{28,24},{1,5},{5... | collective-permute-start | bytes 491528 | tf_op jit(solution)/shard_map/ppermute | solution.py:327
  2.0 4.4 %copy-start.1 = (bf16[2,1,16,8,8192]{4,3,2,1,0:T(8,128)(2,1)S(1)}, bf16[2,1,16,8,8192]{4,3,2,1,0:T(8,128)(2,1)}, u32[]{:S(2)}) copy-start(bf16[2,1,16,8,8192]{4,3,2,1,0:T(8,128)(2,1)} %param.8) | copy-start | bytes 12582916
  2.0 4.3 %copy-start.2 = (bf16[2,1,8192,128]{3,2,1,0:T(8,128)(2,1)S(1)}, bf16[2,1,8192,128]{3,2,1,0:T(8,128)(2,1)}, u32[]{:S(2)}) copy-start(bf16[2,1,8192,128]{3,2,1,0:T(8,128)(2,1)} %param.10) | copy-start | bytes 12582916
  2.1 4.3 %copy-start.3 = (bf16[2,1,16,8,128]{4,3,2,1,0:T(8,128)(2,1)S(1)}, bf16[2,1,16,8,128]{4,3,2,1,0:T(8,128)(2,1)}, u32[]{:S(2)}) copy-start(bf16[2,1,16,8,128]{4,3,2,1,0:T(8,128)(2,1)} %param.9) | copy-start | bytes 196612
  2.1 4.3 %copy-start.4 = (s32[16,8]{0,1:T(8,128)S(1)}, s32[16,8]{0,1:T(8,128)}, u32[]{:S(2)}) copy-start(s32[16,8]{0,1:T(8,128)} %param.13) | copy-start | bytes 1540
  2.1 4.3 %copy-start.5 = (s32[16]{0:T(128)S(1)}, s32[16]{0:T(128)}, u32[]{:S(2)}) copy-start(s32[16]{0:T(128)} %len_ref.1) | copy-start | bytes 196
  2.2 28.0 %collective-permute-start.3 = (bf16[2,2,8,5120]{3,2,1,0:T(8,128)(2,1)S(1)}, bf16[2,2,8,5120]{3,2,1,0:T(8,128)(2,1)S(1)}, u32[]{:S(2)}, u32[]{:S(2)}) collective-permute-start(bf16[2,2,8,5120]{3,2,1,0:T(8,128)(2,1)S(1)} %place1.1.refs_2_), channel_id=1, source_target_pairs={{0,24},{4,28},{8,16},{12,20},{16,8},{20,12},{24,0},{28,4},{1,25},{... | collective-permute-start | bytes 983048 | tf_op jit(solution)/shard_map/ppermute | solution.py:334
  5.7 24.5 %collective-permute-start.2 = (bf16[2,2,8,5120]{3,2,1,0:T(8,128)(2,1)S(1)}, bf16[2,2,8,5120]{3,2,1,0:T(8,128)(2,1)S(1)}, u32[]{:S(2)}, u32[]{:S(2)}) collective-permute-start(bf16[2,2,8,5120]{3,2,1,0:T(8,128)(2,1)S(1)} %place1.1.refs_2_), channel_id=1, source_target_pairs={{0,16},{4,20},{8,24},{12,28},{16,0},{20,4},{24,8},{28,12},{1,17},{... | collective-permute-start | bytes 983048 | tf_op jit(solution)/shard_map/ppermute | solution.py:334
  6.2 24.0 %collective-permute-start.1 = (bf16[2,2,8,5120]{3,2,1,0:T(8,128)(2,1)S(1)}, bf16[2,2,8,5120]{3,2,1,0:T(8,128)(2,1)S(1)}, u32[]{:S(2)}, u32[]{:S(2)}) collective-permute-start(bf16[2,2,8,5120]{3,2,1,0:T(8,128)(2,1)S(1)} %place1.1.refs_2_), channel_id=1, source_target_pairs={{0,8},{4,12},{8,0},{12,4},{16,24},{20,28},{24,16},{28,20},{1,9},{5... | collective-permute-start | bytes 983048 | tf_op jit(solution)/shard_map/ppermute | solution.py:334
  6.4 23.9 %copy-start = (f32[2]{0:T(128)S(1)}, f32[2]{0:T(128)}, u32[]{:S(2)}) copy-start(f32[2]{0:T(128)} %refs_0_.1) | copy-start | bytes 28
  31.4 6.0 %collective-permute-start.4 = (f32[2,4,128]{2,1,0:T(4,128)S(1)}, f32[2,4,128]{2,1,0:T(4,128)S(1)}, u32[]{:S(2)}, u32[]{:S(2)}) collective-permute-start(f32[2,4,128]{2,1,0:T(4,128)S(1)} %get-tuple-element.10), channel_id=1, source_target_pairs={{0,1},{1,2},{2,3},{3,0},{4,5},{5,6},{6,7},{7,4},{8,9},{9,10},{10,1... | collective-permute-start | bytes 12296 | tf_op jit(solution)/shard_map/ppermute | solution.py:347
  33.4 4.5 %collective-permute-start.5 = (f32[2,4,128]{2,1,0:T(4,128)S(1)}, f32[2,4,128]{2,1,0:T(4,128)S(1)}, u32[]{:S(2)}, u32[]{:S(2)}) collective-permute-start(f32[2,4,128]{2,1,0:T(4,128)S(1)} %get-tuple-element.11), channel_id=1, source_target_pairs={{0,2},{1,3},{2,0},{3,1},{4,6},{5,7},{6,4},{7,5},{8,10},{9,11},{10,... | collective-permute-start | bytes 12296 | tf_op jit(solution)/shard_map/ppermute | solution.py:347
  36.0 3.6 %collective-permute-start.6 = (f32[2,4,128]{2,1,0:T(4,128)S(1)}, f32[2,4,128]{2,1,0:T(4,128)S(1)}, u32[]{:S(2)}, u32[]{:S(2)}) collective-permute-start(f32[2,4,128]{2,1,0:T(4,128)S(1)} %get-tuple-element.12), channel_id=1, source_target_pairs={{0,3},{1,0},{2,1},{3,2},{4,7},{5,4},{6,5},{7,6},{8,11},{9,8},{10,9... | collective-permute-start | bytes 12296 | tf_op jit(solution)/shard_map/ppermute | solution.py:347

commit v8 on v7

--- a/solution.py
+++ b/solution.py
@@ -56,12 +56,10 @@
     hash_base = (
         lax.axis_index("layer") * jnp.int32(668265263) + seed_ref[0] * jnp.int32(374761393)
     )
-    slot_ids = lax.broadcasted_iota(jnp.int32, (slots, 1), 0)
+    slot_ids = lax.broadcasted_iota(jnp.int32, (slots, examples), 0)
+    valid = jnp.where((mask_ref[...] == 1) & (slot_ids < len_ref[...]), 1.0, 0.0)
     for pair in range(pairs):
-        marks = [
-            (mask_ref[:, e : e + 1] == 1) & (slot_ids < len_ref[e])
-            for e in (2 * pair, 2 * pair + 1)
-        ]
+        marks = [valid[:, e : e + 1] > 0.5 for e in (2 * pair, 2 * pair + 1)]
         for c in range(ckpts):
             at = 2 * pair * slots
             first = jnp.where(marks[0], act_ref[c, at : at + slots, :].astype(F32), 0.0)
@@ -194,7 +192,7 @@
     return pl.pallas_call(
         kernel,
         out_shape=jax.ShapeDtypeStruct((ckpts, examples, cols * LANES), BF16),
-        in_specs=[smem, smem] + [vmem] * 4,
+        in_specs=[smem] + [vmem] * 5,
         out_specs=vmem,
         scratch_shapes=[
             pltpu.VMEM((chunk, LANES), BF16),
@@ -237,7 +235,7 @@
                 ]
         wide = feat.astype(F32)
         norm = jnp.sum(wide * wide, axis=1, keepdims=True)
-        sums[c, :, :held] = jnp.transpose(turned[c]) * weight_ref[c]
+        sums[c, :, :held] = jnp.transpose(turned[c]) * weight_ref[:, c : c + 1]
         sums[c, :, held:] = jnp.broadcast_to(norm, (examples, sums.shape[2] - held))
         for step in range(parts):
             owner = lax.rem(me + step, parts)
@@ -254,7 +252,7 @@
     return pl.pallas_call(
         functools.partial(score_kernel, groups=groups, parts=parts),
         out_shape=[jax.ShapeDtypeStruct((ckpts, examples // parts, lanes), F32)] * parts,
-        in_specs=[pl.BlockSpec(memory_space=pltpu.SMEM)] + [vmem] * (1 + groups),
+        in_specs=[vmem] * (2 + groups),
         out_specs=[vmem] * parts,
         scratch_shapes=[
             pltpu.VMEM((ckpts, held, examples), F32),
@@ -334,14 +332,14 @@
             holds.append(lax.ppermute(own, "dp", ring))
         feat = features_of(
             seed,
-            lengths,
+            lengths[None, :],
             mask.T,
             act.reshape(ckpts, examples * slots, rank),
             grad.reshape(ckpts, examples * slots, width),
             var[:, 0],
             cols,
         )
-        pieces = list(scores_of(weight, feat, holds, parts))
+        pieces = list(scores_of(weight[None, :], feat, holds, parts))
         for step in range(1, parts):
             ring = [(i, (i + step) % parts) for i in range(parts)]
             pieces[step] = lax.ppermute(pieces[step], "layer", ring)

time: 40.4 us -> 39.4 us (0.975)
  Pallas kernels: 26.6 us -> 25.5 us
    pallas_call x1, Pallas kernels: 1.1 us -> 0.56 us  [scores_of(): pl.pallas_call(functools.partial(score_kernel, groups=groups, parts=parts...]
    pallas_call x1, Pallas kernels: 23.8 us -> 23.3 us  [features_of(): pl.pallas_call(kernel, out_shape=jax.ShapeDtypeStruct((ckpts, examples, c...]
  transfers between devices with their start and end apart: 7 -> 7, of which waited for: 2 -> 2; matrix products, arithmetic and copies ran while one was open for 0% -> 0% of each run, Pallas kernels for 61% -> 62%
where the time goes in v8:
time: 39.4 us; the launch traced here: 39.2 us
  Pallas kernels  25.5 us (65%)
  starting transfers between devices  10.6 us (27%)
  waiting for transfers between devices  2.27 us (6%)
  between operations  0.78 us (2%)
    pallas_call x1, Pallas kernels, features_of(): pl.pallas_call(kernel, out_shape=jax.ShapeDtypeStruct((ckpts, examples, c...  23.3 us
    ppermute x3, starting transfers between devices, local(): pieces[step] = lax.ppermute(pieces[step], 'layer', ring)  5.96 us
    ppermute x3, starting transfers between devices, local(): holds.append(lax.ppermute(own, 'dp', ring))  4.15 us
    ppermute x3, waiting for transfers between devices, local(): pieces[step] = lax.ppermute(pieces[step], 'layer', ring)  2.26 us
    pallas_call x2, Pallas kernels, together(): pl.pallas_call(functools.partial(place_kernel, turn=turn), out_shape=jax....  1.04 us
  transfers between devices with their start and end apart: 7, of which 2 were waited for; matrix products, arithmetic and copies ran while one was open for 0% of the time, Pallas kernels for 62%

profile of v8, /device:TPU:0, one launch (start us, length us, event | category | flops | bytes accessed | tf_op | source)
XLA Modules:
  0.0 39.2 jit_solution(10263097479148623468)
XLA Ops:
  0.0 0.5 %collective-permute-start = (bf16[2,8,5120]{2,1,0:T(8,128)(2,1)}, bf16[2,8,5120]{2,1,0:T(8,128)(2,1)S(1)}, u32[]{:S(2)}, u32[]{:S(2)}) collective-permute-start(bf16[2,8,5120]{2,1,0:T(8,128)(2,1)} %bitcast.13), channel_id=1, source_target_pairs={{0,4},{4,0},{8,12},{12,8},{16,20},{20,16},{24,28},{28,24},{1,5},{5... | collective-permute-start | bytes 491528 | tf_op jit(solution)/shard_map/ppermute | solution.py:325
  0.5 0.9 %place0.1.refs_1_ = bf16[2,2,8,5120]{3,2,1,0:T(8,128)(2,1)S(1)} custom-call(bf16[2,8,5120]{2,1,0:T(8,128)(2,1)} %bitcast.14), custom_call_target="tpu_custom_call" | custom-call | flops 10000000000 | bytes 700000 | tf_op jit(solution)/shard_map/place0/pallas_call | solution.py:293
  2.0 0.0 copy-start.1
  2.0 0.0 copy-start.2
  2.1 0.0 copy-start.3
  2.1 0.0 copy-start.4
  2.1 0.0 copy-start.5
  2.1 0.0 collective-permute-done.refs_0_
  2.1 0.1 place1.1.refs_2_
  2.2 3.5 %collective-permute-start.3 = (bf16[2,2,8,5120]{3,2,1,0:T(8,128)(2,1)S(1)}, bf16[2,2,8,5120]{3,2,1,0:T(8,128)(2,1)S(1)}, u32[]{:S(2)}, u32[]{:S(2)}) collective-permute-start(bf16[2,2,8,5120]{3,2,1,0:T(8,128)(2,1)S(1)} %place1.1.refs_2_), channel_id=1, source_target_pairs={{0,24},{4,28},{8,16},{12,20},{16,8},{20,12},{24,0},{28,4},{1,25},{... | collective-permute-start | bytes 983048 | tf_op jit(solution)/shard_map/ppermute | solution.py:332
  5.7 0.5 %collective-permute-start.2 = (bf16[2,2,8,5120]{3,2,1,0:T(8,128)(2,1)S(1)}, bf16[2,2,8,5120]{3,2,1,0:T(8,128)(2,1)S(1)}, u32[]{:S(2)}, u32[]{:S(2)}) collective-permute-start(bf16[2,2,8,5120]{3,2,1,0:T(8,128)(2,1)S(1)} %place1.1.refs_2_), channel_id=1, source_target_pairs={{0,16},{4,20},{8,24},{12,28},{16,0},{20,4},{24,8},{28,12},{1,17},{... | collective-permute-start | bytes 983048 | tf_op jit(solution)/shard_map/ppermute | solution.py:332
  6.2 0.1 collective-permute-start.1
  6.4 0.0 copy-start
  6.4 23.3 %features.1.refs_1_ = bf16[2,16,5120]{2,1,0:T(8,128)(2,1)S(1)} custom-call(s32[1]{0:T(128)S(6)} %copy.11.seed_ref, s32[1,16]{1,0:T(1,128)S(1)} %bitcast.12, s32[8,16]{1,0:T(8,128)S(1)} %bitcast.11, bf16[2,128,128]{2,1,0:T(8,128)(2,1)S(1)} %bitcast.10, bf16[2,128,8192]{2,1,0:T(8,128)(2,1)S(1)} %bitcast.8, bf16[2,8192,128]{2,1,0:T(8,128)(2,1)S(1)} %bitcast.9), custom_call_target="tpu_custom_call" | custom-call | flops 40000000000 | bytes 9000000 | tf_op jit(solution)/shard_map/features/pallas_call | solution.py:192
  29.7 0.0 collective-permute-done.2.refs_4_
  29.7 0.0 collective-permute-done.1.refs_3_
  29.8 0.6 %scores.1 = (f32[2,4,128]{2,1,0:T(4,128)S(1)}, f32[2,4,128]{2,1,0:T(4,128)S(1)}, f32[2,4,128]{2,1,0:T(4,128)S(1)}, f32[2,4,128]{2,1,0:T(4,128)S(1)}) custom-call(f32[1,2]{1,0:T(1,128)S(1)} %bitcast.7, bf16[2,16,5120]{2,1,0:T(8,128)(2,1)S(1)} %features.1.refs_1_, bf16[2,2,8,5120]{3,2,1,0:T(8,128)(2,1)S(1)} %place1.1.refs_2_, ...), custom_call_target="tpu_custom_call" | custom-call | tf_op jit(solution)/shard_map/scores/pallas_call | solution.py:252
  30.3 2.0 %collective-permute-start.4 = (f32[2,4,128]{2,1,0:T(4,128)S(1)}, f32[2,4,128]{2,1,0:T(4,128)S(1)}, u32[]{:S(2)}, u32[]{:S(2)}) collective-permute-start(f32[2,4,128]{2,1,0:T(4,128)S(1)} %get-tuple-element.10), channel_id=1, source_target_pairs={{0,1},{1,2},{2,3},{3,0},{4,5},{5,6},{6,7},{7,4},{8,9},{9,10},{10,1... | collective-permute-start | bytes 12296 | tf_op jit(solution)/shard_map/ppermute | solution.py:345
  32.3 2.6 %collective-permute-start.5 = (f32[2,4,128]{2,1,0:T(4,128)S(1)}, f32[2,4,128]{2,1,0:T(4,128)S(1)}, u32[]{:S(2)}, u32[]{:S(2)}) collective-permute-start(f32[2,4,128]{2,1,0:T(4,128)S(1)} %get-tuple-element.11), channel_id=1, source_target_pairs={{0,2},{1,3},{2,0},{3,1},{4,6},{5,7},{6,4},{7,5},{8,10},{9,11},{10,... | collective-permute-start | bytes 12296 | tf_op jit(solution)/shard_map/ppermute | solution.py:345
  34.9 1.3 %collective-permute-start.6 = (f32[2,4,128]{2,1,0:T(4,128)S(1)}, f32[2,4,128]{2,1,0:T(4,128)S(1)}, u32[]{:S(2)}, u32[]{:S(2)}) collective-permute-start(f32[2,4,128]{2,1,0:T(4,128)S(1)} %get-tuple-element.12), channel_id=1, source_target_pairs={{0,3},{1,0},{2,1},{3,2},{4,7},{5,4},{6,5},{7,6},{8,11},{9,8},{10,9... | collective-permute-start | bytes 12296 | tf_op jit(solution)/shard_map/ppermute | solution.py:345
  36.3 0.0 collective-permute-done.4.refs_1_
  36.3 0.6 %collective-permute-done.5.refs_2_ = f32[2,4,128]{2,1,0:T(4,128)S(1)} collective-permute-done((f32[2,4,128]{2,1,0:T(4,128)S(1)}, f32[2,4,128]{2,1,0:T(4,128)S(1)}, u32[]{:S(2)}, u32[]{:S(2)}) %collective-permute-start.5) | collective-permute-done | bytes 4128 | tf_op jit(solution)/shard_map/ppermute | solution.py:345
  36.9 1.7 %collective-permute-done.6.refs_3_ = f32[2,4,128]{2,1,0:T(4,128)S(1)} collective-permute-done((f32[2,4,128]{2,1,0:T(4,128)S(1)}, f32[2,4,128]{2,1,0:T(4,128)S(1)}, u32[]{:S(2)}, u32[]{:S(2)}) %collective-permute-start.6) | collective-permute-done | bytes 4128 | tf_op jit(solution)/shard_map/ppermute | solution.py:345
  38.5 0.7 %finish.1 = f32[4,64]{1,0:T(4,128)} custom-call(f32[2,4,128]{2,1,0:T(4,128)S(1)} %get-tuple-element.9.refs_0_, f32[2,4,128]{2,1,0:T(4,128)S(1)} %collective-permute-done.4.refs_1_, f32[2,4,128]{2,1,0:T(4,128)S(1)} %collective-permute-done.5.refs_2_, f32[2,4,128]{2,1,0:T(4,128)S(1)} %collective-permute-done.6.refs_3_), custom_call_target="tpu_custom_call" | custom-call | tf_op jit(solution)/shard_map/finish/pallas_call | solution.py:347
  (7 shorter events, 0.0 us)
Async XLA Ops:
  0.0 2.1 %collective-permute-start = (bf16[2,8,5120]{2,1,0:T(8,128)(2,1)}, bf16[2,8,5120]{2,1,0:T(8,128)(2,1)S(1)}, u32[]{:S(2)}, u32[]{:S(2)}) collective-permute-start(bf16[2,8,5120]{2,1,0:T(8,128)(2,1)} %bitcast.13), channel_id=1, source_target_pairs={{0,4},{4,0},{8,12},{12,8},{16,20},{20,16},{24,28},{28,24},{1,5},{5... | collective-permute-start | bytes 491528 | tf_op jit(solution)/shard_map/ppermute | solution.py:325
  2.0 4.4 %copy-start.1 = (bf16[2,1,16,8,8192]{4,3,2,1,0:T(8,128)(2,1)S(1)}, bf16[2,1,16,8,8192]{4,3,2,1,0:T(8,128)(2,1)}, u32[]{:S(2)}) copy-start(bf16[2,1,16,8,8192]{4,3,2,1,0:T(8,128)(2,1)} %param.8) | copy-start | bytes 12582916
  2.0 4.3 %copy-start.2 = (bf16[2,1,8192,128]{3,2,1,0:T(8,128)(2,1)S(1)}, bf16[2,1,8192,128]{3,2,1,0:T(8,128)(2,1)}, u32[]{:S(2)}) copy-start(bf16[2,1,8192,128]{3,2,1,0:T(8,128)(2,1)} %param.10) | copy-start | bytes 12582916
  2.1 4.3 %copy-start.3 = (bf16[2,1,16,8,128]{4,3,2,1,0:T(8,128)(2,1)S(1)}, bf16[2,1,16,8,128]{4,3,2,1,0:T(8,128)(2,1)}, u32[]{:S(2)}) copy-start(bf16[2,1,16,8,128]{4,3,2,1,0:T(8,128)(2,1)} %param.9) | copy-start | bytes 196612
  2.1 4.3 %copy-start.4 = (s32[16,8]{0,1:T(8,128)S(1)}, s32[16,8]{0,1:T(8,128)}, u32[]{:S(2)}) copy-start(s32[16,8]{0,1:T(8,128)} %param.13) | copy-start | bytes 1540
  2.1 4.3 %copy-start.5 = (s32[16]{0:T(128)S(1)}, s32[16]{0:T(128)}, u32[]{:S(2)}) copy-start(s32[16]{0:T(128)} %param.12) | copy-start | bytes 196
  2.2 27.5 %collective-permute-start.3 = (bf16[2,2,8,5120]{3,2,1,0:T(8,128)(2,1)S(1)}, bf16[2,2,8,5120]{3,2,1,0:T(8,128)(2,1)S(1)}, u32[]{:S(2)}, u32[]{:S(2)}) collective-permute-start(bf16[2,2,8,5120]{3,2,1,0:T(8,128)(2,1)S(1)} %place1.1.refs_2_), channel_id=1, source_target_pairs={{0,24},{4,28},{8,16},{12,20},{16,8},{20,12},{24,0},{28,4},{1,25},{... | collective-permute-start | bytes 983048 | tf_op jit(solution)/shard_map/ppermute | solution.py:332
  5.7 24.0 %collective-permute-start.2 = (bf16[2,2,8,5120]{3,2,1,0:T(8,128)(2,1)S(1)}, bf16[2,2,8,5120]{3,2,1,0:T(8,128)(2,1)S(1)}, u32[]{:S(2)}, u32[]{:S(2)}) collective-permute-start(bf16[2,2,8,5120]{3,2,1,0:T(8,128)(2,1)S(1)} %place1.1.refs_2_), channel_id=1, source_target_pairs={{0,16},{4,20},{8,24},{12,28},{16,0},{20,4},{24,8},{28,12},{1,17},{... | collective-permute-start | bytes 983048 | tf_op jit(solution)/shard_map/ppermute | solution.py:332
  6.2 23.5 %collective-permute-start.1 = (bf16[2,2,8,5120]{3,2,1,0:T(8,128)(2,1)S(1)}, bf16[2,2,8,5120]{3,2,1,0:T(8,128)(2,1)S(1)}, u32[]{:S(2)}, u32[]{:S(2)}) collective-permute-start(bf16[2,2,8,5120]{3,2,1,0:T(8,128)(2,1)S(1)} %place1.1.refs_2_), channel_id=1, source_target_pairs={{0,8},{4,12},{8,0},{12,4},{16,24},{20,28},{24,16},{28,20},{1,9},{5... | collective-permute-start | bytes 983048 | tf_op jit(solution)/shard_map/ppermute | solution.py:332
  6.4 23.3 %copy-start = (f32[2]{0:T(128)S(1)}, f32[2]{0:T(128)}, u32[]{:S(2)}) copy-start(f32[2]{0:T(128)} %param.15) | copy-start | bytes 28
  30.3 6.0 %collective-permute-start.4 = (f32[2,4,128]{2,1,0:T(4,128)S(1)}, f32[2,4,128]{2,1,0:T(4,128)S(1)}, u32[]{:S(2)}, u32[]{:S(2)}) collective-permute-start(f32[2,4,128]{2,1,0:T(4,128)S(1)} %get-tuple-element.10), channel_id=1, source_target_pairs={{0,1},{1,2},{2,3},{3,0},{4,5},{5,6},{6,7},{7,4},{8,9},{9,10},{10,1... | collective-permute-start | bytes 12296 | tf_op jit(solution)/shard_map/ppermute | solution.py:345
  32.3 4.5 %collective-permute-start.5 = (f32[2,4,128]{2,1,0:T(4,128)S(1)}, f32[2,4,128]{2,1,0:T(4,128)S(1)}, u32[]{:S(2)}, u32[]{:S(2)}) collective-permute-start(f32[2,4,128]{2,1,0:T(4,128)S(1)} %get-tuple-element.11), channel_id=1, source_target_pairs={{0,2},{1,3},{2,0},{3,1},{4,6},{5,7},{6,4},{7,5},{8,10},{9,11},{10,... | collective-permute-start | bytes 12296 | tf_op jit(solution)/shard_map/ppermute | solution.py:345
  34.9 3.6 %collective-permute-start.6 = (f32[2,4,128]{2,1,0:T(4,128)S(1)}, f32[2,4,128]{2,1,0:T(4,128)S(1)}, u32[]{:S(2)}, u32[]{:S(2)}) collective-permute-start(f32[2,4,128]{2,1,0:T(4,128)S(1)} %get-tuple-element.12), channel_id=1, source_target_pairs={{0,3},{1,0},{2,1},{3,2},{4,7},{5,4},{6,5},{7,6},{8,11},{9,8},{10,9... | collective-permute-start | bytes 12296 | tf_op jit(solution)/shard_map/ppermute | solution.py:345

commit v9 on v8

--- a/solution.py
+++ b/solution.py
@@ -13,7 +13,7 @@
 TILE = 256
 LANES = 128
 AHEAD = 2
-READY = 2
+READY = 1
 
 
 def target(index, step, size):
@@ -287,8 +287,6 @@
     anywhere = pl.BlockSpec(memory_space=pl.ANY)
     joined = ()
     for turn, block in enumerate(blocks):
-        if turn == 0:
-            block = pltpu.with_memory_space_constraint(block, pltpu.HBM)
         joined = (
             pl.pallas_call(
                 functools.partial(place_kernel, turn=turn),

time: 39.4 us -> 39.3 us (level)
  local copies, waits for them, and re-layouts: 0.04 us -> 0.95 us
  Pallas kernels: 25.5 us -> 24.6 us
    unnamed x12 -> x14, local copies, waits for them, and re-layouts: 0.04 us -> 0.95 us
    pallas_call x2, Pallas kernels: 1.04 us -> 0.21 us  [together(): pl.pallas_call(functools.partial(place_kernel, turn=turn), out_shape=jax....]
  transfers between devices with their start and end apart: 7 -> 7, of which waited for: 2 -> 2; matrix products, arithmetic and copies ran while one was open for 0% -> 0% of each run, Pallas kernels for 62% -> 59%
where the time goes in v9:
time: 39.3 us; the launch traced here: 39.2 us
  Pallas kernels  24.6 us (63%)
  starting transfers between devices  10.6 us (27%)
  waiting for transfers between devices  2.27 us (6%)
  local copies, waits for them, and re-layouts  0.95 us (2%)
  between operations  0.79 us (2%)
    pallas_call x1, Pallas kernels, features_of(): pl.pallas_call(kernel, out_shape=jax.ShapeDtypeStruct((ckpts, examples, c...  23.1 us
    ppermute x3, starting transfers between devices, local(): pieces[step] = lax.ppermute(pieces[step], 'layer', ring)  5.96 us
    ppermute x3, starting transfers between devices, local(): holds.append(lax.ppermute(own, 'dp', ring))  4.15 us
    ppermute x3, waiting for transfers between devices, local(): pieces[step] = lax.ppermute(pieces[step], 'layer', ring)  2.26 us
    unnamed x14, local copies, waits for them, and re-layouts  0.95 us
  transfers between devices with their start and end apart: 7, of which 2 were waited for; matrix products, arithmetic and copies ran while one was open for 0% of the time, Pallas kernels for 59%

profile of v9, /device:TPU:0, one launch (start us, length us, event | category | flops | bytes accessed | tf_op | source)
XLA Modules:
  0.0 39.2 jit_solution(6531214901914427140)
XLA Ops:
  0.0 0.5 %collective-permute-start = (bf16[2,8,5120]{2,1,0:T(8,128)(2,1)}, bf16[2,8,5120]{2,1,0:T(8,128)(2,1)S(1)}, u32[]{:S(2)}, u32[]{:S(2)}) collective-permute-start(bf16[2,8,5120]{2,1,0:T(8,128)(2,1)} %bitcast.10), channel_id=1, source_target_pairs={{0,4},{4,0},{8,12},{12,8},{16,20},{20,16},{24,28},{28,24},{1,5},{5... | collective-permute-start | bytes 491528 | tf_op jit(solution)/shard_map/ppermute | solution.py:323
  0.5 0.9 %copy-done.3 = bf16[2,1,8,5120]{3,2,1,0:T(8,128)(2,1)S(1)} copy-done((bf16[2,1,8,5120]{3,2,1,0:T(8,128)(2,1)S(1)}, bf16[2,1,8,5120]{3,2,1,0:T(8,128)(2,1)}, u32[]{:S(2)}) %copy-start.3) | copy-done | bytes 163864
  1.4 0.1 place0.1.refs_1_
  2.1 0.0 copy-start.1
  2.1 0.0 copy-start.2
  2.1 0.0 copy-start.4
  2.2 0.0 copy-start.5
  2.2 0.0 copy-start.6
  2.2 0.0 collective-permute-done.refs_0_
  2.2 0.1 place1.1.refs_2_
  2.3 3.5 %collective-permute-start.3 = (bf16[2,2,8,5120]{3,2,1,0:T(8,128)(2,1)S(1)}, bf16[2,2,8,5120]{3,2,1,0:T(8,128)(2,1)S(1)}, u32[]{:S(2)}, u32[]{:S(2)}) collective-permute-start(bf16[2,2,8,5120]{3,2,1,0:T(8,128)(2,1)S(1)} %place1.1.refs_2_), channel_id=1, source_target_pairs={{0,24},{4,28},{8,16},{12,20},{16,8},{20,12},{24,0},{28,4},{1,25},{... | collective-permute-start | bytes 983048 | tf_op jit(solution)/shard_map/ppermute | solution.py:330
  5.8 0.5 %collective-permute-start.2 = (bf16[2,2,8,5120]{3,2,1,0:T(8,128)(2,1)S(1)}, bf16[2,2,8,5120]{3,2,1,0:T(8,128)(2,1)S(1)}, u32[]{:S(2)}, u32[]{:S(2)}) collective-permute-start(bf16[2,2,8,5120]{3,2,1,0:T(8,128)(2,1)S(1)} %place1.1.refs_2_), channel_id=1, source_target_pairs={{0,16},{4,20},{8,24},{12,28},{16,0},{20,4},{24,8},{28,12},{1,17},{... | collective-permute-start | bytes 983048 | tf_op jit(solution)/shard_map/ppermute | solution.py:330
  6.3 0.1 collective-permute-start.1
  6.5 0.0 copy-start
  6.5 23.1 %features.1.refs_1_ = bf16[2,16,5120]{2,1,0:T(8,128)(2,1)S(1)} custom-call(s32[1]{0:T(128)S(6)} %copy.11.seed_ref, s32[1,16]{1,0:T(1,128)S(1)} %bitcast.14, s32[8,16]{1,0:T(8,128)S(1)} %bitcast.13, bf16[2,128,128]{2,1,0:T(8,128)(2,1)S(1)} %bitcast.12, bf16[2,128,8192]{2,1,0:T(8,128)(2,1)S(1)} %bitcast.8, bf16[2,8192,128]{2,1,0:T(8,128)(2,1)S(1)} %bitcast.9), custom_call_target="tpu_custom_call" | custom-call | flops 40000000000 | bytes 9000000 | tf_op jit(solution)/shard_map/features/pallas_call | solution.py:192
  29.7 0.0 collective-permute-done.3.refs_5_
  29.7 0.0 collective-permute-done.1.refs_3_
  29.7 0.6 %scores.1 = (f32[2,4,128]{2,1,0:T(4,128)S(1)}, f32[2,4,128]{2,1,0:T(4,128)S(1)}, f32[2,4,128]{2,1,0:T(4,128)S(1)}, f32[2,4,128]{2,1,0:T(4,128)S(1)}) custom-call(f32[1,2]{1,0:T(1,128)S(1)} %bitcast.7, bf16[2,16,5120]{2,1,0:T(8,128)(2,1)S(1)} %features.1.refs_1_, bf16[2,2,8,5120]{3,2,1,0:T(8,128)(2,1)S(1)} %place1.1.refs_2_, ...), custom_call_target="tpu_custom_call" | custom-call | tf_op jit(solution)/shard_map/scores/pallas_call | solution.py:252
  30.3 2.0 %collective-permute-start.4 = (f32[2,4,128]{2,1,0:T(4,128)S(1)}, f32[2,4,128]{2,1,0:T(4,128)S(1)}, u32[]{:S(2)}, u32[]{:S(2)}) collective-permute-start(f32[2,4,128]{2,1,0:T(4,128)S(1)} %get-tuple-element.10), channel_id=1, source_target_pairs={{0,1},{1,2},{2,3},{3,0},{4,5},{5,6},{6,7},{7,4},{8,9},{9,10},{10,1... | collective-permute-start | bytes 12296 | tf_op jit(solution)/shard_map/ppermute | solution.py:343
  32.3 2.6 %collective-permute-start.5 = (f32[2,4,128]{2,1,0:T(4,128)S(1)}, f32[2,4,128]{2,1,0:T(4,128)S(1)}, u32[]{:S(2)}, u32[]{:S(2)}) collective-permute-start(f32[2,4,128]{2,1,0:T(4,128)S(1)} %get-tuple-element.11), channel_id=1, source_target_pairs={{0,2},{1,3},{2,0},{3,1},{4,6},{5,7},{6,4},{7,5},{8,10},{9,11},{10,... | collective-permute-start | bytes 12296 | tf_op jit(solution)/shard_map/ppermute | solution.py:343
  34.9 1.3 %collective-permute-start.6 = (f32[2,4,128]{2,1,0:T(4,128)S(1)}, f32[2,4,128]{2,1,0:T(4,128)S(1)}, u32[]{:S(2)}, u32[]{:S(2)}) collective-permute-start(f32[2,4,128]{2,1,0:T(4,128)S(1)} %get-tuple-element.12), channel_id=1, source_target_pairs={{0,3},{1,0},{2,1},{3,2},{4,7},{5,4},{6,5},{7,6},{8,11},{9,8},{10,9... | collective-permute-start | bytes 12296 | tf_op jit(solution)/shard_map/ppermute | solution.py:343
  36.2 0.6 %collective-permute-done.5.refs_2_ = f32[2,4,128]{2,1,0:T(4,128)S(1)} collective-permute-done((f32[2,4,128]{2,1,0:T(4,128)S(1)}, f32[2,4,128]{2,1,0:T(4,128)S(1)}, u32[]{:S(2)}, u32[]{:S(2)}) %collective-permute-start.5) | collective-permute-done | bytes 4128 | tf_op jit(solution)/shard_map/ppermute | solution.py:343
  36.8 1.7 %collective-permute-done.6.refs_3_ = f32[2,4,128]{2,1,0:T(4,128)S(1)} collective-permute-done((f32[2,4,128]{2,1,0:T(4,128)S(1)}, f32[2,4,128]{2,1,0:T(4,128)S(1)}, u32[]{:S(2)}, u32[]{:S(2)}) %collective-permute-start.6) | collective-permute-done | bytes 4128 | tf_op jit(solution)/shard_map/ppermute | solution.py:343
  38.5 0.7 %finish.1 = f32[4,64]{1,0:T(4,128)} custom-call(f32[2,4,128]{2,1,0:T(4,128)S(1)} %get-tuple-element.9.refs_0_, f32[2,4,128]{2,1,0:T(4,128)S(1)} %collective-permute-done.4.refs_1_, f32[2,4,128]{2,1,0:T(4,128)S(1)} %collective-permute-done.5.refs_2_, f32[2,4,128]{2,1,0:T(4,128)S(1)} %collective-permute-done.6.refs_3_), custom_call_target="tpu_custom_call" | custom-call | tf_op jit(solution)/shard_map/finish/pallas_call | solution.py:345
  (9 shorter events, 0.0 us)
Async XLA Ops:
  0.0 2.2 %collective-permute-start = (bf16[2,8,5120]{2,1,0:T(8,128)(2,1)}, bf16[2,8,5120]{2,1,0:T(8,128)(2,1)S(1)}, u32[]{:S(2)}, u32[]{:S(2)}) collective-permute-start(bf16[2,8,5120]{2,1,0:T(8,128)(2,1)} %bitcast.10), channel_id=1, source_target_pairs={{0,4},{4,0},{8,12},{12,8},{16,20},{20,16},{24,28},{28,24},{1,5},{5... | collective-permute-start | bytes 491528 | tf_op jit(solution)/shard_map/ppermute | solution.py:323
  0.5 0.9 %copy-start.3 = (bf16[2,1,8,5120]{3,2,1,0:T(8,128)(2,1)S(1)}, bf16[2,1,8,5120]{3,2,1,0:T(8,128)(2,1)}, u32[]{:S(2)}) copy-start(bf16[2,1,8,5120]{3,2,1,0:T(8,128)(2,1)} %param.11) | copy-start | bytes 491524
  2.1 4.4 %copy-start.1 = (bf16[2,1,16,8,8192]{4,3,2,1,0:T(8,128)(2,1)S(1)}, bf16[2,1,16,8,8192]{4,3,2,1,0:T(8,128)(2,1)}, u32[]{:S(2)}) copy-start(bf16[2,1,16,8,8192]{4,3,2,1,0:T(8,128)(2,1)} %param.8) | copy-start | bytes 12582916
  2.1 4.3 %copy-start.2 = (bf16[2,1,8192,128]{3,2,1,0:T(8,128)(2,1)S(1)}, bf16[2,1,8192,128]{3,2,1,0:T(8,128)(2,1)}, u32[]{:S(2)}) copy-start(bf16[2,1,8192,128]{3,2,1,0:T(8,128)(2,1)} %param.10) | copy-start | bytes 12582916
  2.1 4.3 %copy-start.4 = (bf16[2,1,16,8,128]{4,3,2,1,0:T(8,128)(2,1)S(1)}, bf16[2,1,16,8,128]{4,3,2,1,0:T(8,128)(2,1)}, u32[]{:S(2)}) copy-start(bf16[2,1,16,8,128]{4,3,2,1,0:T(8,128)(2,1)} %param.9) | copy-start | bytes 196612
  2.2 4.3 %copy-start.5 = (s32[16,8]{0,1:T(8,128)S(1)}, s32[16,8]{0,1:T(8,128)}, u32[]{:S(2)}) copy-start(s32[16,8]{0,1:T(8,128)} %param.13) | copy-start | bytes 1540
  2.2 4.3 %copy-start.6 = (s32[16]{0:T(128)S(1)}, s32[16]{0:T(128)}, u32[]{:S(2)}) copy-start(s32[16]{0:T(128)} %param.12) | copy-start | bytes 196
  2.3 27.3 %collective-permute-start.3 = (bf16[2,2,8,5120]{3,2,1,0:T(8,128)(2,1)S(1)}, bf16[2,2,8,5120]{3,2,1,0:T(8,128)(2,1)S(1)}, u32[]{:S(2)}, u32[]{:S(2)}) collective-permute-start(bf16[2,2,8,5120]{3,2,1,0:T(8,128)(2,1)S(1)} %place1.1.refs_2_), channel_id=1, source_target_pairs={{0,24},{4,28},{8,16},{12,20},{16,8},{20,12},{24,0},{28,4},{1,25},{... | collective-permute-start | bytes 983048 | tf_op jit(solution)/shard_map/ppermute | solution.py:330
  5.8 23.8 %collective-permute-start.2 = (bf16[2,2,8,5120]{3,2,1,0:T(8,128)(2,1)S(1)}, bf16[2,2,8,5120]{3,2,1,0:T(8,128)(2,1)S(1)}, u32[]{:S(2)}, u32[]{:S(2)}) collective-permute-start(bf16[2,2,8,5120]{3,2,1,0:T(8,128)(2,1)S(1)} %place1.1.refs_2_), channel_id=1, source_target_pairs={{0,16},{4,20},{8,24},{12,28},{16,0},{20,4},{24,8},{28,12},{1,17},{... | collective-permute-start | bytes 983048 | tf_op jit(solution)/shard_map/ppermute | solution.py:330
  6.3 23.4 %collective-permute-start.1 = (bf16[2,2,8,5120]{3,2,1,0:T(8,128)(2,1)S(1)}, bf16[2,2,8,5120]{3,2,1,0:T(8,128)(2,1)S(1)}, u32[]{:S(2)}, u32[]{:S(2)}) collective-permute-start(bf16[2,2,8,5120]{3,2,1,0:T(8,128)(2,1)S(1)} %place1.1.refs_2_), channel_id=1, source_target_pairs={{0,8},{4,12},{8,0},{12,4},{16,24},{20,28},{24,16},{28,20},{1,9},{5... | collective-permute-start | bytes 983048 | tf_op jit(solution)/shard_map/ppermute | solution.py:330
  6.5 23.2 %copy-start = (f32[2]{0:T(128)S(1)}, f32[2]{0:T(128)}, u32[]{:S(2)}) copy-start(f32[2]{0:T(128)} %param.15) | copy-start | bytes 28
  30.3 6.0 %collective-permute-start.4 = (f32[2,4,128]{2,1,0:T(4,128)S(1)}, f32[2,4,128]{2,1,0:T(4,128)S(1)}, u32[]{:S(2)}, u32[]{:S(2)}) collective-permute-start(f32[2,4,128]{2,1,0:T(4,128)S(1)} %get-tuple-element.10), channel_id=1, source_target_pairs={{0,1},{1,2},{2,3},{3,0},{4,5},{5,6},{6,7},{7,4},{8,9},{9,10},{10,1... | collective-permute-start | bytes 12296 | tf_op jit(solution)/shard_map/ppermute | solution.py:343
  32.3 4.5 %collective-permute-start.5 = (f32[2,4,128]{2,1,0:T(4,128)S(1)}, f32[2,4,128]{2,1,0:T(4,128)S(1)}, u32[]{:S(2)}, u32[]{:S(2)}) collective-permute-start(f32[2,4,128]{2,1,0:T(4,128)S(1)} %get-tuple-element.11), channel_id=1, source_target_pairs={{0,2},{1,3},{2,0},{3,1},{4,6},{5,7},{6,4},{7,5},{8,10},{9,11},{10,... | collective-permute-start | bytes 12296 | tf_op jit(solution)/shard_map/ppermute | solution.py:343
  34.9 3.6 %collective-permute-start.6 = (f32[2,4,128]{2,1,0:T(4,128)S(1)}, f32[2,4,128]{2,1,0:T(4,128)S(1)}, u32[]{:S(2)}, u32[]{:S(2)}) collective-permute-start(f32[2,4,128]{2,1,0:T(4,128)S(1)} %get-tuple-element.12), channel_id=1, source_target_pairs={{0,3},{1,0},{2,1},{3,2},{4,7},{5,4},{6,5},{7,6},{8,11},{9,8},{10,9... | collective-permute-start | bytes 12296 | tf_op jit(solution)/shard_map/ppermute | solution.py:343
